TPU v7x, 32 devices: a whole 2x2x4 slice. The times are simulated.
32 devices in a mesh: tiles: 2 (over y), strip: 4 (over z), col: 2 (over x), expo: 2 (over core).
Axes of the slice: x: 2, y: 2, z: 4, core: 2. Of those that a mesh axis runs over, the one named last changes fastest.
Arguments:
- mask_params: float32 [2, 2048, 256], P('expo', ('tiles', 'strip'), 'col'), parts along dimension 1, may hold values from -3 to 3
- target: int32 [2048, 256], P(('tiles', 'strip'), 'col'), parts along dimension 0, may hold values from 0 to 1, as said below
- col_taps: bfloat16 [24, 2, 65], replicated, may hold values from -0.75 to 0.75
- row_taps: bfloat16 [24, 2, 65], replicated, may hold values from -0.75 to 0.75
- kernel_weights: float32 [24], replicated, may hold values from 0.05 to 0.5
Outputs:
- new_params: float32 [2, 2048, 256], P('expo', ('tiles', 'strip'), 'col'), parts along dimension 1
- resist: float32 [2048, 256], P(('tiles', 'strip'), 'col'), parts along dimension 0
- mean_loss: float32 [2], P('tiles'), parts along dimension 0
There are 2 independent parts, one for each index of `tiles`. A program takes and returns all parts, laid end to end along the dimension named above; an argument that names none is the same for every part. Nothing has to cross between parts.
Inputs may be any that keep to these rules, and one draw needn't show every extreme that they name: `target`: 1 where the layout is printed, 0 elsewhere.
All inputs are finite; a program needn't handle non-finite values.
Results may differ from a plain program's by a relative error of at most 0.0078.
Values may be sent and summed in bfloat16 or wider, within the bound.
No kernel may reach another device: no remote copies, remote signals or barrier semaphores. Data moves between devices by JAX's collectives and lax.ppermute only.
A program may use at most 64 MiB of HBM per device.

v0:
```python
import jax
import jax.numpy as jnp
from jax import lax
from jax.sharding import PartitionSpec as P

HALF = 32


mask_slope = 4.0
resist_steep = 4.0
resist_level = 3.0
step_length = 0.5
norm_eps = 1e-06


def extended(array, sides, width):
    for axis, dim in sides:
        peers, length = (lax.axis_size(axis), array.shape[dim])
        up = [(i, (i + 1) % peers) for i in range(peers - 1)]
        down = [(j, i) for i, j in up]
        last = lax.slice_in_dim(array, length - width, length, axis=dim)
        first = lax.slice_in_dim(array, 0, width, axis=dim)
        before = lax.ppermute(last, axis, up)
        after = lax.ppermute(first, axis, down)
        array = jnp.concatenate([before, array, after], axis=dim)
    return array


def block_size():
    return 128


def toeplitz(tap_values, block_len):
    tap_count = tap_values.shape[-1]
    window_len = block_len + tap_count - 1
    padded_taps = jnp.concatenate(
        [tap_values, jnp.zeros(tap_values.shape[:-1] + (block_len,), tap_values.dtype)], axis=-1
    )
    repeated = jnp.tile(padded_taps, (1,) * (tap_values.ndim - 1) + (block_len,))
    return repeated[..., : block_len * window_len].reshape(
        tap_values.shape[:-1] + (block_len, window_len)
    )


def col_pass(source, tap_table):
    block_len, window_len = (tap_table.shape[1], tap_table.shape[2])
    length = source.shape[-1] - window_len + block_len
    windows = jnp.stack([source], axis=1)
    result = jnp.einsum("rnw,pow->prno", windows, tap_table, preferred_element_type=jnp.float32)
    return result.reshape(tap_table.shape[0], source.shape[0], length)


def row_pass(source, tap_table):
    block_len, window_len = (tap_table.shape[1], tap_table.shape[2])
    length = source.shape[1] - window_len + block_len
    windows = jnp.stack(
        [
            source[:, offset * block_len : offset * block_len + window_len, :]
            for offset in range(length // block_len)
        ],
        axis=1,
    )
    result = jnp.einsum("pnwc,qow->pqnoc", windows, tap_table, preferred_element_type=jnp.float32)
    return result.reshape(source.shape[0], tap_table.shape[0], length, source.shape[2])


def col_adjoint(source, tap_table):
    block_len, window_len = (tap_table.shape[1], tap_table.shape[2])
    length = source.shape[-1] - window_len + block_len
    windows = jnp.stack([source], axis=2)
    result = jnp.einsum("prnw,pow->rno", windows, tap_table, preferred_element_type=jnp.float32)
    return result.reshape(source.shape[1], length)


def shards(mask_params, target, col_taps, row_taps, kernel_weights):
    row_count, col_count = target.shape
    mask_field = jax.nn.sigmoid(mask_slope * mask_params[0])
    mask_half = mask_field.astype(jnp.bfloat16)
    col_block = block_size()
    row_block = block_size()
    mask_ext = extended(mask_half, (("strip", 0), ("col", 1)), HALF)

    def add_intensity(running, kernel):
        col_pair = col_taps[kernel]
        row_pair = row_taps[kernel]
        columns = col_pass(mask_ext, toeplitz(col_pair, col_block)).astype(jnp.bfloat16)
        pair_sums = row_pass(columns, toeplitz(row_pair, row_block))
        real_part = pair_sums[0, 0] - pair_sums[1, 1]
        imag_part = pair_sums[0, 1] + pair_sums[1, 0]
        updated = running + kernel_weights[kernel] * (real_part * real_part + imag_part * imag_part)
        return (updated, (real_part, imag_part))

    kernel_ids = jnp.arange(kernel_weights.shape[0], dtype=jnp.int32)
    zero_field = jnp.zeros((row_count, col_count), jnp.float32)
    intensity, stored = lax.scan(add_intensity, zero_field, kernel_ids)
    summed = lax.psum(intensity, "expo")
    resist = jax.nn.sigmoid(resist_steep * (summed - resist_level))
    mismatch = resist - target.astype(jnp.float32)
    pixels = row_count * col_count * lax.axis_size("strip") * lax.axis_size("col")
    loss_local = jnp.sum(mismatch * mismatch)
    loss_sum = lax.psum(loss_local, ("strip", "col"))
    slope_field = 2.0 * mismatch * resist_steep * resist * (1.0 - resist)

    def add_gradient(running, inputs):
        kernel, real_part, imag_part = inputs
        col_pair = col_taps[kernel]
        row_pair = row_taps[kernel]
        weighting = 2.0 * kernel_weights[kernel] * slope_field
        products = jnp.stack([weighting * real_part, weighting * imag_part]).astype(jnp.bfloat16)
        product_ext = extended(products, (("strip", 1),), HALF)
        returned = row_pass(product_ext, toeplitz(row_pair[:, ::-1], row_block))
        unrolled = jnp.stack(
            [returned[0, 0] + returned[1, 1], returned[1, 0] - returned[0, 1]]
        ).astype(jnp.bfloat16)
        unrolled_ext = extended(unrolled, (("col", 2),), HALF)
        return (running + col_adjoint(unrolled_ext, toeplitz(col_pair[:, ::-1], col_block)), None)

    descent, unused = lax.scan(add_gradient, zero_field, (kernel_ids, stored[0], stored[1]))
    gradient = descent * mask_slope * mask_field * (1.0 - mask_field)
    grad_squares = jnp.sum(gradient * gradient)
    square_sum = lax.psum(grad_squares, ("strip", "col", "expo"))
    root_mean = jnp.sqrt(square_sum / (lax.axis_size("expo") * pixels) + norm_eps)
    new_params = mask_params - step_length * gradient[None] / root_mean
    mean_loss = (loss_sum / pixels).reshape(1)
    return (new_params, resist, mean_loss)


def solution(mesh):
    return jax.shard_map(
        shards,
        mesh=mesh,
        in_specs=(
            P("expo", ("tiles", "strip"), "col"),
            P(("tiles", "strip"), "col"),
            P(),
            P(),
            P(),
        ),
        out_specs=(P("expo", ("tiles", "strip"), "col"), P(("tiles", "strip"), "col"), P("tiles")),
        check_vma=False,
    )
```

profile of v0, /device:TPU:0, one launch (start us, length us, event | category | flops | bytes accessed | tf_op | source)
XLA Modules:
  0.0 801.6 jit_solution(15718260283883890776)
XLA Ops:
  8.2 5.0 collective-permute-start.4
  28.8 172.5 %while.26 = (s32[]{:T(128)}, f32[256,128]{1,0:T(8,128)S(1)}, f32[24,256,128]{2,1,0:T(8,128)}, f32[24,256,128]{2,1,0:T(8,128)}, s32[24]{0:T(128)S(1)}, /*index=5*...) while((s32[]{:T(128)}, f32[256,128]{1,0:T(8,128)S(1)}, ...), condition=%wide.region_1.2_spmd.clone, body=%wide.region_0.1_spmd.clone.sunk | while | flops 82296832 | bytes 4555409 | solution.py:95
  202.0 17.4 %all-reduce.6.cloned.1.call-done = f32[256,128]{1,0:T(8,128)} async-done(((f32[256,128]{1,0:T(8,128)}), f32[256,128]{1,0:T(8,128)}) %all-reduce.6.cloned.1.call-update) | async-done | bytes 131088 | tf_op jit(solution)/shard_map/psum | solution.py:96
  221.7 521.3 %while.27 = (s32[]{:T(128)}, f32[256,128]{1,0:T(8,128)S(1)}, s32[24]{0:T(128)S(1)}, bf16[24,2,65]{2,1,0:T(2,128)(2,1)}, f32[24]{0:T(128)}, /*index=5*/f32[256,12...) while((s32[]{:T(128)}, f32[256,128]{1,0:T(8,128)S(1)}, ...), condition=%wide.region_4.5_spmd.clone, body=%wide.region_3.4_spmd.clone.sunk | while | flops 77824000 | bytes 7152573 | solution.py:118
  238.5 4.5 collective-permute-start.3
  261.5 4.5 collective-permute-start.3
  284.5 4.5 collective-permute-start.3
  306.0 4.5 collective-permute-start.3
  327.5 4.5 collective-permute-start.3
  349.0 4.5 collective-permute-start.3
  370.5 4.5 collective-permute-start.3
  392.1 4.5 collective-permute-start.3
  413.6 4.5 collective-permute-start.3
  435.1 4.5 collective-permute-start.3
  456.6 4.5 collective-permute-start.3
  478.3 4.5 collective-permute-start.3
  499.8 4.5 collective-permute-start.3
  521.3 4.5 collective-permute-start.3
  542.8 4.5 collective-permute-start.3
  564.3 4.5 collective-permute-start.3
  585.8 4.5 collective-permute-start.3
  607.4 4.5 collective-permute-start.3
  743.7 30.1 %psum.22 = f32[]{:T(128)} all-reduce(f32[]{:T(128)} %multiply_reduce_fusion.1), channel_id=1, replica_groups=mesh['tiles'=2,'strip'=4,'col'=2,'expo'=2] {'strip','col','expo'}, use_global_device_ids=true, to_apply=%region_6.7 | all-reduce | flops 1 | bytes 8 | tf_op jit(solution)/shard_map/psum | solution.py:121
  775.2 17.7 %psum.23 = f32[]{:T(128)} all-reduce(f32[]{:T(128)} %get-tuple-element.217), channel_id=1, replica_groups=mesh['tiles'=2,'strip'=4,'col'=2,'expo'=2] {'strip','col'}, use_global_device_ids=true, to_apply=%region_8.9 | all-reduce | flops 1 | bytes 8 | tf_op jit(solution)/shard_map/psum | solution.py:101
  (1359 shorter events, 517.0 us)
Async XLA Ops:
  7.2 212.2 %all-reduce.6.cloned.1.call-start = ((), (), s32[]{:S(2)}) async-start(), calls=%async_computation | async-start | bytes 262144 | tf_op jit(solution)/shard_map/psum | solution.py:96
  237.2 6.6 collective-permute-start.2
  260.2 6.6 collective-permute-start.2
  283.2 6.6 collective-permute-start.2
  304.7 6.6 collective-permute-start.2
  326.2 6.6 collective-permute-start.2
  347.7 6.6 collective-permute-start.2
  369.2 6.6 collective-permute-start.2
  390.8 6.6 collective-permute-start.2
  412.3 6.6 collective-permute-start.2
  433.8 6.6 collective-permute-start.2
  455.3 6.6 collective-permute-start.2
  477.0 6.6 collective-permute-start.2
  498.5 6.6 collective-permute-start.2
  520.0 6.6 collective-permute-start.2
  541.5 6.6 collective-permute-start.2
  563.0 6.6 collective-permute-start.2
  584.5 6.6 collective-permute-start.2
  606.1 6.6 collective-permute-start.2
  627.6 6.6 collective-permute-start.2
  649.1 6.6 collective-permute-start.2
  670.7 6.6 collective-permute-start.2
  692.2 6.6 collective-permute-start.2
  713.8 6.6 collective-permute-start.2
  (105 other events, 1284.2 us)
Sparse Core Ops, SparseCore 0:
  202.1 17.2 all-reduce.5
where the time goes:
time: 807 us; the launch traced here: 802 us
  starting transfers between devices  233 us (29%)
  local copies, waits for them, and re-layouts  185 us (23%)
  loops' own time  116 us (14%)
  waiting for transfers between devices  114 us (14%)
  other arithmetic  65.4 us (8%)
  blocking collectives  47.8 us (6%)
  matrix products  23.3 us (3%)
  between operations  16.7 us (2%)
    ppermute x50, starting transfers between devices, extended(): before = lax.ppermute(last, axis, up)  169 us
    ppermute x50, waiting for transfers between devices, extended(): after = lax.ppermute(first, axis, down)  77.3 us
    another operation x1, loops' own time, shards(): lax.scan(add_gradient, zero_field, (kernel_ids, stored[0], stored[1]))  67 us
    ppermute x50, starting transfers between devices, extended(): after = lax.ppermute(first, axis, down)  64.6 us
    another operation x1, loops' own time, shards(): intensity, stored = lax.scan(add_intensity, zero_field, kernel_ids)  48.9 us
    another operation x192, local copies, waits for them, and re-layouts, toeplitz(): jnp.tile(padded_taps, (1,) * (tap_values.ndim - 1) + (block_len,))  42.5 us
    psum x1, blocking collectives, shards(): square_sum = lax.psum(grad_squares, ('strip', 'col', 'expo'))  30.1 us
    dynamic_slice x24, local copies, waits for them, and re-layouts, add_gradient(): weighting = 2.0 * kernel_weights[kernel] * slope_field  29.8 us
  transfers between devices with their start and end apart: 101, of which 52 were waited for; matrix products, arithmetic and copies ran while one was open for 7% of the time, Pallas kernels for 0%

commit v1 on v0

v1 whole, which is shorter than its diff:
```python
import functools
import jax
import jax.numpy as jnp
from jax import lax
from jax.experimental import pallas as pl
from jax.experimental.pallas import tpu as pltpu
from jax.sharding import PartitionSpec as P

HALF = 32
LANES = 128
UNROLL = 4

mask_slope = 4.0
resist_steep = 4.0
resist_level = 3.0
step_length = 0.5
norm_eps = 1e-06

BF16 = jnp.bfloat16
F32 = jnp.float32


def neighbours(axis, to_next, to_previous):
    peers = lax.axis_size(axis)
    if peers == 1:
        return jnp.zeros_like(to_next), jnp.zeros_like(to_previous)
    if peers == 2:
        first = lax.axis_index(axis) == 0
        got = lax.ppermute(jnp.where(first, to_next, to_previous), axis, [(0, 1), (1, 0)])
        nothing = jnp.zeros_like(got)
        return jnp.where(first, nothing, got), jnp.where(first, got, nothing)
    up = [(i, i + 1) for i in range(peers - 1)]
    down = [(j, i) for i, j in up]
    return lax.ppermute(to_next, axis, up), lax.ppermute(to_previous, axis, down)


def total_over(value, axis):
    peers = lax.axis_size(axis)
    if peers & (peers - 1):
        return lax.psum(value, axis)
    reach = 1
    while reach < peers:
        value = value + lax.ppermute(value, axis, [(i, i ^ reach) for i in range(peers)])
        reach *= 2
    return value


def circulant(row, shift):
    spread = jnp.broadcast_to(row, (LANES, LANES))
    return pltpu.roll(spread, shift, 1, stride=1, stride_axis=0)


def index_pair(shape):
    return lax.broadcasted_iota(jnp.int32, shape, 0), lax.broadcasted_iota(jnp.int32, shape, 1)


def assemble_kernel(mask_ref, up_ref, down_ref, code_ref, centre_ref, code_out_ref, right_ref, left_ref):
    rows, cols = mask_ref.shape
    wide = 2 * HALF
    tall = jnp.concatenate([up_ref[0:wide, :], mask_ref[...], down_ref[0:wide, :]], axis=0)
    turned = tall.astype(F32).T.astype(BF16)
    code = jnp.concatenate(
        [up_ref[wide:, :], code_ref[...], down_ref[wide:, :], jnp.zeros((wide, cols), BF16)], axis=0
    )
    code = code.astype(F32).T.astype(BF16)
    centre_ref[...] = turned
    code_out_ref[...] = code
    right_ref[0:wide, :] = turned[cols - wide :, :]
    right_ref[wide:, :] = code[cols - HALF :, :]
    left_ref[0:wide, :] = turned[0:wide, :]
    left_ref[wide:, :] = code[0:HALF, :]


def forward_kernel(
    weights_ref, centre_ref, before_ref, after_ref, taps_ref, field_ref, intensity_ref, mask_ref, total_ref
):
    step = pl.program_id(0)
    cols = centre_ref.shape[0]
    wide = 2 * HALF
    tiles = centre_ref.shape[1] // LANES
    span = cols + wide

    @pl.when(step == 0)
    def _():
        mask_ref[0:wide, :] = before_ref[0:wide, :]
        mask_ref[wide : wide + cols, :] = centre_ref[...]
        mask_ref[wide + cols :, :] = after_ref[0:wide, :]
        total_ref[...] = jnp.zeros_like(total_ref)

    a, b = index_pair((LANES, LANES))
    upper, lower = b >= a, a >= b
    zero = jnp.zeros((LANES, LANES), F32)
    for unit in range(UNROLL):
        weight = weights_ref[step * UNROLL + unit]
        stack = []
        for part in range(2):
            base = circulant(taps_ref[unit, part : part + 1, :], 0)
            near = jnp.where(upper, base, zero).astype(BF16)
            far = jnp.where(upper, zero, base).astype(BF16)
            stack.append(jnp.concatenate([near, far], axis=1))
            stack.append(jnp.concatenate([jnp.zeros((wide, LANES), BF16), near[0:wide]], axis=1))
        table = jnp.concatenate(stack, axis=0)
        columns = jnp.dot(table, mask_ref[...], preferred_element_type=F32).astype(BF16)
        near, far = [], []
        for part in range(2):
            base = circulant(taps_ref[unit, 2 + part : 3 + part, :], LANES // 2)
            near.append(jnp.where(lower, base, zero).astype(BF16))
            far.append(jnp.where(lower, zero, base).astype(BF16))
        table = jnp.concatenate(
            [
                jnp.concatenate([near[0], near[1]], axis=1),
                jnp.concatenate([-near[1], near[0]], axis=1),
                jnp.concatenate([far[0], far[1]], axis=1),
                jnp.concatenate([-far[1], far[0]], axis=1),
            ],
            axis=0,
        )
        pieces = [
            jnp.concatenate(
                [columns[part * span : (part + 1) * span, t * LANES : (t + 1) * LANES] for part in range(2)],
                axis=1,
            )
            for t in range(tiles)
        ]
        for t in range(tiles):
            if t + 1 < tiles:
                window = jnp.concatenate([pieces[t], pieces[t + 1]], axis=1)
                field = jnp.dot(window, table, preferred_element_type=F32)
            else:
                field = jnp.dot(pieces[t], table[0 : 2 * LANES], preferred_element_type=F32)
            field_ref[unit, t] = field.astype(field_ref.dtype)
            total_ref[t] += weight * (field * field)

    @pl.when(step == pl.num_programs(0) - 1)
    def _():
        for t in range(tiles):
            intensity_ref[t] = total_ref[t, :, 0:LANES] + total_ref[t, :, LANES:]


def backward_kernel(
    weights_ref,
    own_ref,
    other_ref,
    code_ref,
    code_before_ref,
    code_after_ref,
    params_ref,
    field_ref,
    taps_ref,
    gradient_ref,
    resist_ref,
    sums_ref,
    slope_ref,
    descent_ref,
    resist_all_ref,
    mismatch_ref,
):
    step = pl.program_id(0)
    cols = code_ref.shape[0]
    wide = 2 * HALF
    tiles = own_ref.shape[0]
    rows = (tiles - 1) * LANES

    @pl.when(step == 0)
    def _():
        for t in range(tiles):
            lanes = slice(t * LANES, (t + 1) * LANES)
            code = jnp.concatenate(
                [code_before_ref[wide:, lanes], code_ref[:, lanes], code_after_ref[wide:, lanes]], axis=0
            ).astype(F32)
            summed = own_ref[t] + other_ref[t]
            resist = jax.nn.sigmoid(resist_steep * (summed - resist_level))
            mismatch = resist - (code - 1.0)
            slope = 2.0 * mismatch * resist_steep * resist * (1.0 - resist)
            slope = jnp.where(code > 0.5, slope, 0.0)
            slope_ref[t, :, 0:LANES] = slope
            slope_ref[t, :, LANES:] = slope
            resist_all_ref[:, lanes] = resist[HALF : HALF + cols]
            mismatch_ref[:, lanes] = mismatch[HALF : HALF + cols]
        descent_ref[...] = jnp.zeros_like(descent_ref)

    a, b = index_pair((LANES, LANES))
    upper, lower = b >= a, a >= b
    zero = jnp.zeros((LANES, LANES), F32)
    for unit in range(UNROLL):
        weight = 2.0 * weights_ref[step * UNROLL + unit]
        near, far = [], []
        for part in range(2):
            base = circulant(taps_ref[unit, 2 + part : 3 + part, :], LANES // 2)
            near.append(jnp.where(lower, base, zero).astype(BF16))
            far.append(jnp.where(lower, zero, base).astype(BF16))
        table = jnp.concatenate(
            [
                jnp.concatenate([near[0], -near[1]], axis=1),
                jnp.concatenate([near[1], near[0]], axis=1),
                jnp.concatenate([far[0], -far[1]], axis=1),
                jnp.concatenate([far[1], far[0]], axis=1),
            ],
            axis=0,
        )
        products = [
            ((weight * slope_ref[t]) * field_ref[unit, t].astype(F32)).astype(BF16) for t in range(tiles)
        ]
        returned = []
        for t in range(tiles - 1):
            window = jnp.concatenate([products[t], products[t + 1]], axis=1)
            returned.append(jnp.dot(window, table, preferred_element_type=F32).astype(BF16))
        split = [
            jnp.concatenate([r[:, part * LANES : (part + 1) * LANES] for r in returned], axis=1)
            for part in range(2)
        ]
        near, far = [], []
        for part in range(2):
            base = circulant(taps_ref[unit, part : part + 1, :], 0)
            near.append(jnp.where(upper, base, zero).astype(BF16))
            far.append(jnp.where(upper, zero, base))
        joined = jnp.where(b < wide, far[0], pltpu.roll(far[1], wide, 1)).astype(BF16)
        table = jnp.concatenate([near[0], near[1], joined], axis=1)
        source = jnp.concatenate([split[0][0:cols], split[1][0:cols], split[0][cols:], split[1][cols:]], axis=0)
        descent_ref[...] += jnp.dot(table, source, preferred_element_type=F32)

    @pl.when(step == pl.num_programs(0) - 1)
    def _():
        mask = jax.nn.sigmoid(mask_slope * params_ref[...])
        gradient = descent_ref[...].T * mask_slope * mask * (1.0 - mask)
        gradient_ref[...] = gradient
        resist_ref[...] = resist_all_ref[...].T[HALF : HALF + rows]
        a, b = index_pair(mismatch_ref.shape)
        mismatch = jnp.where((b >= HALF) & (b < HALF + rows), mismatch_ref[...], 0.0)
        squares = jnp.sum(gradient * gradient, axis=0, keepdims=True)
        loss = jnp.sum(mismatch * mismatch)
        sums_ref[0:1, :] = jnp.broadcast_to(jnp.sum(squares), (1, LANES))
        sums_ref[1:2, :] = jnp.broadcast_to(loss, (1, LANES))


def whole(shape):
    return pl.BlockSpec(shape, lambda *_: (0,) * len(shape))


def shards(mask_params, target, col_taps, row_taps, kernel_weights):
    rows, cols = target.shape
    kernels, _, taps = col_taps.shape
    wide = 2 * HALF
    tiles = rows // LANES + 1
    long, span = tiles * LANES, cols + wide
    if cols != LANES or rows % LANES or taps != wide + 1 or kernels % UNROLL:
        raise ValueError("block shape")
    params = mask_params[0]
    mask_half = jax.nn.sigmoid(mask_slope * params).astype(BF16)
    code = (target + 1).astype(BF16)
    strip_up, strip_down = neighbours(
        "strip",
        jnp.concatenate([mask_half[rows - wide :], code[rows - HALF :]], axis=0),
        jnp.concatenate([mask_half[:wide], code[:HALF]], axis=0),
    )
    side = jax.ShapeDtypeStruct((wide + HALF, long), BF16)
    turned = jax.ShapeDtypeStruct((cols, long), BF16)
    centre, code_turned, to_right, to_left = pl.pallas_call(
        assemble_kernel, out_shape=(turned, turned, side, side), name="assemble"
    )(mask_half, strip_up, strip_down, code)
    before, after = neighbours("col", to_right, to_left)

    pad = ((0, 0), (0, 0), (0, LANES - taps))
    col_plain, row_plain = jnp.pad(col_taps, pad), jnp.pad(row_taps, pad)
    col_turned, row_turned = jnp.pad(col_taps[..., ::-1], pad), jnp.pad(row_taps[..., ::-1], pad)
    forward_taps = jnp.concatenate([col_plain, row_turned], axis=1).astype(F32)
    backward_taps = jnp.concatenate([col_turned, row_plain], axis=1).astype(F32)

    smem = pl.BlockSpec(memory_space=pltpu.SMEM)
    taps_spec = pl.BlockSpec((UNROLL, 4, LANES), lambda k: (k, 0, 0))
    field_spec = pl.BlockSpec((UNROLL, tiles, span, 2 * LANES), lambda k: (k, 0, 0, 0))
    plane = (tiles, span, LANES)
    field, intensity = pl.pallas_call(
        forward_kernel,
        grid=(kernels // UNROLL,),
        in_specs=[smem, whole((cols, long)), whole((wide + HALF, long)), whole((wide + HALF, long)), taps_spec],
        out_specs=[field_spec, whole(plane)],
        out_shape=(
            jax.ShapeDtypeStruct((kernels, tiles, span, 2 * LANES), BF16),
            jax.ShapeDtypeStruct(plane, F32),
        ),
        scratch_shapes=[
            pltpu.VMEM((cols + 2 * wide, long), BF16),
            pltpu.VMEM((tiles, span, 2 * LANES), F32),
        ],
        name="forward",
    )(kernel_weights, centre, before, after, forward_taps)

    exposures = lax.axis_size("expo")
    other = lax.ppermute(intensity, "expo", [(i, (i + 1) % exposures) for i in range(exposures)])

    gradient, resist, sums = pl.pallas_call(
        backward_kernel,
        grid=(kernels // UNROLL,),
        in_specs=[
            smem,
            whole(plane),
            whole(plane),
            whole((cols, long)),
            whole((wide + HALF, long)),
            whole((wide + HALF, long)),
            whole((rows, cols)),
            field_spec,
            taps_spec,
        ],
        out_specs=[whole((rows, cols)), whole((rows, cols)), whole((2, LANES))],
        out_shape=(
            jax.ShapeDtypeStruct((rows, cols), F32),
            jax.ShapeDtypeStruct((rows, cols), F32),
            jax.ShapeDtypeStruct((2, LANES), F32),
        ),
        scratch_shapes=[
            pltpu.VMEM((tiles, span, 2 * LANES), F32),
            pltpu.VMEM((cols, rows), F32),
            pltpu.VMEM((cols, long), F32),
            pltpu.VMEM((cols, long), F32),
        ],
        name="backward",
    )(kernel_weights, intensity, other, code_turned, before, after, params, field, backward_taps)

    for axis in ("expo", "col", "strip"):
        sums = total_over(sums, axis)
    pixels = rows * cols * lax.axis_size("strip") * lax.axis_size("col")
    count = exposures * pixels
    root_mean = jnp.sqrt(sums[0, 0] / count + norm_eps)
    new_params = mask_params - step_length * gradient[None] / root_mean
    mean_loss = sums[1, 0:1] / count
    return (new_params, resist, mean_loss)


def solution(mesh):
    if mesh.shape["expo"] != 2:
        raise ValueError("two exposures")
    return jax.shard_map(
        shards,
        mesh=mesh,
        in_specs=(
            P("expo", ("tiles", "strip"), "col"),
            P(("tiles", "strip"), "col"),
            P(),
            P(),
            P(),
        ),
        out_specs=(P("expo", ("tiles", "strip"), "col"), P(("tiles", "strip"), "col"), P("tiles")),
        check_vma=False,
    )
```

time: 807 us -> 65.1 us (0.08)
  starting transfers between devices: 233 us -> 14.1 us
  local copies, waits for them, and re-layouts: 185 us -> 3.48 us
  loops' own time: 116 us -> 0 us
  waiting for transfers between devices: 114 us -> 12 us
  other arithmetic: 65.4 us -> 8.45 us
  blocking collectives: 47.8 us -> 0 us
  Pallas kernels: 0 us -> 23.4 us
  matrix products: 23.3 us -> 0 us
  between operations: 16.7 us -> 3.17 us
    ppermute x100 -> x8, starting transfers between devices: 233 us -> 14.1 us  [the longest x4 6.25 us: total_over(): lax.ppermute(value, axis, [(i, i ^ reach) for i in range(peers)])]
    another operation x2 -> x0, loops' own time: 116 us -> none  [the longest x1 67 us: shards(): lax.scan(add_gradient, zero_field, (kernel_ids, stored[0], stored[1]))]
    ppermute x100 -> x8, waiting for transfers between devices: 96.9 us -> 12 us  [the longest x4 6.91 us: total_over(): lax.ppermute(value, axis, [(i, i ^ reach) for i in range(peers)])]
    dynamic_slice x96 -> x0, local copies, waits for them, and re-layouts: 72 us -> none  [the longest x24 29.8 us: add_gradient(): weighting = 2.0 * kernel_weights[kernel] * slope_field]
    psum x2 -> x0, blocking collectives: 47.8 us -> none  [the longest x1 30.1 us: shards(): square_sum = lax.psum(grad_squares, ('strip', 'col', 'expo'))]
    another operation x216 -> x0, local copies, waits for them, and re-layouts: 43 us -> none  [the longest x192 42.5 us: toeplitz(): jnp.tile(padded_taps, (1,) * (tap_values.ndim - 1) + (block_len,))]
    squeeze x48 -> x0, local copies, waits for them, and re-layouts: 32.7 us -> none  [the longest x24 16.4 us: add_gradient(): row_pair = row_taps[kernel]]
    another operation x50 -> x0, other arithmetic: 24.5 us -> none
  transfers between devices with their start and end apart: 101 -> 8, of which waited for: 52 -> 6; matrix products, arithmetic and copies ran while one was open for 7% -> 7% of each run, Pallas kernels for 0% -> 0%
where the time goes in v1:
time: 65.1 us; the launch traced here: 64.5 us
  Pallas kernels  23.4 us (36%)
  starting transfers between devices  14.1 us (22%)
  waiting for transfers between devices  12 us (18%)
  other arithmetic  8.45 us (13%)
  local copies, waits for them, and re-layouts  3.48 us (5%)
  between operations  3.17 us (5%)
    pallas_call x1, Pallas kernels, shards(): pl.pallas_call(forward_kernel, grid=(kernels // UNROLL,), in_specs=[smem,...  10.9 us
    pallas_call x1, Pallas kernels, shards(): pl.pallas_call(backward_kernel, grid=(kernels // UNROLL,), in_specs=[smem...  10.7 us
    ppermute x4, waiting for transfers between devices, total_over(): lax.ppermute(value, axis, [(i, i ^ reach) for i in range(peers)])  6.91 us
    ppermute x4, starting transfers between devices, total_over(): lax.ppermute(value, axis, [(i, i ^ reach) for i in range(peers)])  6.25 us
    ppermute x1, starting transfers between devices, neighbours(): lax.ppermute(to_next, axis, up)  4.96 us
    ppermute x1, waiting for transfers between devices, neighbours(): lax.ppermute(to_previous, axis, down)  3.57 us
    pallas_call x1, Pallas kernels, shards(): pl.pallas_call(assemble_kernel, out_shape=(turned, turned, side, side), n...  1.74 us
    sub x1, other arithmetic, shards(): new_params = mask_params - step_length * gradient[None] / root_mean  1.58 us
  transfers between devices with their start and end apart: 8, of which 6 were waited for; matrix products, arithmetic and copies ran while one was open for 7% of the time, Pallas kernels for 0%

profile of v1, /device:TPU:0, one launch (start us, length us, event | category | flops | bytes accessed | tf_op | source)
XLA Modules:
  0.0 64.5 jit_solution(994985537101553842)
XLA Ops:
  0.6 1.0 %add_convert_fusion.code_ref = bf16[256,128]{1,0:T(8,128)(2,1)S(1)} fusion(s32[256,128]{1,0:T(8,128)} %param.6), kind=kLoop, calls=%fused_computation.1 | loop fusion | flops 65536 | bytes 196608 | tf_op jit(solution)/shard_map/convert_element_type | solution.py:250
  1.6 1.0 %divide_convert_fusion.mask_ref = bf16[256,128]{1,0:T(8,128)(2,1)S(1)} fusion(f32[1,256,128]{2,1,0:T(8,128)} %param.5), kind=kLoop, calls=%fused_computation.2 | loop fusion | flops 163840 | bytes 196608 | tf_op jit(solution)/shard_map/convert_element_type | solution.py:249
  2.6 5.0 %collective-permute-start = (bf16[96,128]{1,0:T(8,128)(2,1)S(1)}, bf16[96,128]{1,0:T(8,128)(2,1)S(1)}, u32[]{:S(2)}, u32[]{:S(2)}) collective-permute-start(bf16[96,128]{1,0:T(8,128)(2,1)S(1)} %pad_maximum_fusion), channel_id=1, source_target_pairs={{0,4},{4,8},{8,12},{1,5},{5,9},{9,13},{2,6},{6,10},{10,14},{3,7},{... | collective-permute-start | bytes 73736 | tf_op jit(solution)/shard_map/ppermute | solution.py:34
  7.6 1.3 %collective-permute-start.1 = (bf16[96,128]{1,0:T(8,128)(2,1)S(1)}, bf16[96,128]{1,0:T(8,128)(2,1)S(1)}, u32[]{:S(2)}, u32[]{:S(2)}) collective-permute-start(bf16[96,128]{1,0:T(8,128)(2,1)S(1)} %pad_maximum_fusion.1), channel_id=1, source_target_pairs={{4,0},{8,4},{12,8},{5,1},{9,5},{13,9},{6,2},{10,6},{14,10},{7,3},{... | collective-permute-start | bytes 73736 | tf_op jit(solution)/shard_map/ppermute | solution.py:34
  8.9 0.8 %rev.6 = bf16[24,2,65]{2,1,0:T(2,128)(2,1)S(1)} reverse(bf16[24,2,65]{2,1,0:T(2,128)(2,1)} %param.8), dimensions={2} | reverse | bytes 12480 | tf_op jit(solution)/shard_map/rev | solution.py:265
  9.8 3.6 %collective-permute-done.1.down_ref = bf16[96,128]{1,0:T(8,128)(2,1)S(1)} collective-permute-done((bf16[96,128]{1,0:T(8,128)(2,1)S(1)}, bf16[96,128]{1,0:T(8,128)(2,1)S(1)}, u32[]{:S(2)}, u32[]{:S(2)}) %collective-permute-start.1) | collective-permute-done | bytes 24608 | tf_op jit(solution)/shard_map/ppermute | solution.py:34
  13.9 1.7 %assemble.1 = (bf16[128,384]{1,0:T(8,128)(2,1)}, bf16[128,384]{1,0:T(8,128)(2,1)}, bf16[96,384]{1,0:T(8,128)(2,1)}, bf16[96,384]{1,0:T(8,128)(2,1)}) custom-call(bf16[256,128]{1,0:T(8,128)(2,1)} %copy-done.1, bf16[96,128]{1,0:T(8,128)(2,1)} %copy-done.4, bf16[96,128]{1,0:T(8,128)(2,1)} %copy-done.5, bf16[256,128]{1,0:T(8,128)(2,1)} %copy-done.2), custom_call_target="tpu_custom_call" | custom-call | tf_op jit(solution)/shard_map/assemble/pallas_call | solution.py:258
  15.7 0.9 %broadcast_select_fusion.2 = bf16[96,384]{1,0:T(8,128)(2,1)S(1)} fusion(bf16[96,384]{1,0:T(8,128)(2,1)} %get-tuple-element.13, bf16[96,384]{1,0:T(8,128)(2,1)} %get-tuple-element.14, pred[]{:T(512)S(6)} %eq.3), kind=kLoop, calls=%fused_computation.5 | loop fusion | flops 36864 | bytes 221185 | tf_op jit(solution)/shard_map/jit(_where)/select_n | solution.py:29
  16.6 1.6 %collective-permute-start.2 = (bf16[96,384]{1,0:T(8,128)(2,1)S(1)}, bf16[96,384]{1,0:T(8,128)(2,1)S(1)}, u32[]{:S(2)}, u32[]{:S(2)}) collective-permute-start(bf16[96,384]{1,0:T(8,128)(2,1)S(1)} %broadcast_select_fusion.2), channel_id=1, source_target_pairs={{0,2},{2,0},{1,3},{3,1},{4,6},{6,4},{5,7},{7,5},{8,10},{10,8},{9,1... | collective-permute-start | bytes 221192 | tf_op jit(solution)/shard_map/ppermute | solution.py:29
  18.1 1.4 %fusion.5.taps_ref = f32[24,4,128]{2,1,0:T(4,128)} fusion(bf16[24,2,65]{2,1,0:T(2,128)(2,1)S(1)} %rev.6, bf16[24,2,65]{2,1,0:T(2,128)(2,1)} %param.7), kind=kLoop, calls=%fused_computation.13 | loop fusion | flops 98304 | bytes 61632 | tf_op jit(solution)/shard_map/convert_element_type | solution.py:266
  19.5 1.5 %collective-permute-done.2 = bf16[96,384]{1,0:T(8,128)(2,1)S(1)} collective-permute-done((bf16[96,384]{1,0:T(8,128)(2,1)S(1)}, bf16[96,384]{1,0:T(8,128)(2,1)S(1)}, u32[]{:S(2)}, u32[]{:S(2)}) %collective-permute-start.2) | collective-permute-done | bytes 73760 | tf_op jit(solution)/shard_map/ppermute | solution.py:29
  21.7 10.9 %forward.1 = (bf16[24,3,192,256]{3,2,1,0:T(8,128)(2,1)}, f32[3,192,128]{2,1,0:T(8,128)}) custom-call(f32[24]{0:T(128)} %weights_ref.3, bf16[128,384]{1,0:T(8,128)(2,1)} %get-tuple-element.12.centre_ref, bf16[96,384]{1,0:T(8,128)(2,1)} %get-tuple-element.22.before_ref.code_before_ref, bf16[96,384]{1,0:T(8,128)(2,1)} %get-tuple-element.21.after_ref.code_after_ref, ...), custom_call_target="tpu_custom_call" | custom-call | tf_op jit(solution)/shard_map/forward/pallas_call | solution.py:273
  32.6 0.8 %rev.7 = bf16[24,2,65]{2,1,0:T(2,128)(2,1)S(1)} reverse(bf16[24,2,65]{2,1,0:T(2,128)(2,1)} %param.7), dimensions={2} | reverse | bytes 12480 | tf_op jit(solution)/shard_map/rev | solution.py:265
  33.4 1.4 %fusion.7.taps_ref = f32[24,4,128]{2,1,0:T(4,128)} fusion(bf16[24,2,65]{2,1,0:T(2,128)(2,1)} %param.8, bf16[24,2,65]{2,1,0:T(2,128)(2,1)S(1)} %rev.7), kind=kLoop, calls=%fused_computation.15 | loop fusion | flops 98304 | bytes 61632 | tf_op jit(solution)/shard_map/convert_element_type | solution.py:267
  34.8 0.7 %copy-done.3 = f32[3,192,128]{2,1,0:T(8,128)} copy-done((f32[3,192,128]{2,1,0:T(8,128)}, f32[3,192,128]{2,1,0:T(8,128)S(1)}, u32[]{:S(2)}) %copy-start.3) | copy-done | bytes 294936
  35.5 10.7 %backward.1 = (f32[256,128]{1,0:T(8,128)}, f32[256,128]{1,0:T(8,128)}, f32[2,128]{1,0:T(2,128)}) custom-call(f32[24]{0:T(128)} %weights_ref.3, f32[3,192,128]{2,1,0:T(8,128)} %get-tuple-element.15.own_ref, f32[3,192,128]{2,1,0:T(8,128)} %copy-done.3, bf16[128,384]{1,0:T(8,128)(2,1)} %get-tuple-element.16.code_ref, ...), custom_call_target="tpu_custom_call" | custom-call | tf_op jit(solution)/shard_map/backward/pallas_call | solution.py:292
  46.7 1.0 %collective-permute-done.4 = f32[2,128]{1,0:T(2,128)S(1)} collective-permute-done((f32[2,128]{1,0:T(2,128)}, f32[2,128]{1,0:T(2,128)S(1)}, u32[]{:S(2)}, u32[]{:S(2)}) %collective-permute-start.4) | collective-permute-done | bytes 1056 | tf_op jit(solution)/shard_map/ppermute | solution.py:43
  48.4 1.5 %collective-permute-start.5 = (f32[2,128]{1,0:T(2,128)S(1)}, f32[2,128]{1,0:T(2,128)S(1)}, u32[]{:S(2)}, u32[]{:S(2)}) collective-permute-start(f32[2,128]{1,0:T(2,128)S(1)} %add.36), channel_id=1, source_target_pairs={{0,2},{2,0},{1,3},{3,1},{4,6},{6,4},{5,7},{7,5},{8,10},{10,8},{9,1... | collective-permute-start | bytes 3080 | tf_op jit(solution)/shard_map/ppermute | solution.py:43
  49.9 2.1 %collective-permute-done.5 = f32[2,128]{1,0:T(2,128)S(1)} collective-permute-done((f32[2,128]{1,0:T(2,128)S(1)}, f32[2,128]{1,0:T(2,128)S(1)}, u32[]{:S(2)}, u32[]{:S(2)}) %collective-permute-start.5) | collective-permute-done | bytes 1056 | tf_op jit(solution)/shard_map/ppermute | solution.py:43
  51.9 1.6 %collective-permute-start.6 = (f32[2,128]{1,0:T(2,128)S(1)}, f32[2,128]{1,0:T(2,128)S(1)}, u32[]{:S(2)}, u32[]{:S(2)}) collective-permute-start(f32[2,128]{1,0:T(2,128)S(1)} %add.37), channel_id=1, source_target_pairs={{0,4},{4,0},{8,12},{12,8},{1,5},{5,1},{9,13},{13,9},{2,6},{6,2},{1... | collective-permute-start | bytes 3080 | tf_op jit(solution)/shard_map/ppermute | solution.py:43
  53.5 2.0 %collective-permute-done.6 = f32[2,128]{1,0:T(2,128)S(1)} collective-permute-done((f32[2,128]{1,0:T(2,128)S(1)}, f32[2,128]{1,0:T(2,128)S(1)}, u32[]{:S(2)}, u32[]{:S(2)}) %collective-permute-start.6) | collective-permute-done | bytes 1056 | tf_op jit(solution)/shard_map/ppermute | solution.py:43
  55.5 2.6 %collective-permute-start.7 = (f32[2,128]{1,0:T(2,128)S(1)}, f32[2,128]{1,0:T(2,128)S(1)}, u32[]{:S(2)}, u32[]{:S(2)}) collective-permute-start(f32[2,128]{1,0:T(2,128)S(1)} %add.38), channel_id=1, source_target_pairs={{0,8},{4,12},{8,0},{12,4},{1,9},{5,13},{9,1},{13,5},{2,10},{6,14},... | collective-permute-start | bytes 3080 | tf_op jit(solution)/shard_map/ppermute | solution.py:43
  58.2 1.8 %collective-permute-done.7 = f32[2,128]{1,0:T(2,128)S(1)} collective-permute-done((f32[2,128]{1,0:T(2,128)S(1)}, f32[2,128]{1,0:T(2,128)S(1)}, u32[]{:S(2)}, u32[]{:S(2)}) %collective-permute-start.7) | collective-permute-done | bytes 1056 | tf_op jit(solution)/shard_map/ppermute | solution.py:43
  61.8 1.6 %bitcast_subtract_fusion = f32[1,256,128]{2,1,0:T(8,128)} fusion(f32[1,256,128]{2,1,0:T(8,128)S(1)} %copy-done, f32[256,128]{1,0:T(8,128)} %get-tuple-element.18, f32[]{:T(128)} %bitcast.1), kind=kLoop, calls=%fused_computation | loop fusion | flops 98304 | bytes 393220 | tf_op jit(solution)/shard_map/sub | solution.py:326
  (25 shorter events, 3.0 us)
Async XLA Ops:
  0.6 61.2 %copy-start = (f32[1,256,128]{2,1,0:T(8,128)S(1)}, f32[1,256,128]{2,1,0:T(8,128)}, u32[]{:S(2)}) copy-start(f32[1,256,128]{2,1,0:T(8,128)} %param.5) | copy-start | bytes 393220
  1.6 11.7 %copy-start.2 = (bf16[256,128]{1,0:T(8,128)(2,1)}, bf16[256,128]{1,0:T(8,128)(2,1)S(1)}, u32[]{:S(2)}) copy-start(bf16[256,128]{1,0:T(8,128)(2,1)S(1)} %add_convert_fusion.code_ref) | copy-start | bytes 196612
  2.6 10.7 %copy-start.1 = (bf16[256,128]{1,0:T(8,128)(2,1)}, bf16[256,128]{1,0:T(8,128)(2,1)S(1)}, u32[]{:S(2)}) copy-start(bf16[256,128]{1,0:T(8,128)(2,1)S(1)} %divide_convert_fusion.mask_ref) | copy-start | bytes 196612
  2.6 7.1 %collective-permute-start = (bf16[96,128]{1,0:T(8,128)(2,1)S(1)}, bf16[96,128]{1,0:T(8,128)(2,1)S(1)}, u32[]{:S(2)}, u32[]{:S(2)}) collective-permute-start(bf16[96,128]{1,0:T(8,128)(2,1)S(1)} %pad_maximum_fusion), channel_id=1, source_target_pairs={{0,4},{4,8},{8,12},{1,5},{5,9},{9,13},{2,6},{6,10},{10,14},{3,7},{... | collective-permute-start | bytes 73736 | tf_op jit(solution)/shard_map/ppermute | solution.py:34
  7.6 5.7 %collective-permute-start.1 = (bf16[96,128]{1,0:T(8,128)(2,1)S(1)}, bf16[96,128]{1,0:T(8,128)(2,1)S(1)}, u32[]{:S(2)}, u32[]{:S(2)}) collective-permute-start(bf16[96,128]{1,0:T(8,128)(2,1)S(1)} %pad_maximum_fusion.1), channel_id=1, source_target_pairs={{4,0},{8,4},{12,8},{5,1},{9,5},{13,9},{6,2},{10,6},{14,10},{7,3},{... | collective-permute-start | bytes 73736 | tf_op jit(solution)/shard_map/ppermute | solution.py:34
  9.8 3.6 %copy-start.4 = (bf16[96,128]{1,0:T(8,128)(2,1)}, bf16[96,128]{1,0:T(8,128)(2,1)S(1)}, u32[]{:S(2)}) copy-start(bf16[96,128]{1,0:T(8,128)(2,1)S(1)} %collective-permute-done.up_ref) | copy-start | bytes 73732
  13.3 0.6 copy-start.5
  16.6 4.4 %collective-permute-start.2 = (bf16[96,384]{1,0:T(8,128)(2,1)S(1)}, bf16[96,384]{1,0:T(8,128)(2,1)S(1)}, u32[]{:S(2)}, u32[]{:S(2)}) collective-permute-start(bf16[96,384]{1,0:T(8,128)(2,1)S(1)} %broadcast_select_fusion.2), channel_id=1, source_target_pairs={{0,2},{2,0},{1,3},{3,1},{4,6},{6,4},{5,7},{7,5},{8,10},{10,8},{9,1... | collective-permute-start | bytes 221192 | tf_op jit(solution)/shard_map/ppermute | solution.py:29
  32.6 2.2 %collective-permute-start.3 = (f32[3,192,128]{2,1,0:T(8,128)}, f32[3,192,128]{2,1,0:T(8,128)S(1)}, u32[]{:S(2)}, u32[]{:S(2)}) collective-permute-start(f32[3,192,128]{2,1,0:T(8,128)} %get-tuple-element.15.own_ref), channel_id=1, source_target_pairs={{0,1},{1,0},{2,3},{3,2},{4,5},{5,4},{6,7},{7,6},{8,9},{9,8},{10,11... | collective-permute-start | bytes 884744 | tf_op jit(solution)/shard_map/ppermute | solution.py:290
  34.8 0.7 %copy-start.3 = (f32[3,192,128]{2,1,0:T(8,128)}, f32[3,192,128]{2,1,0:T(8,128)S(1)}, u32[]{:S(2)}) copy-start(f32[3,192,128]{2,1,0:T(8,128)S(1)} %collective-permute-done.3.other_ref) | copy-start | bytes 884740
  46.2 1.5 %collective-permute-start.4 = (f32[2,128]{1,0:T(2,128)}, f32[2,128]{1,0:T(2,128)S(1)}, u32[]{:S(2)}, u32[]{:S(2)}) collective-permute-start(f32[2,128]{1,0:T(2,128)} %get-tuple-element.19), channel_id=1, source_target_pairs={{0,1},{1,0},{2,3},{3,2},{4,5},{5,4},{6,7},{7,6},{8,9},{9,8},{10,11... | collective-permute-start | bytes 3080 | tf_op jit(solution)/shard_map/ppermute | solution.py:43
  48.4 3.6 %collective-permute-start.5 = (f32[2,128]{1,0:T(2,128)S(1)}, f32[2,128]{1,0:T(2,128)S(1)}, u32[]{:S(2)}, u32[]{:S(2)}) collective-permute-start(f32[2,128]{1,0:T(2,128)S(1)} %add.36), channel_id=1, source_target_pairs={{0,2},{2,0},{1,3},{3,1},{4,6},{6,4},{5,7},{7,5},{8,10},{10,8},{9,1... | collective-permute-start | bytes 3080 | tf_op jit(solution)/shard_map/ppermute | solution.py:43
  51.9 3.6 %collective-permute-start.6 = (f32[2,128]{1,0:T(2,128)S(1)}, f32[2,128]{1,0:T(2,128)S(1)}, u32[]{:S(2)}, u32[]{:S(2)}) collective-permute-start(f32[2,128]{1,0:T(2,128)S(1)} %add.37), channel_id=1, source_target_pairs={{0,4},{4,0},{8,12},{12,8},{1,5},{5,1},{9,13},{13,9},{2,6},{6,2},{1... | collective-permute-start | bytes 3080 | tf_op jit(solution)/shard_map/ppermute | solution.py:43
  55.5 4.5 %collective-permute-start.7 = (f32[2,128]{1,0:T(2,128)S(1)}, f32[2,128]{1,0:T(2,128)S(1)}, u32[]{:S(2)}, u32[]{:S(2)}) collective-permute-start(f32[2,128]{1,0:T(2,128)S(1)} %add.38), channel_id=1, source_target_pairs={{0,8},{4,12},{8,0},{12,4},{1,9},{5,13},{9,1},{13,5},{2,10},{6,14},... | collective-permute-start | bytes 3080 | tf_op jit(solution)/shard_map/ppermute | solution.py:43

commit v2 on v1

v2 whole, which is shorter than its diff:
```python
import functools
import jax
import jax.numpy as jnp
from jax import lax
from jax.experimental import pallas as pl
from jax.experimental.pallas import tpu as pltpu
from jax.sharding import PartitionSpec as P

HALF = 32
LANES = 128
FORWARD_UNROLL = 8
BACKWARD_UNROLL = 8
VMEM = 26 * 2**20

mask_slope = 4.0
resist_steep = 4.0
resist_level = 3.0
step_length = 0.5
norm_eps = 1e-06

BF16 = jnp.bfloat16
F32 = jnp.float32


def total_over(value, axis):
    peers = lax.axis_size(axis)
    if peers & (peers - 1):
        return lax.psum(value, axis)
    reach = 1
    while reach < peers:
        value = value + lax.ppermute(value, axis, [(i, i ^ reach) for i in range(peers)])
        reach *= 2
    return value


def circulant(row, shift):
    spread = jnp.broadcast_to(row, (LANES, LANES))
    return pltpu.roll(spread, shift, 1, stride=1, stride_axis=0).astype(BF16)


def index_pair(shape):
    return lax.broadcasted_iota(jnp.int32, shape, 0), lax.broadcasted_iota(jnp.int32, shape, 1)


def write_masks(masks_ref):
    a, b = index_pair((LANES, LANES))
    one, zero = jnp.ones((LANES, LANES), F32), jnp.zeros((LANES, LANES), F32)
    for slot, keep in enumerate((b >= a, b < a, a >= b, a < b)):
        masks_ref[slot] = jnp.where(keep, one, zero).astype(BF16)


def taps_kernel(col_ref, row_ref, out_ref):
    kernels, _, taps = col_ref.shape
    t, l = index_pair((taps, 2 * LANES))
    pick = jnp.where((l == t) | (l == LANES + taps - 1 - t), 1.0, 0.0).astype(BF16)
    for k in range(kernels):
        both = jnp.concatenate([col_ref[k].astype(F32), row_ref[k].astype(F32)], axis=0).astype(BF16)
        out_ref[k] = jnp.dot(both, pick, preferred_element_type=F32)


def prepare_kernel(params_ref, target_ref, mask_ref, code_ref, down_ref, up_ref):
    rows = params_ref.shape[0]
    wide = 2 * HALF
    mask = jax.nn.sigmoid(mask_slope * params_ref[...]).astype(BF16)
    code = (target_ref[...] + 1).astype(F32).astype(BF16)
    mask_ref[...] = mask
    code_ref[...] = code
    down_ref[0:wide, :] = mask[rows - wide :]
    down_ref[wide:, :] = code[rows - HALF :]
    up_ref[0:wide, :] = mask[0:wide]
    up_ref[wide:, :] = code[0:HALF]


def assemble_kernel(first_ref, mask_ref, code_ref, up_ref, down_ref, centre_ref, code_out_ref, *side_refs):
    rows, cols = mask_ref.shape
    wide = 2 * HALF
    tall = jnp.concatenate([up_ref[0:wide, :], mask_ref[...], down_ref[0:wide, :]], axis=0)
    turned = tall.astype(F32).T.astype(BF16)
    code = jnp.concatenate(
        [up_ref[wide:, :], code_ref[...], down_ref[wide:, :], jnp.zeros((wide, cols), BF16)], axis=0
    )
    code = code.astype(F32).T.astype(BF16)
    centre_ref[...] = turned
    code_out_ref[...] = code

    def right(ref):
        ref[0:wide, :] = turned[cols - wide :, :]
        ref[wide:, :] = code[cols - HALF :, :]

    def left(ref):
        ref[0:wide, :] = turned[0:wide, :]
        ref[wide:, :] = code[0:HALF, :]

    if len(side_refs) == 2:
        right(side_refs[0])
        left(side_refs[1])
    else:
        pl.when(first_ref[0] == 1)(lambda: right(side_refs[0]))
        pl.when(first_ref[0] == 0)(lambda: left(side_refs[0]))


def forward_kernel(
    weights_ref,
    ends_ref,
    centre_ref,
    before_ref,
    after_ref,
    taps_ref,
    field_ref,
    intensity_ref,
    mask_ref,
    total_ref,
    masks_ref,
    table_ref,
    columns_ref,
):
    step = pl.program_id(0)
    units = taps_ref.shape[0]
    cols = centre_ref.shape[0]
    wide = 2 * HALF
    tiles = centre_ref.shape[1] // LANES
    span = cols + wide

    @pl.when(step == 0)
    def _():
        mask_ref[0:wide, :] = jnp.where(ends_ref[0] == 1, 0.0, before_ref[0:wide, :].astype(F32)).astype(BF16)
        mask_ref[wide : wide + cols, :] = centre_ref[...]
        mask_ref[wide + cols :, :] = jnp.where(ends_ref[1] == 1, 0.0, after_ref[0:wide, :].astype(F32)).astype(BF16)
        total_ref[...] = jnp.zeros_like(total_ref)
        write_masks(masks_ref)
        table_ref[...] = jnp.zeros_like(table_ref)

    for unit in range(units):
        for part in range(2):
            base = circulant(taps_ref[unit, part : part + 1, 0:LANES], 0)
            near, far = base * masks_ref[0], base * masks_ref[1]
            table_ref[unit, part, 0:LANES, 0:LANES] = near
            table_ref[unit, part, 0:LANES, LANES:] = far
            table_ref[unit, part, LANES:, LANES:] = near[0:wide]
    table = table_ref[...].reshape(units * 2 * span, cols + 2 * wide)
    columns = jnp.dot(table, mask_ref[...], preferred_element_type=F32).astype(BF16)
    for unit in range(units):
        for part in range(2):
            at = (unit * 2 + part) * span
            for t in range(tiles):
                columns_ref[unit, t * span : (t + 1) * span, part * LANES : (part + 1) * LANES] = columns[
                    at : at + span, t * LANES : (t + 1) * LANES
                ]
    for unit in range(units):
        weight = weights_ref[step * units + unit]
        near, far = [], []
        for part in range(2):
            base = circulant(taps_ref[unit, 2 + part : 3 + part, LANES:], LANES // 2)
            near.append(base * masks_ref[2])
            far.append(base * masks_ref[3])

        def joined(half):
            return jnp.concatenate(
                [jnp.concatenate([half[0], half[1]], axis=1), jnp.concatenate([-half[1], half[0]], axis=1)], axis=0
            )

        field = jnp.dot(columns_ref[unit], joined(near), preferred_element_type=F32)
        rest = jnp.dot(columns_ref[unit, span:, :], joined(far), preferred_element_type=F32)
        for t in range(tiles):
            part = field[t * span : (t + 1) * span]
            if t + 1 < tiles:
                part = part + rest[t * span : (t + 1) * span]
            scaled = weight * part
            field_ref[unit, t] = scaled.astype(field_ref.dtype)
            total_ref[t] += scaled * part

    @pl.when(step == pl.num_programs(0) - 1)
    def _():
        for t in range(tiles):
            intensity_ref[t] = total_ref[t, :, 0:LANES] + total_ref[t, :, LANES:]


def backward_kernel(
    ends_ref,
    own_ref,
    other_ref,
    code_ref,
    code_before_ref,
    code_after_ref,
    params_ref,
    field_ref,
    taps_ref,
    gradient_ref,
    resist_ref,
    sums_ref,
    slope_ref,
    descent_ref,
    resist_all_ref,
    mismatch_ref,
    masks_ref,
    table_ref,
    source_ref,
):
    step = pl.program_id(0)
    units = taps_ref.shape[0]
    cols = code_ref.shape[0]
    wide = 2 * HALF
    tiles = own_ref.shape[0]
    span = cols + wide
    rows = (tiles - 1) * LANES

    @pl.when(step == 0)
    def _():
        for t in range(tiles):
            lanes = slice(t * LANES, (t + 1) * LANES)
            code = jnp.concatenate(
                [
                    jnp.where(ends_ref[0] == 1, 0.0, code_before_ref[wide:, lanes].astype(F32)),
                    code_ref[:, lanes].astype(F32),
                    jnp.where(ends_ref[1] == 1, 0.0, code_after_ref[wide:, lanes].astype(F32)),
                ],
                axis=0,
            )
            summed = own_ref[t] + other_ref[t]
            resist = jax.nn.sigmoid(resist_steep * (summed - resist_level))
            mismatch = resist - (code - 1.0)
            slope = 4.0 * mismatch * resist_steep * resist * (1.0 - resist)
            slope_ref[t] = jnp.where(code > 0.5, slope, 0.0)
            resist_all_ref[:, lanes] = resist[HALF : HALF + cols]
            mismatch_ref[:, lanes] = mismatch[HALF : HALF + cols]
        descent_ref[...] = jnp.zeros_like(descent_ref)
        write_masks(masks_ref)

    _, b = index_pair((LANES, LANES))
    for unit in range(units):
        near, far = [], []
        for part in range(2):
            base = circulant(taps_ref[unit, 2 + part : 3 + part, 0:LANES], LANES // 2)
            near.append(base * masks_ref[2])
            far.append(base * masks_ref[3])
        table = jnp.concatenate(
            [
                jnp.concatenate([near[0], -near[1]], axis=1),
                jnp.concatenate([near[1], near[0]], axis=1),
                jnp.concatenate([far[0], -far[1]], axis=1),
                jnp.concatenate([far[1], far[0]], axis=1),
            ],
            axis=0,
        )
        products = []
        for t in range(tiles):
            slope = jnp.concatenate([slope_ref[t], slope_ref[t]], axis=1)
            products.append((slope * field_ref[unit, t].astype(F32)).astype(BF16))
        window = jnp.concatenate(
            [
                jnp.concatenate(products[:-1], axis=0),
                jnp.concatenate(products[1:], axis=0),
            ],
            axis=1,
        )
        returned = jnp.dot(window, table, preferred_element_type=F32).astype(BF16)
        at = unit * 2 * span
        for t in range(tiles - 1):
            to = slice(t * LANES, (t + 1) * LANES)
            for part in range(2):
                piece = returned[t * span : (t + 1) * span, part * LANES : (part + 1) * LANES]
                source_ref[at + part * cols : at + (part + 1) * cols, to] = piece[0:cols]
                tail = at + 2 * cols + part * wide
                source_ref[tail : tail + wide, to] = piece[cols:]
        for part in range(2):
            base = circulant(taps_ref[unit, part : part + 1, LANES:], 0)
            table_ref[:, at + part * LANES : at + (part + 1) * LANES] = base * masks_ref[0]
        spread = [
            jnp.broadcast_to(taps_ref[unit, part : part + 1, LANES:], (LANES, LANES)) for part in range(2)
        ]
        turned = [pltpu.roll(spread[part], part * wide, 1, stride=1, stride_axis=0) for part in range(2)]
        a, _ = index_pair((LANES, LANES))
        both = jnp.where(b < wide, turned[0], turned[1])
        inside = jnp.where(b < wide, b, b - wide) < a
        table_ref[:, at + 2 * LANES : at + 3 * LANES] = jnp.where(inside, both, 0.0).astype(BF16)
    descent_ref[...] += jnp.dot(table_ref[...], source_ref[...], preferred_element_type=F32)

    @pl.when(step == pl.num_programs(0) - 1)
    def _():
        mask = jax.nn.sigmoid(mask_slope * params_ref[...])
        gradient = descent_ref[...].T * mask_slope * mask * (1.0 - mask)
        gradient_ref[...] = gradient
        resist_ref[...] = resist_all_ref[...].T[HALF : HALF + rows]
        _, b = index_pair(mismatch_ref.shape)
        mismatch = jnp.where((b >= HALF) & (b < HALF + rows), mismatch_ref[...], 0.0)
        sums_ref[0:1, :] = jnp.broadcast_to(jnp.sum(gradient * gradient), (1, LANES))
        sums_ref[1:2, :] = jnp.broadcast_to(jnp.sum(mismatch * mismatch), (1, LANES))


def finish_kernel(params_ref, gradient_ref, sums_ref, new_ref, loss_ref, *, count):
    mean = sums_ref[...] * (1.0 / count)
    scale = step_length / jnp.sqrt(mean[0:1] + norm_eps)
    new_ref[...] = params_ref[...] - gradient_ref[...] * scale
    loss_ref[...] = mean[1:2]


def whole(shape):
    return pl.BlockSpec(shape, lambda *_: (0,) * len(shape))


def limit(size):
    return pltpu.CompilerParams(vmem_limit_bytes=size)


def shards(mask_params, target, col_taps, row_taps, kernel_weights):
    rows, cols = target.shape
    kernels, _, taps = col_taps.shape
    wide = 2 * HALF
    tiles = rows // LANES + 1
    long, span = tiles * LANES, cols + wide
    units, back_units = FORWARD_UNROLL, BACKWARD_UNROLL
    if cols != LANES or rows % LANES or taps != wide + 1 or kernels % units or kernels % back_units:
        raise ValueError("block shape")
    params = mask_params[0]
    smem = pl.BlockSpec(memory_space=pltpu.SMEM)
    small = limit(4 * 2**20)

    plain = jax.ShapeDtypeStruct((rows, cols), BF16)
    edge = jax.ShapeDtypeStruct((wide + HALF, cols), BF16)
    mask_half, code, to_down, to_up = pl.pallas_call(
        prepare_kernel, out_shape=(plain, plain, edge, edge), compiler_params=small, name="prepare"
    )(params, target)
    strips = lax.axis_size("strip")
    onward = [(i, i + 1) for i in range(strips - 1)]
    back = [(i + 1, i) for i in range(strips - 1)]
    from_up = lax.ppermute(to_down, "strip", onward)
    from_down = lax.ppermute(to_up, "strip", back)
    tap_rows = pl.pallas_call(
        taps_kernel,
        out_shape=jax.ShapeDtypeStruct((kernels, 4, 2 * LANES), F32),
        compiler_params=small,
        cost_estimate=pl.CostEstimate(flops=10**8, bytes_accessed=10**6, transcendentals=0),
        name="taps",
    )(col_taps, row_taps)

    sides = lax.axis_size("col")
    place = lax.axis_index("col")
    ends = jnp.stack([place == 0, place == sides - 1]).astype(jnp.int32)
    side = jax.ShapeDtypeStruct((wide + HALF, long), BF16)
    turned = jax.ShapeDtypeStruct((cols, long), BF16)
    vmem = pl.BlockSpec(memory_space=pltpu.VMEM)
    centre, code_turned, *messages = pl.pallas_call(
        assemble_kernel,
        in_specs=[smem, vmem, vmem, vmem, vmem],
        out_shape=(turned, turned) + (side,) * (1 if sides == 2 else 2),
        compiler_params=small,
        name="assemble",
    )(ends, mask_half, code, from_up, from_down)
    if sides == 2:
        before = after = lax.ppermute(messages[0], "col", [(0, 1), (1, 0)])
    else:
        before = lax.ppermute(messages[0], "col", [(i, i + 1) for i in range(sides - 1)])
        after = lax.ppermute(messages[1], "col", [(i + 1, i) for i in range(sides - 1)])

    def taps_spec(n):
        return pl.BlockSpec((n, 4, 2 * LANES), lambda k: (k, 0, 0))

    def field_spec(n):
        return pl.BlockSpec((n, tiles, span, 2 * LANES), lambda k: (k, 0, 0, 0))

    plane = (tiles, span, LANES)
    masks = pltpu.VMEM((4, LANES, LANES), BF16)
    field, intensity = pl.pallas_call(
        forward_kernel,
        grid=(kernels // units,),
        in_specs=[smem, smem, whole((cols, long)), whole(side.shape), whole(side.shape), taps_spec(units)],
        out_specs=[field_spec(units), whole(plane)],
        out_shape=(
            jax.ShapeDtypeStruct((kernels, tiles, span, 2 * LANES), BF16),
            jax.ShapeDtypeStruct(plane, F32),
        ),
        scratch_shapes=[
            pltpu.VMEM((cols + 2 * wide, long), BF16),
            pltpu.VMEM((tiles, span, 2 * LANES), F32),
            masks,
            pltpu.VMEM((units, 2, span, cols + 2 * wide), BF16),
            pltpu.VMEM((units, tiles * span, 2 * LANES), BF16),
        ],
        compiler_params=limit(VMEM),
        name="forward",
    )(kernel_weights, ends, centre, before, after, tap_rows)

    other = lax.ppermute(intensity, "expo", [(0, 1), (1, 0)])

    gradient, resist, sums = pl.pallas_call(
        backward_kernel,
        grid=(kernels // back_units,),
        in_specs=[
            smem,
            whole(plane),
            whole(plane),
            whole((cols, long)),
            whole(side.shape),
            whole(side.shape),
            whole((rows, cols)),
            field_spec(back_units),
            taps_spec(back_units),
        ],
        out_specs=[whole((rows, cols)), whole((rows, cols)), whole((2, LANES))],
        out_shape=(
            jax.ShapeDtypeStruct((rows, cols), F32),
            jax.ShapeDtypeStruct((rows, cols), F32),
            jax.ShapeDtypeStruct((2, LANES), F32),
        ),
        scratch_shapes=[
            pltpu.VMEM(plane, F32),
            pltpu.VMEM((cols, rows), F32),
            pltpu.VMEM((cols, long), F32),
            pltpu.VMEM((cols, long), F32),
            masks,
            pltpu.VMEM((cols, back_units * 2 * span), BF16),
            pltpu.VMEM((back_units * 2 * span, rows), BF16),
        ],
        compiler_params=limit(VMEM),
        name="backward",
    )(ends, intensity, other, code_turned, before, after, params, field, tap_rows)

    for axis in ("expo", "col", "strip"):
        sums = total_over(sums, axis)
    count = 2 * rows * cols * lax.axis_size("strip") * lax.axis_size("col")
    new_params, loss = pl.pallas_call(
        functools.partial(finish_kernel, count=count),
        out_shape=(jax.ShapeDtypeStruct((rows, cols), F32), jax.ShapeDtypeStruct((1, LANES), F32)),
        compiler_params=small,
        name="finish",
    )(params, gradient, sums)
    return (new_params[None], resist, loss[0, 0:1])


def solution(mesh):
    if mesh.shape["expo"] != 2:
        raise ValueError("two exposures")
    return jax.shard_map(
        shards,
        mesh=mesh,
        in_specs=(
            P("expo", ("tiles", "strip"), "col"),
            P(("tiles", "strip"), "col"),
            P(),
            P(),
            P(),
        ),
        out_specs=(P("expo", ("tiles", "strip"), "col"), P(("tiles", "strip"), "col"), P("tiles")),
        check_vma=False,
    )
```

time: 65.1 us -> 48.5 us (0.75)
  Pallas kernels: 23.4 us -> 14.8 us
  other arithmetic: 8.45 us -> 0.09 us
  between operations: 3.17 us -> 0.7 us
  waiting for transfers between devices: 12 us -> 14.1 us
  local copies, waits for them, and re-layouts: 3.48 us -> 4.78 us
    pallas_call x3 -> x6, Pallas kernels: 23.4 us -> 14.8 us  [the longest x1 7.08 us: shards(): pl.pallas_call(forward_kernel, grid=(kernels // units,), in_specs=[smem,...]
    convert_element_type x4 -> x1, other arithmetic: 4.66 us -> 0.08 us  [shards(): ends = jnp.stack([place == 0, place == sides - 1]).astype(jnp.int32)]
    unnamed x12, local copies, waits for them, and re-layouts: 1.31 us -> 4.78 us
    ppermute x4, waiting for transfers between devices: 5.07 us -> 7.12 us  [the longest x1 4.22 us: shards(): from_down = lax.ppermute(to_up, 'strip', back)]
    rev x2 -> x0, local copies, waits for them, and re-layouts: 1.64 us -> none  [the longest x1 0.82 us: shards(): row_taps[..., ::-1]]
    sub x1 -> x0, other arithmetic: 1.58 us -> none  [shards(): new_params = mask_params - step_length * gradient[None] / root_mean]
    select_n x2 -> x0, other arithmetic: 1.58 us -> none  [the longest x1 0.9 us: neighbours(): jnp.where(first, to_next, to_previous)]
  transfers between devices with their start and end apart: 8 -> 8, of which waited for: 6 -> 8; matrix products, arithmetic and copies ran while one was open for 7% -> 0% of each run, Pallas kernels for 0% -> 0%
where the time goes in v2:
time: 48.5 us; the launch traced here: 48.2 us
  Pallas kernels  14.8 us (31%)
  waiting for transfers between devices  14.1 us (29%)
  starting transfers between devices  13.7 us (28%)
  local copies, waits for them, and re-layouts  4.78 us (10%)
  between operations  0.7 us (1%)
    pallas_call x1, Pallas kernels, shards(): pl.pallas_call(forward_kernel, grid=(kernels // units,), in_specs=[smem,...  7.08 us
    ppermute x4, waiting for transfers between devices, total_over(): lax.ppermute(value, axis, [(i, i ^ reach) for i in range(peers)])  6.97 us
    pallas_call x1, Pallas kernels, shards(): pl.pallas_call(backward_kernel, grid=(kernels // back_units,), in_specs=[...  6.13 us
    ppermute x4, starting transfers between devices, total_over(): lax.ppermute(value, axis, [(i, i ^ reach) for i in range(peers)])  5.81 us
    ppermute x1, starting transfers between devices, shards(): from_up = lax.ppermute(to_down, 'strip', onward)  4.96 us
    unnamed x12, local copies, waits for them, and re-layouts  4.78 us
    ppermute x1, waiting for transfers between devices, shards(): from_down = lax.ppermute(to_up, 'strip', back)  4.22 us
    ppermute x1, waiting for transfers between devices, shards(): other = lax.ppermute(intensity, 'expo', [(0, 1), (1, 0)])  1.57 us
  transfers between devices with their start and end apart: 8, of which 8 were waited for; matrix products, arithmetic and copies ran while one was open for 0% of the time, Pallas kernels for 0%

profile of v2, /device:TPU:0, one launch (start us, length us, event | category | flops | bytes accessed | tf_op | source)
XLA Modules:
  0.0 48.2 jit_solution(2567876709074790192)
XLA Ops:
  0.6 0.9 %copy-done = f32[1,256,128]{2,1,0:T(8,128)S(1)} copy-done((f32[1,256,128]{2,1,0:T(8,128)S(1)}, f32[1,256,128]{2,1,0:T(8,128)}, u32[]{:S(2)}) %copy-start) | copy-done | bytes 131096
  1.5 0.9 %copy-done.2 = s32[256,128]{1,0:T(8,128)S(1)} copy-done((s32[256,128]{1,0:T(8,128)S(1)}, s32[256,128]{1,0:T(8,128)}, u32[]{:S(2)}) %copy-start.2) | copy-done | bytes 131096
  2.5 5.0 %collective-permute-start = (bf16[96,128]{1,0:T(8,128)(2,1)S(1)}, bf16[96,128]{1,0:T(8,128)(2,1)S(1)}, u32[]{:S(2)}, u32[]{:S(2)}) collective-permute-start(bf16[96,128]{1,0:T(8,128)(2,1)S(1)} %get-tuple-element.19), channel_id=1, source_target_pairs={{0,4},{4,8},{8,12},{1,5},{5,9},{9,13},{2,6},{6,10},{10,14},{3,7},{... | collective-permute-start | bytes 73736 | tf_op jit(solution)/shard_map/ppermute | solution.py:326
  7.4 1.3 %collective-permute-start.1 = (bf16[96,128]{1,0:T(8,128)(2,1)S(1)}, bf16[96,128]{1,0:T(8,128)(2,1)S(1)}, u32[]{:S(2)}, u32[]{:S(2)}) collective-permute-start(bf16[96,128]{1,0:T(8,128)(2,1)S(1)} %get-tuple-element.20), channel_id=1, source_target_pairs={{4,0},{8,4},{12,8},{5,1},{9,5},{13,9},{6,2},{10,6},{14,10},{7,3},{... | collective-permute-start | bytes 73736 | tf_op jit(solution)/shard_map/ppermute | solution.py:327
  8.9 4.2 %collective-permute-done.1.down_ref = bf16[96,128]{1,0:T(8,128)(2,1)S(1)} collective-permute-done((bf16[96,128]{1,0:T(8,128)(2,1)S(1)}, bf16[96,128]{1,0:T(8,128)(2,1)S(1)}, u32[]{:S(2)}, u32[]{:S(2)}) %collective-permute-start.1) | collective-permute-done | bytes 24608 | tf_op jit(solution)/shard_map/ppermute | solution.py:327
  13.2 0.7 %assemble.1 = (bf16[128,384]{1,0:T(8,128)(2,1)S(1)}, bf16[128,384]{1,0:T(8,128)(2,1)S(1)}, bf16[96,384]{1,0:T(8,128)(2,1)S(1)}) custom-call(s32[2]{0:T(128)S(1)} %add_convert_fusion.first_ref.ends_ref, bf16[256,128]{1,0:T(8,128)(2,1)S(1)} %get-tuple-element.17.mask_ref, bf16[256,128]{1,0:T(8,128)(2,1)S(1)} %get-tuple-element.18.code_ref, ...), custom_call_target="tpu_custom_call" | custom-call | tf_op jit(solution)/shard_map/assemble/pallas_call | solution.py:342
  13.9 1.6 %collective-permute-start.2 = (bf16[96,384]{1,0:T(8,128)(2,1)S(1)}, bf16[96,384]{1,0:T(8,128)(2,1)S(1)}, u32[]{:S(2)}, u32[]{:S(2)}) collective-permute-start(bf16[96,384]{1,0:T(8,128)(2,1)S(1)} %get-tuple-element.22), channel_id=1, source_target_pairs={{0,2},{2,0},{1,3},{3,1},{4,6},{6,4},{5,7},{7,5},{8,10},{10,8},{9,1... | collective-permute-start | bytes 221192 | tf_op jit(solution)/shard_map/ppermute | solution.py:350
  15.4 0.7 %copy-done.4 = bf16[24,2,65]{2,1,0:T(2,128)(2,1)S(1)} copy-done((bf16[24,2,65]{2,1,0:T(2,128)(2,1)S(1)}, bf16[24,2,65]{2,1,0:T(2,128)(2,1)}, u32[]{:S(2)}) %copy-start.4) | copy-done | bytes 6264
  16.1 0.7 %copy-done.5 = bf16[24,2,65]{2,1,0:T(2,128)(2,1)S(1)} copy-done((bf16[24,2,65]{2,1,0:T(2,128)(2,1)S(1)}, bf16[24,2,65]{2,1,0:T(2,128)(2,1)}, u32[]{:S(2)}) %copy-start.5) | copy-done | bytes 6264
  16.8 0.2 taps.1.taps_ref
  17.1 1.2 %collective-permute-done.2.before_ref.after_ref.code_before_ref.code_after_ref = bf16[96,384]{1,0:T(8,128)(2,1)S(1)} collective-permute-done((bf16[96,384]{1,0:T(8,128)(2,1)S(1)}, bf16[96,384]{1,0:T(8,128)(2,1)S(1)}, u32[]{:S(2)}, u32[]{:S(2)}) %collective-permute-start.2) | collective-permute-done | bytes 73760 | tf_op jit(solution)/shard_map/ppermute | solution.py:350
  18.3 0.7 %copy-done.3 = f32[24]{0:T(128)S(1)} copy-done((f32[24]{0:T(128)S(1)}, f32[24]{0:T(128)}, u32[]{:S(2)}) %copy-start.3) | copy-done | bytes 120
  18.9 7.1 %forward.1 = (bf16[24,3,192,256]{3,2,1,0:T(8,128)(2,1)S(1)}, f32[3,192,128]{2,1,0:T(8,128)S(1)}) custom-call(f32[24]{0:T(128)S(1)} %copy-done.3, s32[2]{0:T(128)S(1)} %add_convert_fusion.first_ref.ends_ref, bf16[128,384]{1,0:T(8,128)(2,1)S(1)} %get-tuple-element.21.centre_ref, ...), custom_call_target="tpu_custom_call" | custom-call | tf_op jit(solution)/shard_map/forward/pallas_call | solution.py:363
  26.1 1.6 %collective-permute-done.3.other_ref = f32[3,192,128]{2,1,0:T(8,128)S(1)} collective-permute-done((f32[3,192,128]{2,1,0:T(8,128)S(1)}, f32[3,192,128]{2,1,0:T(8,128)S(1)}, u32[]{:S(2)}, u32[]{:S(2)}) %collective-permute-start.3) | collective-permute-done | bytes 294944 | tf_op jit(solution)/shard_map/ppermute | solution.py:383
  27.7 0.9 %copy-done.1 = f32[1,256,128]{2,1,0:T(8,128)S(1)} copy-done((f32[1,256,128]{2,1,0:T(8,128)S(1)}, f32[1,256,128]{2,1,0:T(8,128)}, u32[]{:S(2)}) %copy-start.1) | copy-done | bytes 131096
  28.6 6.1 %backward.1 = (f32[256,128]{1,0:T(8,128)S(1)}, f32[256,128]{1,0:T(8,128)}, f32[2,128]{1,0:T(2,128)S(1)}) custom-call(s32[2]{0:T(128)S(1)} %add_convert_fusion.first_ref.ends_ref, f32[3,192,128]{2,1,0:T(8,128)S(1)} %get-tuple-element.23.own_ref, f32[3,192,128]{2,1,0:T(8,128)S(1)} %collective-permute-done.3.other_ref, ...), custom_call_target="tpu_custom_call" | custom-call | tf_op jit(solution)/shard_map/backward/pallas_call | solution.py:385
  34.8 1.0 %collective-permute-done.4 = f32[2,128]{1,0:T(2,128)S(1)} collective-permute-done((f32[2,128]{1,0:T(2,128)S(1)}, f32[2,128]{1,0:T(2,128)S(1)}, u32[]{:S(2)}, u32[]{:S(2)}) %collective-permute-start.4) | collective-permute-done | bytes 1056 | tf_op jit(solution)/shard_map/ppermute | solution.py:31
  35.9 1.5 %collective-permute-start.5 = (f32[2,128]{1,0:T(2,128)S(1)}, f32[2,128]{1,0:T(2,128)S(1)}, u32[]{:S(2)}, u32[]{:S(2)}) collective-permute-start(f32[2,128]{1,0:T(2,128)S(1)} %add.12), channel_id=1, source_target_pairs={{0,2},{2,0},{1,3},{3,1},{4,6},{6,4},{5,7},{7,5},{8,10},{10,8},{9,1... | collective-permute-start | bytes 3080 | tf_op jit(solution)/shard_map/ppermute | solution.py:31
  37.4 2.1 %collective-permute-done.5 = f32[2,128]{1,0:T(2,128)S(1)} collective-permute-done((f32[2,128]{1,0:T(2,128)S(1)}, f32[2,128]{1,0:T(2,128)S(1)}, u32[]{:S(2)}, u32[]{:S(2)}) %collective-permute-start.5) | collective-permute-done | bytes 1056 | tf_op jit(solution)/shard_map/ppermute | solution.py:31
  39.4 1.6 %collective-permute-start.6 = (f32[2,128]{1,0:T(2,128)S(1)}, f32[2,128]{1,0:T(2,128)S(1)}, u32[]{:S(2)}, u32[]{:S(2)}) collective-permute-start(f32[2,128]{1,0:T(2,128)S(1)} %add.13), channel_id=1, source_target_pairs={{0,4},{4,0},{8,12},{12,8},{1,5},{5,1},{9,13},{13,9},{2,6},{6,2},{1... | collective-permute-start | bytes 3080 | tf_op jit(solution)/shard_map/ppermute | solution.py:31
  41.0 2.0 %collective-permute-done.6 = f32[2,128]{1,0:T(2,128)S(1)} collective-permute-done((f32[2,128]{1,0:T(2,128)S(1)}, f32[2,128]{1,0:T(2,128)S(1)}, u32[]{:S(2)}, u32[]{:S(2)}) %collective-permute-start.6) | collective-permute-done | bytes 1056 | tf_op jit(solution)/shard_map/ppermute | solution.py:31
  43.0 2.6 %collective-permute-start.7 = (f32[2,128]{1,0:T(2,128)S(1)}, f32[2,128]{1,0:T(2,128)S(1)}, u32[]{:S(2)}, u32[]{:S(2)}) collective-permute-start(f32[2,128]{1,0:T(2,128)S(1)} %add.14), channel_id=1, source_target_pairs={{0,8},{4,12},{8,0},{12,4},{1,9},{5,13},{9,1},{13,5},{2,10},{6,14},... | collective-permute-start | bytes 3080 | tf_op jit(solution)/shard_map/ppermute | solution.py:31
  45.6 1.9 %collective-permute-done.7 = f32[2,128]{1,0:T(2,128)S(1)} collective-permute-done((f32[2,128]{1,0:T(2,128)S(1)}, f32[2,128]{1,0:T(2,128)S(1)}, u32[]{:S(2)}, u32[]{:S(2)}) %collective-permute-start.7) | collective-permute-done | bytes 1056 | tf_op jit(solution)/shard_map/ppermute | solution.py:31
  47.5 0.7 %finish.1 = (f32[256,128]{1,0:T(8,128)}, f32[1,128]{1,0:T(1,128)}) custom-call(f32[256,128]{1,0:T(8,128)S(1)} %bitcast.8, f32[256,128]{1,0:T(8,128)S(1)} %get-tuple-element.26.gradient_ref, f32[2,128]{1,0:T(2,128)S(1)} %add.15.sums_ref), custom_call_target="tpu_custom_call" | custom-call | tf_op jit(solution)/shard_map/finish/pallas_call | solution.py:421
  (15 shorter events, 0.5 us)
Async XLA Ops:
  0.6 0.9 %copy-start = (f32[1,256,128]{2,1,0:T(8,128)S(1)}, f32[1,256,128]{2,1,0:T(8,128)}, u32[]{:S(2)}) copy-start(f32[1,256,128]{2,1,0:T(8,128)} %param.5) | copy-start | bytes 393220
  1.5 0.9 %copy-start.2 = (s32[256,128]{1,0:T(8,128)S(1)}, s32[256,128]{1,0:T(8,128)}, u32[]{:S(2)}) copy-start(s32[256,128]{1,0:T(8,128)} %target_ref.1) | copy-start | bytes 393220
  2.5 6.5 %collective-permute-start = (bf16[96,128]{1,0:T(8,128)(2,1)S(1)}, bf16[96,128]{1,0:T(8,128)(2,1)S(1)}, u32[]{:S(2)}, u32[]{:S(2)}) collective-permute-start(bf16[96,128]{1,0:T(8,128)(2,1)S(1)} %get-tuple-element.19), channel_id=1, source_target_pairs={{0,4},{4,8},{8,12},{1,5},{5,9},{9,13},{2,6},{6,10},{10,14},{3,7},{... | collective-permute-start | bytes 73736 | tf_op jit(solution)/shard_map/ppermute | solution.py:326
  7.4 5.7 %collective-permute-start.1 = (bf16[96,128]{1,0:T(8,128)(2,1)S(1)}, bf16[96,128]{1,0:T(8,128)(2,1)S(1)}, u32[]{:S(2)}, u32[]{:S(2)}) collective-permute-start(bf16[96,128]{1,0:T(8,128)(2,1)S(1)} %get-tuple-element.20), channel_id=1, source_target_pairs={{4,0},{8,4},{12,8},{5,1},{9,5},{13,9},{6,2},{10,6},{14,10},{7,3},{... | collective-permute-start | bytes 73736 | tf_op jit(solution)/shard_map/ppermute | solution.py:327
  13.9 4.4 %collective-permute-start.2 = (bf16[96,384]{1,0:T(8,128)(2,1)S(1)}, bf16[96,384]{1,0:T(8,128)(2,1)S(1)}, u32[]{:S(2)}, u32[]{:S(2)}) collective-permute-start(bf16[96,384]{1,0:T(8,128)(2,1)S(1)} %get-tuple-element.22), channel_id=1, source_target_pairs={{0,2},{2,0},{1,3},{3,1},{4,6},{6,4},{5,7},{7,5},{8,10},{10,8},{9,1... | collective-permute-start | bytes 221192 | tf_op jit(solution)/shard_map/ppermute | solution.py:350
  15.4 0.7 %copy-start.4 = (bf16[24,2,65]{2,1,0:T(2,128)(2,1)S(1)}, bf16[24,2,65]{2,1,0:T(2,128)(2,1)}, u32[]{:S(2)}) copy-start(bf16[24,2,65]{2,1,0:T(2,128)(2,1)} %col_ref.1) | copy-start | bytes 18724
  16.1 0.7 %copy-start.5 = (bf16[24,2,65]{2,1,0:T(2,128)(2,1)S(1)}, bf16[24,2,65]{2,1,0:T(2,128)(2,1)}, u32[]{:S(2)}) copy-start(bf16[24,2,65]{2,1,0:T(2,128)(2,1)} %row_ref.1) | copy-start | bytes 18724
  18.3 0.7 %copy-start.3 = (f32[24]{0:T(128)S(1)}, f32[24]{0:T(128)}, u32[]{:S(2)}) copy-start(f32[24]{0:T(128)} %weights_ref.1) | copy-start | bytes 292
  26.0 1.6 %collective-permute-start.3 = (f32[3,192,128]{2,1,0:T(8,128)S(1)}, f32[3,192,128]{2,1,0:T(8,128)S(1)}, u32[]{:S(2)}, u32[]{:S(2)}) collective-permute-start(f32[3,192,128]{2,1,0:T(8,128)S(1)} %get-tuple-element.23.own_ref), channel_id=1, source_target_pairs={{0,1},{1,0},{2,3},{3,2},{4,5},{5,4},{6,7},{7,6},{8,9},{9,8},{10,11... | collective-permute-start | bytes 884744 | tf_op jit(solution)/shard_map/ppermute | solution.py:383
  27.7 0.9 %copy-start.1 = (f32[1,256,128]{2,1,0:T(8,128)S(1)}, f32[1,256,128]{2,1,0:T(8,128)}, u32[]{:S(2)}) copy-start(f32[1,256,128]{2,1,0:T(8,128)} %param.5) | copy-start | bytes 393220
  34.7 1.2 %collective-permute-start.4 = (f32[2,128]{1,0:T(2,128)S(1)}, f32[2,128]{1,0:T(2,128)S(1)}, u32[]{:S(2)}, u32[]{:S(2)}) collective-permute-start(f32[2,128]{1,0:T(2,128)S(1)} %get-tuple-element.27), channel_id=1, source_target_pairs={{0,1},{1,0},{2,3},{3,2},{4,5},{5,4},{6,7},{7,6},{8,9},{9,8},{10,11... | collective-permute-start | bytes 3080 | tf_op jit(solution)/shard_map/ppermute | solution.py:31
  35.9 3.6 %collective-permute-start.5 = (f32[2,128]{1,0:T(2,128)S(1)}, f32[2,128]{1,0:T(2,128)S(1)}, u32[]{:S(2)}, u32[]{:S(2)}) collective-permute-start(f32[2,128]{1,0:T(2,128)S(1)} %add.12), channel_id=1, source_target_pairs={{0,2},{2,0},{1,3},{3,1},{4,6},{6,4},{5,7},{7,5},{8,10},{10,8},{9,1... | collective-permute-start | bytes 3080 | tf_op jit(solution)/shard_map/ppermute | solution.py:31
  39.4 3.6 %collective-permute-start.6 = (f32[2,128]{1,0:T(2,128)S(1)}, f32[2,128]{1,0:T(2,128)S(1)}, u32[]{:S(2)}, u32[]{:S(2)}) collective-permute-start(f32[2,128]{1,0:T(2,128)S(1)} %add.13), channel_id=1, source_target_pairs={{0,4},{4,0},{8,12},{12,8},{1,5},{5,1},{9,13},{13,9},{2,6},{6,2},{1... | collective-permute-start | bytes 3080 | tf_op jit(solution)/shard_map/ppermute | solution.py:31
  43.0 4.5 %collective-permute-start.7 = (f32[2,128]{1,0:T(2,128)S(1)}, f32[2,128]{1,0:T(2,128)S(1)}, u32[]{:S(2)}, u32[]{:S(2)}) collective-permute-start(f32[2,128]{1,0:T(2,128)S(1)} %add.14), channel_id=1, source_target_pairs={{0,8},{4,12},{8,0},{12,4},{1,9},{5,13},{9,1},{13,5},{2,10},{6,14},... | collective-permute-start | bytes 3080 | tf_op jit(solution)/shard_map/ppermute | solution.py:31

commit v3 on v0

v3 whole, which is shorter than its diff:
```python
import functools
import jax
import jax.numpy as jnp
from jax import lax
from jax.experimental import pallas as pl
from jax.experimental.pallas import tpu as pltpu
from jax.sharding import PartitionSpec as P

HALF = 32
LANES = 128
FORWARD_UNROLL = 8
BACKWARD_UNROLL = 8
VMEM = 16 * 2**20

mask_slope = 4.0
resist_steep = 4.0
resist_level = 3.0
step_length = 0.5
norm_eps = 1e-06

BF16 = jnp.bfloat16
F32 = jnp.float32


def ring(axis, step):
    peers = lax.axis_size(axis)
    return [(i, (i + step) % peers) for i in range(peers)]


def partners(peers, other):
    return [(2 * i + core, 2 * other(i) + 1 - core) for i in range(peers) for core in range(2)]


def total_over(value, axis):
    peers = lax.axis_size(axis)
    if peers & (peers - 1):
        return lax.psum(value, axis)
    both = (axis, "expo")
    if peers == 4:
        one, two, three = (
            lax.ppermute(value, both, partners(peers, lambda i, d=d: (i + d) % peers)) for d in (1, 2, 3)
        )
        return (value + two) + (one + three)
    reach = 1
    while reach < peers:
        value = value + lax.ppermute(value, both, partners(peers, lambda i, r=reach: i ^ r))
        reach *= 2
    return value


def circulant(row, shift):
    spread = jnp.broadcast_to(row, (LANES, LANES))
    return pltpu.roll(spread, shift, 1, stride=1, stride_axis=0).astype(BF16)


def index_pair(shape):
    return lax.broadcasted_iota(jnp.int32, shape, 0), lax.broadcasted_iota(jnp.int32, shape, 1)


def write_masks(masks_ref):
    a, b = index_pair((LANES, LANES))
    one, zero = jnp.ones((LANES, LANES), F32), jnp.zeros((LANES, LANES), F32)
    for slot, keep in enumerate((b >= a, b < a, a >= b, a < b)):
        masks_ref[slot] = jnp.where(keep, one, zero).astype(BF16)


def taps_kernel(weights_ref, col_ref, row_ref, out_ref):
    kernels, _, taps = col_ref.shape
    t, l = index_pair((taps, 2 * LANES))
    pick = jnp.where((l == t) | (l == LANES + taps - 1 - t), 1.0, 0.0).astype(BF16)
    for k in range(kernels):
        both = jnp.concatenate([col_ref[k].astype(F32), row_ref[k].astype(F32)], axis=0).astype(BF16)
        out_ref[k, 0:4] = jnp.dot(both, pick, preferred_element_type=F32)
        out_ref[k, 4:8] = jnp.full((4, 2 * LANES), weights_ref[k], F32)


def prepare_kernel(
    params_hbm, target_hbm, params_ref, mask_ref, code_ref, down_ref, up_ref, target_ref, sems
):
    rows = params_ref.shape[0]
    wide = 2 * HALF
    copies = [
        pltpu.make_async_copy(params_hbm, params_ref, sems.at[0]),
        pltpu.make_async_copy(target_hbm, target_ref, sems.at[1]),
    ]
    for copy in copies:
        copy.start()
    for copy in copies:
        copy.wait()
    mask = jax.nn.sigmoid(mask_slope * params_ref[...]).astype(BF16)
    code = (target_ref[...] + 1).astype(F32).astype(BF16)
    mask_ref[...] = mask
    code_ref[...] = code
    down_ref[0:wide, :] = mask[rows - wide :]
    down_ref[wide:, :] = code[rows - HALF :]
    up_ref[0:wide, :] = mask[0:wide]
    up_ref[wide:, :] = code[0:HALF]


def unless(end, values):
    return jnp.where(end == 1, 0.0, values.astype(F32))


def assemble_kernel(
    ends_ref, mask_ref, code_ref, up_ref, down_ref, _, centre_ref, code_out_ref, *side_refs
):
    rows, cols = mask_ref.shape
    wide = 2 * HALF
    above, below = unless(ends_ref[2], up_ref[...]), unless(ends_ref[3], down_ref[...])
    tall = jnp.concatenate([above[0:wide], mask_ref[...].astype(F32), below[0:wide]], axis=0)
    turned = tall.T.astype(BF16)
    code = jnp.concatenate(
        [above[wide:], code_ref[...].astype(F32), below[wide:], jnp.zeros((wide, cols), F32)], axis=0
    )
    code = code.T.astype(BF16)
    centre_ref[...] = turned
    code_out_ref[...] = code

    def right(ref):
        ref[0:wide, :] = turned[cols - wide :, :]
        ref[wide:, :] = code[cols - HALF :, :]

    def left(ref):
        ref[0:wide, :] = turned[0:wide, :]
        ref[wide:, :] = code[0:HALF, :]

    if len(side_refs) == 2:
        right(side_refs[0])
        left(side_refs[1])
    else:
        pl.when(ends_ref[0] == 1)(lambda: right(side_refs[0]))
        pl.when(ends_ref[0] == 0)(lambda: left(side_refs[0]))


def forward_kernel(
    ends_ref,
    centre_ref,
    before_ref,
    after_ref,
    taps_ref,
    field_ref,
    intensity_ref,
    mask_ref,
    total_ref,
    masks_ref,
    table_ref,
    columns_ref,
):
    kernels = taps_ref.shape[0]
    units = columns_ref.shape[0]
    cols = centre_ref.shape[0]
    wide = 2 * HALF
    long = centre_ref.shape[1]
    tiles = long // LANES
    blocks = cols // wide + 1
    span = cols + wide

    mask = jnp.concatenate(
        [
            unless(ends_ref[0], before_ref[0:wide, :]).astype(BF16),
            centre_ref[...],
            unless(ends_ref[1], after_ref[0:wide, :]).astype(BF16),
        ],
        axis=0,
    )
    for block in range(blocks):
        mask_ref[:, block * long : (block + 1) * long] = mask[block * wide : block * wide + LANES]
    total_ref[...] = jnp.zeros_like(total_ref)
    write_masks(masks_ref)

    def group(step, carry):
        for unit in range(units):
            for part in range(2):
                row = taps_ref[step * units + unit, part : part + 1, 0:LANES]
                base = circulant(row, 0)[0:wide]
                at = (unit * 2 + part) * wide
                table_ref[at : at + wide, :] = base * masks_ref[0, 0:wide]
        columns = jnp.dot(table_ref[...], mask_ref[...], preferred_element_type=F32).astype(BF16)
        for unit in range(units):
            for part in range(2):
                at = (unit * 2 + part) * wide
                for block in range(blocks):
                    for t in range(tiles):
                        lane = block * long + t * LANES
                        to = t * span + block * wide
                        columns_ref[unit, to : to + wide, part * LANES : (part + 1) * LANES] = columns[
                            at : at + wide, lane : lane + LANES
                        ]
        for unit in range(units):
            kernel = step * units + unit
            near, far = [], []
            for part in range(2):
                base = circulant(taps_ref[kernel, 2 + part : 3 + part, LANES:], LANES // 2)
                near.append(base * masks_ref[2])
                far.append(base * masks_ref[3])
            near = [
                jnp.concatenate([near[0], near[1]], axis=1),
                jnp.concatenate([-near[1], near[0]], axis=1),
            ]
            far = [
                jnp.concatenate([far[0], far[1]], axis=1),
                jnp.concatenate([-far[1], far[0]], axis=1),
            ]
            weight = taps_ref[kernel, 4:5, :]
            edge = (tiles - 1) * span
            window = jnp.concatenate([columns_ref[unit, 0:edge], columns_ref[unit, span:]], axis=1)
            inner = jnp.dot(window, jnp.concatenate(near + far, axis=0), preferred_element_type=F32)
            outer = jnp.dot(
                columns_ref[unit, edge:], jnp.concatenate(near, axis=0), preferred_element_type=F32
            )
            for t in range(tiles):
                part = inner[t * span : (t + 1) * span] if t + 1 < tiles else outer
                scaled = weight * part
                field_ref[kernel, t] = scaled.astype(field_ref.dtype)
                total_ref[t] += scaled * part
        return carry

    lax.fori_loop(0, kernels // units, group, 0)
    for t in range(tiles):
        intensity_ref[t] = total_ref[t, :, 0:LANES] + total_ref[t, :, LANES:]


def backward_kernel(
    ends_ref,
    own_ref,
    other_ref,
    code_ref,
    code_before_ref,
    code_after_ref,
    params_ref,
    field_ref,
    taps_ref,
    gradient_ref,
    resist_hbm,
    sums_ref,
    slope_ref,
    descent_ref,
    resist_ref,
    masks_ref,
    table_ref,
    source_ref,
    sem,
):
    kernels = taps_ref.shape[0]
    cols = code_ref.shape[0]
    wide = 2 * HALF
    tiles = own_ref.shape[0]
    span = cols + wide
    rows = (tiles - 1) * LANES
    units = table_ref.shape[1] // (2 * span)

    resists, loss = [], 0.0
    for t in range(tiles):
        lanes = slice(t * LANES, (t + 1) * LANES)
        code = jnp.concatenate(
            [
                unless(ends_ref[0], code_before_ref[wide:, lanes]),
                code_ref[:, lanes].astype(F32),
                unless(ends_ref[1], code_after_ref[wide:, lanes]),
            ],
            axis=0,
        )
        summed = own_ref[t] + other_ref[t]
        resist = jax.nn.sigmoid(resist_steep * (summed - resist_level))
        mismatch = resist - (code - 1.0)
        slope = 4.0 * mismatch * resist_steep * resist * (1.0 - resist)
        slope = jnp.where(code > 0.5, slope, 0.0).astype(BF16)
        slope_ref[t] = jnp.concatenate([slope, slope], axis=1)
        resists.append(resist[HALF : HALF + cols])
        mine = mismatch[HALF : HALF + cols]
        _, lane = index_pair(mine.shape)
        lane = lane + t * LANES
        mine = jnp.where((lane >= HALF) & (lane < HALF + rows), mine, 0.0)
        loss = loss + mine * mine
    resist_ref[...] = jnp.concatenate(resists, axis=1).T[HALF : HALF + rows]
    copy = pltpu.make_async_copy(resist_ref, resist_hbm, sem)
    copy.start()
    descent_ref[...] = jnp.zeros_like(descent_ref)
    write_masks(masks_ref)

    def group(step, carry):
        a, b = index_pair((LANES, LANES))
        inside = jnp.where(b < wide, b, b - wide) < a
        for unit in range(units):
            kernel = step * units + unit
            near, far = [], []
            for part in range(2):
                base = circulant(taps_ref[kernel, 2 + part : 3 + part, 0:LANES], LANES // 2)
                near.append(base * masks_ref[2])
                far.append(base * masks_ref[3])
            table = jnp.concatenate(
                [
                    jnp.concatenate([near[0], -near[1]], axis=1),
                    jnp.concatenate([near[1], near[0]], axis=1),
                    jnp.concatenate([far[0], -far[1]], axis=1),
                    jnp.concatenate([far[1], far[0]], axis=1),
                ],
                axis=0,
            )
            products = [slope_ref[t] * field_ref[kernel, t] for t in range(tiles)]
            window = jnp.concatenate(
                [jnp.concatenate(products[:-1], axis=0), jnp.concatenate(products[1:], axis=0)], axis=1
            )
            returned = jnp.dot(window, table, preferred_element_type=F32).astype(BF16)
            at = unit * 2 * span
            for t in range(tiles - 1):
                to = slice(t * LANES, (t + 1) * LANES)
                for part in range(2):
                    piece = returned[t * span : (t + 1) * span, part * LANES : (part + 1) * LANES]
                    source_ref[at + part * cols : at + (part + 1) * cols, to] = piece[0:cols]
                    tail = at + 2 * cols + part * wide
                    source_ref[tail : tail + wide, to] = piece[cols:]
            turned = []
            for part in range(2):
                row = taps_ref[kernel, part : part + 1, LANES:]
                table_ref[:, at + part * LANES : at + (part + 1) * LANES] = circulant(row, 0) * masks_ref[0]
                spread = jnp.broadcast_to(row, (LANES, LANES))
                turned.append(pltpu.roll(spread, part * wide, 1, stride=1, stride_axis=0))
            both = jnp.where(b < wide, turned[0], turned[1])
            table_ref[:, at + 2 * LANES : at + 3 * LANES] = jnp.where(inside, both, 0.0).astype(BF16)
        descent_ref[...] += jnp.dot(table_ref[...], source_ref[...], preferred_element_type=F32)
        return carry

    lax.fori_loop(0, kernels // units, group, 0)
    mask = jax.nn.sigmoid(mask_slope * params_ref[...])
    gradient = descent_ref[...].T * mask_slope * mask * (1.0 - mask)
    gradient_ref[...] = gradient
    sums_ref[0:1, :] = jnp.broadcast_to(jnp.sum(gradient * gradient), (1, LANES))
    sums_ref[1:2, :] = jnp.broadcast_to(jnp.sum(loss), (1, LANES))
    copy.wait()


def finish_kernel(params_ref, gradient_ref, sums_ref, new_ref, loss_ref, *, count):
    mean = sums_ref[...] * (1.0 / count)
    scale = step_length / jnp.sqrt(mean[0:1] + norm_eps)
    new_ref[...] = params_ref[...] - gradient_ref[...] * scale
    loss_ref[...] = mean[1:2]


def shards(mask_params, target, col_taps, row_taps, kernel_weights):
    rows, cols = target.shape
    kernels, _, taps = col_taps.shape
    wide = 2 * HALF
    tiles = rows // LANES + 1
    long, span = tiles * LANES, cols + wide
    units, back_units = FORWARD_UNROLL, BACKWARD_UNROLL
    if cols != LANES or rows % LANES or taps != wide + 1 or kernels % units or kernels % back_units:
        raise ValueError("block shape")
    smem = pl.BlockSpec(memory_space=pltpu.SMEM)
    vmem = pl.BlockSpec(memory_space=pltpu.VMEM)
    hbm = pl.BlockSpec(memory_space=pltpu.HBM)
    array = jax.ShapeDtypeStruct

    def call(body, name, specs, outs, out_specs=None, scratch=(), grant=4 * 2**20, flops=10**6):
        return pl.pallas_call(
            body,
            in_specs=specs,
            out_shape=outs,
            out_specs=[vmem] * len(outs) if out_specs is None else out_specs,
            scratch_shapes=scratch,
            compiler_params=pltpu.CompilerParams(vmem_limit_bytes=grant),
            cost_estimate=pl.CostEstimate(flops=flops, bytes_accessed=10**6, transcendentals=0),
            name=name,
        )

    plain, edge = array((rows, cols), BF16), array((wide + HALF, cols), BF16)
    full = array((rows, cols), F32)
    params, mask_half, code, to_down, to_up = call(
        prepare_kernel,
        "prepare",
        [hbm, hbm],
        (full, plain, plain, edge, edge),
        scratch=[pltpu.VMEM((rows, cols), target.dtype), pltpu.SemaphoreType.DMA((2,))],
    )(mask_params[0], target)
    from_up = lax.ppermute(to_down, "strip", ring("strip", 1))
    from_down = lax.ppermute(to_up, "strip", ring("strip", -1))
    (tap_rows,) = call(
        taps_kernel, "taps", [smem, vmem, vmem], (array((kernels, 8, 2 * LANES), F32),), flops=10**8
    )(kernel_weights, col_taps, row_taps)

    sides, strips = lax.axis_size("col"), lax.axis_size("strip")
    place, level = lax.axis_index("col"), lax.axis_index("strip")
    ends = jnp.stack([place == 0, place == sides - 1, level == 0, level == strips - 1]).astype(jnp.int32)
    side, turned = array((wide + HALF, long), BF16), array((cols, long), BF16)
    centre, code_turned, *messages = call(
        assemble_kernel,
        "assemble",
        [smem, vmem, vmem, vmem, vmem, pl.BlockSpec(memory_space=pl.ANY)],
        (turned, turned) + (side,) * (1 if sides == 2 else 2),
    )(ends, mask_half, code, from_up, from_down, tap_rows)
    if sides == 2:
        before = after = lax.ppermute(messages[0], "col", ring("col", 1))
    else:
        before = lax.ppermute(messages[0], "col", ring("col", 1))
        after = lax.ppermute(messages[1], "col", ring("col", -1))

    masks = pltpu.VMEM((4, LANES, LANES), BF16)
    plane = (tiles, span, LANES)
    field, intensity = call(
        forward_kernel,
        "forward",
        [smem] + [vmem] * 4,
        (array((kernels, tiles, span, 2 * LANES), BF16), array(plane, F32)),
        scratch=[
            pltpu.VMEM((LANES, (cols // wide + 1) * long), BF16),
            pltpu.VMEM((tiles, span, 2 * LANES), F32),
            masks,
            pltpu.VMEM((units * 2 * wide, LANES), BF16),
            pltpu.VMEM((units, tiles * span, 2 * LANES), BF16),
        ],
        grant=VMEM,
    )(ends, centre, before, after, tap_rows)

    other = lax.ppermute(intensity, "expo", [(0, 1), (1, 0)])

    gradient, resist, sums = call(
        backward_kernel,
        "backward",
        [smem] + [vmem] * 8,
        (full, full, array((2, LANES), F32)),
        out_specs=[vmem, hbm, vmem],
        scratch=[
            pltpu.VMEM((tiles, span, 2 * LANES), BF16),
            pltpu.VMEM((cols, rows), F32),
            pltpu.VMEM((rows, cols), F32),
            masks,
            pltpu.VMEM((cols, back_units * 2 * span), BF16),
            pltpu.VMEM((back_units * 2 * span, rows), BF16),
            pltpu.SemaphoreType.DMA,
        ],
        grant=VMEM,
    )(ends, intensity, other, code_turned, before, after, params, field, tap_rows)

    sums = sums + lax.ppermute(sums, "expo", [(0, 1), (1, 0)])
    for axis in ("col", "strip"):
        sums = total_over(sums, axis)
    count = 2 * rows * cols * strips * sides
    new_params, loss = call(
        functools.partial(finish_kernel, count=count), "finish", [vmem] * 3, (full, array((1, LANES), F32))
    )(params, gradient, sums)
    return (new_params[None], resist, loss[0, 0:1])


def solution(mesh):
    if mesh.shape["expo"] != 2:
        raise ValueError("two exposures")
    return jax.shard_map(
        shards,
        mesh=mesh,
        in_specs=(
            P("expo", ("tiles", "strip"), "col"),
            P(("tiles", "strip"), "col"),
            P(),
            P(),
            P(),
        ),
        out_specs=(P("expo", ("tiles", "strip"), "col"), P(("tiles", "strip"), "col"), P("tiles")),
        check_vma=False,
    )
```

time: 807 us -> 42 us (0.05)
  starting transfers between devices: 233 us -> 11.6 us
  local copies, waits for them, and re-layouts: 185 us -> 3.87 us
  loops' own time: 116 us -> 0 us
  waiting for transfers between devices: 114 us -> 11.2 us
  other arithmetic: 65.4 us -> 0.09 us
  blocking collectives: 47.8 us -> 0 us
  matrix products: 23.3 us -> 0 us
  between operations: 16.7 us -> 0.71 us
  Pallas kernels: 0 us -> 14.3 us
    ppermute x100 -> x9, starting transfers between devices: 233 us -> 11.6 us  [the longest x1 3.1 us: shards(): from_up = lax.ppermute(to_down, 'strip', ring('strip', 1))]
    another operation x2 -> x0, loops' own time: 116 us -> none  [the longest x1 67 us: shards(): lax.scan(add_gradient, zero_field, (kernel_ids, stored[0], stored[1]))]
    ppermute x100 -> x9, waiting for transfers between devices: 96.9 us -> 11.2 us  [the longest x3 4.28 us: total_over(): lax.ppermute(value, both, partners(peers, lambda i, d=d: (i + d) % peers))]
    dynamic_slice x96 -> x0, local copies, waits for them, and re-layouts: 72 us -> none  [the longest x24 29.8 us: add_gradient(): weighting = 2.0 * kernel_weights[kernel] * slope_field]
    psum x2 -> x0, blocking collectives: 47.8 us -> none  [the longest x1 30.1 us: shards(): square_sum = lax.psum(grad_squares, ('strip', 'col', 'expo'))]
    another operation x216 -> x0, local copies, waits for them, and re-layouts: 43 us -> none  [the longest x192 42.5 us: toeplitz(): jnp.tile(padded_taps, (1,) * (tap_values.ndim - 1) + (block_len,))]
    squeeze x48 -> x0, local copies, waits for them, and re-layouts: 32.7 us -> none  [the longest x24 16.4 us: add_gradient(): row_pair = row_taps[kernel]]
    another operation x50 -> x0, other arithmetic: 24.5 us -> none
  transfers between devices with their start and end apart: 101 -> 9, of which waited for: 52 -> 6; matrix products, arithmetic and copies ran while one was open for 7% -> 0% of each run, Pallas kernels for 0% -> 2%
where the time goes in v3:
time: 42 us; the launch traced here: 41.7 us
  Pallas kernels  14.3 us (34%)
  starting transfers between devices  11.6 us (28%)
  waiting for transfers between devices  11.2 us (27%)
  local copies, waits for them, and re-layouts  3.87 us (9%)
  between operations  0.71 us (2%)
    pallas_call x1, Pallas kernels, shards(): call(forward_kernel, 'forward', [smem] + [vmem] * 4, (array((kernels, til...  6.36 us
    pallas_call x1, Pallas kernels, shards(): call(backward_kernel, 'backward', [smem] + [vmem] * 8, (full, full, array...  5.44 us
    ppermute x3, waiting for transfers between devices, total_over(): lax.ppermute(value, both, partners(peers, lambda i, d=d: (i + d) % peers))  4.28 us
    unnamed x10, local copies, waits for them, and re-layouts  3.87 us
    ppermute x1, starting transfers between devices, shards(): from_up = lax.ppermute(to_down, 'strip', ring('strip', 1))  3.1 us
    ppermute x3, starting transfers between devices, total_over(): lax.ppermute(value, both, partners(peers, lambda i, d=d: (i + d) % peers))  2.97 us
    ppermute x1, waiting for transfers between devices, shards(): before = after = lax.ppermute(messages[0], 'col', ring('col', 1))  2.7 us
    ppermute x1, starting transfers between devices, shards(): from_down = lax.ppermute(to_up, 'strip', ring('strip', -1))  2.09 us
  transfers between devices with their start and end apart: 9, of which 6 were waited for; matrix products, arithmetic and copies ran while one was open for 0% of the time, Pallas kernels for 2%

profile of v3, /device:TPU:0, one launch (start us, length us, event | category | flops | bytes accessed | tf_op | source)
XLA Modules:
  0.0 41.7 jit_solution(1899090760420076962)
XLA Ops:
  0.6 0.9 %copy-done = f32[1,256,128]{2,1,0:T(8,128)S(1)} copy-done((f32[1,256,128]{2,1,0:T(8,128)S(1)}, f32[1,256,128]{2,1,0:T(8,128)}, u32[]{:S(2)}) %copy-start) | copy-done | bytes 131096
  1.5 0.9 %copy-done.1 = s32[256,128]{1,0:T(8,128)S(1)} copy-done((s32[256,128]{1,0:T(8,128)S(1)}, s32[256,128]{1,0:T(8,128)}, u32[]{:S(2)}) %copy-start.1) | copy-done | bytes 131096
  2.4 0.4 prepare.1
  2.8 3.1 %collective-permute-start = (bf16[96,128]{1,0:T(8,128)(2,1)S(1)}, bf16[96,128]{1,0:T(8,128)(2,1)S(1)}, u32[]{:S(2)}, u32[]{:S(2)}) collective-permute-start(bf16[96,128]{1,0:T(8,128)(2,1)S(1)} %get-tuple-element.21), channel_id=1, source_target_pairs={{0,4},{4,8},{8,12},{12,0},{1,5},{5,9},{9,13},{13,1},{2,6},{6,10},{... | collective-permute-start | bytes 73736 | tf_op jit(solution)/shard_map/ppermute | solution.py:375
  5.9 2.1 %collective-permute-start.1 = (bf16[96,128]{1,0:T(8,128)(2,1)S(1)}, bf16[96,128]{1,0:T(8,128)(2,1)S(1)}, u32[]{:S(2)}, u32[]{:S(2)}) collective-permute-start(bf16[96,128]{1,0:T(8,128)(2,1)S(1)} %get-tuple-element.22), channel_id=1, source_target_pairs={{0,12},{4,0},{8,4},{12,8},{1,13},{5,1},{9,5},{13,9},{2,14},{6,2},{... | collective-permute-start | bytes 73736 | tf_op jit(solution)/shard_map/ppermute | solution.py:376
  8.1 0.7 %copy-done.2 = bf16[24,2,65]{2,1,0:T(2,128)(2,1)S(1)} copy-done((bf16[24,2,65]{2,1,0:T(2,128)(2,1)S(1)}, bf16[24,2,65]{2,1,0:T(2,128)(2,1)}, u32[]{:S(2)}) %copy-start.2) | copy-done | bytes 6264
  8.8 0.7 %copy-done.3 = bf16[24,2,65]{2,1,0:T(2,128)(2,1)S(1)} copy-done((bf16[24,2,65]{2,1,0:T(2,128)(2,1)S(1)}, bf16[24,2,65]{2,1,0:T(2,128)(2,1)}, u32[]{:S(2)}) %copy-start.3) | copy-done | bytes 6264
  9.5 0.7 %copy-done.4 = f32[24]{0:T(128)S(1)} copy-done((f32[24]{0:T(128)S(1)}, f32[24]{0:T(128)}, u32[]{:S(2)}) %copy-start.4) | copy-done | bytes 120
  10.1 0.8 %taps.1._.taps_ref = f32[24,8,256]{2,1,0:T(8,128)S(1)} custom-call(f32[24]{0:T(128)S(1)} %copy-done.4, bf16[24,2,65]{2,1,0:T(2,128)(2,1)S(1)} %copy-done.2, bf16[24,2,65]{2,1,0:T(2,128)(2,1)S(1)} %copy-done.3), custom_call_target="tpu_custom_call" | custom-call | flops 100000000 | bytes 1000000 | tf_op jit(solution)/shard_map/taps/pallas_call | solution.py:377
  10.9 0.7 %assemble.1 = (bf16[128,384]{1,0:T(8,128)(2,1)S(1)}, bf16[128,384]{1,0:T(8,128)(2,1)S(1)}, bf16[96,384]{1,0:T(8,128)(2,1)S(1)}) custom-call(s32[4]{0:T(128)S(1)} %add_convert_fusion.ends_ref, bf16[256,128]{1,0:T(8,128)(2,1)S(1)} %get-tuple-element.19.mask_ref, bf16[256,128]{1,0:T(8,128)(2,1)S(1)} %get-tuple-element.20.code_ref, ...), custom_call_target="tpu_custom_call" | custom-call | flops 1000000 | bytes 1000000 | tf_op jit(solution)/shard_map/assemble/pallas_call | solution.py:385
  11.6 1.7 %collective-permute-start.2 = (bf16[96,384]{1,0:T(8,128)(2,1)S(1)}, bf16[96,384]{1,0:T(8,128)(2,1)S(1)}, u32[]{:S(2)}, u32[]{:S(2)}) collective-permute-start(bf16[96,384]{1,0:T(8,128)(2,1)S(1)} %get-tuple-element.24), channel_id=1, source_target_pairs={{0,2},{2,0},{1,3},{3,1},{4,6},{6,4},{5,7},{7,5},{8,10},{10,8},{9,1... | collective-permute-start | bytes 221192 | tf_op jit(solution)/shard_map/ppermute | solution.py:392
  13.4 2.7 %collective-permute-done.2.before_ref.after_ref.code_before_ref.code_after_ref = bf16[96,384]{1,0:T(8,128)(2,1)S(1)} collective-permute-done((bf16[96,384]{1,0:T(8,128)(2,1)S(1)}, bf16[96,384]{1,0:T(8,128)(2,1)S(1)}, u32[]{:S(2)}, u32[]{:S(2)}) %collective-permute-start.2) | collective-permute-done | bytes 73760 | tf_op jit(solution)/shard_map/ppermute | solution.py:392
  16.1 6.4 %forward.1 = (bf16[24,3,192,256]{3,2,1,0:T(8,128)(2,1)S(1)}, f32[3,192,128]{2,1,0:T(8,128)S(1)}) custom-call(s32[4]{0:T(128)S(1)} %add_convert_fusion.ends_ref, bf16[128,384]{1,0:T(8,128)(2,1)S(1)} %get-tuple-element.23.centre_ref, bf16[96,384]{1,0:T(8,128)(2,1)S(1)} %collective-permute-done.2.before_ref.after_ref.code_before_ref.code_after_ref, ...), custom_call_target="tpu_custom_call" | custom-call | flops 1000000 | bytes 1000000 | tf_op jit(solution)/shard_map/forward/pallas_call | solution.py:399
  22.5 1.6 %collective-permute-done.3.other_ref = f32[3,192,128]{2,1,0:T(8,128)S(1)} collective-permute-done((f32[3,192,128]{2,1,0:T(8,128)S(1)}, f32[3,192,128]{2,1,0:T(8,128)S(1)}, u32[]{:S(2)}, u32[]{:S(2)}) %collective-permute-start.3) | collective-permute-done | bytes 294944 | tf_op jit(solution)/shard_map/ppermute | solution.py:414
  24.1 5.4 %backward.1 = (f32[256,128]{1,0:T(8,128)S(1)}, f32[256,128]{1,0:T(8,128)}, f32[2,128]{1,0:T(2,128)S(1)}) custom-call(s32[4]{0:T(128)S(1)} %add_convert_fusion.ends_ref, f32[3,192,128]{2,1,0:T(8,128)S(1)} %get-tuple-element.25.own_ref, f32[3,192,128]{2,1,0:T(8,128)S(1)} %collective-permute-done.3.other_ref, bf16[128,384]{1,0:T(8,128)(2,1)S(1)} %get-tuple-element.26.code_ref, ...), custom_call_target="tpu_custom_call" | custom-call | flops 1000000 | bytes 1000000 | tf_op jit(solution)/shard_map/backward/pallas_call | solution.py:416
  29.5 0.2 collective-permute-start.4
  29.7 1.0 %collective-permute-done.4 = f32[2,128]{1,0:T(2,128)S(1)} collective-permute-done((f32[2,128]{1,0:T(2,128)S(1)}, f32[2,128]{1,0:T(2,128)S(1)}, u32[]{:S(2)}, u32[]{:S(2)}) %collective-permute-start.4) | collective-permute-done | bytes 1056 | tf_op jit(solution)/shard_map/ppermute | solution.py:434
  30.7 1.4 %collective-permute-start.5 = (f32[2,128]{1,0:T(2,128)S(1)}, f32[2,128]{1,0:T(2,128)S(1)}, u32[]{:S(2)}, u32[]{:S(2)}) collective-permute-start(f32[2,128]{1,0:T(2,128)S(1)} %add.15), channel_id=1, source_target_pairs={{0,3},{1,2},{2,1},{3,0},{4,7},{5,6},{6,5},{7,4},{8,11},{9,10},{10,... | collective-permute-start | bytes 3080 | tf_op jit(solution)/shard_map/ppermute | solution.py:46
  32.2 1.6 %collective-permute-done.5 = f32[2,128]{1,0:T(2,128)S(1)} collective-permute-done((f32[2,128]{1,0:T(2,128)S(1)}, f32[2,128]{1,0:T(2,128)S(1)}, u32[]{:S(2)}, u32[]{:S(2)}) %collective-permute-start.5) | collective-permute-done | bytes 1056 | tf_op jit(solution)/shard_map/ppermute | solution.py:46
  33.8 2.5 %collective-permute-start.8 = (f32[2,128]{1,0:T(2,128)S(1)}, f32[2,128]{1,0:T(2,128)S(1)}, u32[]{:S(2)}, u32[]{:S(2)}) collective-permute-start(f32[2,128]{1,0:T(2,128)S(1)} %add.16), channel_id=1, source_target_pairs={{0,13},{1,12},{4,1},{5,0},{8,5},{9,4},{12,9},{13,8},{2,15},{3,14},... | collective-permute-start | bytes 3080 | tf_op jit(solution)/shard_map/ppermute | solution.py:41
  36.2 0.5 %collective-permute-start.6 = (f32[2,128]{1,0:T(2,128)S(1)}, f32[2,128]{1,0:T(2,128)S(1)}, u32[]{:S(2)}, u32[]{:S(2)}) collective-permute-start(f32[2,128]{1,0:T(2,128)S(1)} %add.16), channel_id=1, source_target_pairs={{0,9},{1,8},{4,13},{5,12},{8,1},{9,0},{12,5},{13,4},{2,11},{3,10},... | collective-permute-start | bytes 3080 | tf_op jit(solution)/shard_map/ppermute | solution.py:41
  36.7 0.8 %collective-permute-done.8 = f32[2,128]{1,0:T(2,128)S(1)} collective-permute-done((f32[2,128]{1,0:T(2,128)S(1)}, f32[2,128]{1,0:T(2,128)S(1)}, u32[]{:S(2)}, u32[]{:S(2)}) %collective-permute-start.8) | collective-permute-done | bytes 1056 | tf_op jit(solution)/shard_map/ppermute | solution.py:41
  37.5 3.5 %collective-permute-done.7 = f32[2,128]{1,0:T(2,128)S(1)} collective-permute-done((f32[2,128]{1,0:T(2,128)S(1)}, f32[2,128]{1,0:T(2,128)S(1)}, u32[]{:S(2)}, u32[]{:S(2)}) %collective-permute-start.7) | collective-permute-done | bytes 1056 | tf_op jit(solution)/shard_map/ppermute | solution.py:41
  41.0 0.7 %finish.1 = (f32[256,128]{1,0:T(8,128)}, f32[1,128]{1,0:T(1,128)}) custom-call(f32[256,128]{1,0:T(8,128)S(1)} %get-tuple-element.18.params_ref, f32[256,128]{1,0:T(8,128)S(1)} %get-tuple-element.28.gradient_ref, f32[2,128]{1,0:T(2,128)S(1)} %add_add_fusion.sums_ref), custom_call_target="tpu_custom_call" | custom-call | flops 1000000 | bytes 1000000 | tf_op jit(solution)/shard_map/finish/pallas_call | solution.py:438
  (14 shorter events, 0.2 us)
Async XLA Ops:
  0.6 0.9 %copy-start = (f32[1,256,128]{2,1,0:T(8,128)S(1)}, f32[1,256,128]{2,1,0:T(8,128)}, u32[]{:S(2)}) copy-start(f32[1,256,128]{2,1,0:T(8,128)} %param.5) | copy-start | bytes 393220
  1.5 0.9 %copy-start.1 = (s32[256,128]{1,0:T(8,128)S(1)}, s32[256,128]{1,0:T(8,128)}, u32[]{:S(2)}) copy-start(s32[256,128]{1,0:T(8,128)} %target_hbm.1) | copy-start | bytes 393220
  2.8 8.1 %collective-permute-start = (bf16[96,128]{1,0:T(8,128)(2,1)S(1)}, bf16[96,128]{1,0:T(8,128)(2,1)S(1)}, u32[]{:S(2)}, u32[]{:S(2)}) collective-permute-start(bf16[96,128]{1,0:T(8,128)(2,1)S(1)} %get-tuple-element.21), channel_id=1, source_target_pairs={{0,4},{4,8},{8,12},{12,0},{1,5},{5,9},{9,13},{13,1},{2,6},{6,10},{... | collective-permute-start | bytes 73736 | tf_op jit(solution)/shard_map/ppermute | solution.py:375
  5.9 5.0 %collective-permute-start.1 = (bf16[96,128]{1,0:T(8,128)(2,1)S(1)}, bf16[96,128]{1,0:T(8,128)(2,1)S(1)}, u32[]{:S(2)}, u32[]{:S(2)}) collective-permute-start(bf16[96,128]{1,0:T(8,128)(2,1)S(1)} %get-tuple-element.22), channel_id=1, source_target_pairs={{0,12},{4,0},{8,4},{12,8},{1,13},{5,1},{9,5},{13,9},{2,14},{6,2},{... | collective-permute-start | bytes 73736 | tf_op jit(solution)/shard_map/ppermute | solution.py:376
  8.1 0.7 %copy-start.2 = (bf16[24,2,65]{2,1,0:T(2,128)(2,1)S(1)}, bf16[24,2,65]{2,1,0:T(2,128)(2,1)}, u32[]{:S(2)}) copy-start(bf16[24,2,65]{2,1,0:T(2,128)(2,1)} %col_ref.1) | copy-start | bytes 18724
  8.8 0.7 %copy-start.3 = (bf16[24,2,65]{2,1,0:T(2,128)(2,1)S(1)}, bf16[24,2,65]{2,1,0:T(2,128)(2,1)}, u32[]{:S(2)}) copy-start(bf16[24,2,65]{2,1,0:T(2,128)(2,1)} %row_ref.1) | copy-start | bytes 18724
  9.5 0.7 %copy-start.4 = (f32[24]{0:T(128)S(1)}, f32[24]{0:T(128)}, u32[]{:S(2)}) copy-start(f32[24]{0:T(128)} %weights_ref.1) | copy-start | bytes 292
  11.6 4.4 %collective-permute-start.2 = (bf16[96,384]{1,0:T(8,128)(2,1)S(1)}, bf16[96,384]{1,0:T(8,128)(2,1)S(1)}, u32[]{:S(2)}, u32[]{:S(2)}) collective-permute-start(bf16[96,384]{1,0:T(8,128)(2,1)S(1)} %get-tuple-element.24), channel_id=1, source_target_pairs={{0,2},{2,0},{1,3},{3,1},{4,6},{6,4},{5,7},{7,5},{8,10},{10,8},{9,1... | collective-permute-start | bytes 221192 | tf_op jit(solution)/shard_map/ppermute | solution.py:392
  22.4 1.6 %collective-permute-start.3 = (f32[3,192,128]{2,1,0:T(8,128)S(1)}, f32[3,192,128]{2,1,0:T(8,128)S(1)}, u32[]{:S(2)}, u32[]{:S(2)}) collective-permute-start(f32[3,192,128]{2,1,0:T(8,128)S(1)} %get-tuple-element.25.own_ref), channel_id=1, source_target_pairs={{0,1},{1,0},{2,3},{3,2},{4,5},{5,4},{6,7},{7,6},{8,9},{9,8},{10,11... | collective-permute-start | bytes 884744 | tf_op jit(solution)/shard_map/ppermute | solution.py:414
  29.5 1.2 %collective-permute-start.4 = (f32[2,128]{1,0:T(2,128)S(1)}, f32[2,128]{1,0:T(2,128)S(1)}, u32[]{:S(2)}, u32[]{:S(2)}) collective-permute-start(f32[2,128]{1,0:T(2,128)S(1)} %get-tuple-element.29), channel_id=1, source_target_pairs={{0,1},{1,0},{2,3},{3,2},{4,5},{5,4},{6,7},{7,6},{8,9},{9,8},{10,11... | collective-permute-start | bytes 3080 | tf_op jit(solution)/shard_map/ppermute | solution.py:434
  30.7 3.0 %collective-permute-start.5 = (f32[2,128]{1,0:T(2,128)S(1)}, f32[2,128]{1,0:T(2,128)S(1)}, u32[]{:S(2)}, u32[]{:S(2)}) collective-permute-start(f32[2,128]{1,0:T(2,128)S(1)} %add.15), channel_id=1, source_target_pairs={{0,3},{1,2},{2,1},{3,0},{4,7},{5,6},{6,5},{7,4},{8,11},{9,10},{10,... | collective-permute-start | bytes 3080 | tf_op jit(solution)/shard_map/ppermute | solution.py:46
  33.8 3.8 %collective-permute-start.8 = (f32[2,128]{1,0:T(2,128)S(1)}, f32[2,128]{1,0:T(2,128)S(1)}, u32[]{:S(2)}, u32[]{:S(2)}) collective-permute-start(f32[2,128]{1,0:T(2,128)S(1)} %add.16), channel_id=1, source_target_pairs={{0,13},{1,12},{4,1},{5,0},{8,5},{9,4},{12,9},{13,8},{2,15},{3,14},... | collective-permute-start | bytes 3080 | tf_op jit(solution)/shard_map/ppermute | solution.py:41
  36.2 4.8 %collective-permute-start.7 = (f32[2,128]{1,0:T(2,128)S(1)}, f32[2,128]{1,0:T(2,128)S(1)}, u32[]{:S(2)}, u32[]{:S(2)}) collective-permute-start(f32[2,128]{1,0:T(2,128)S(1)} %add.16), channel_id=1, source_target_pairs={{0,5},{1,4},{4,9},{5,8},{8,13},{9,12},{12,1},{13,0},{2,7},{3,6},{6... | collective-permute-start | bytes 3080 | tf_op jit(solution)/shard_map/ppermute | solution.py:41
  36.2 4.8 %collective-permute-start.6 = (f32[2,128]{1,0:T(2,128)S(1)}, f32[2,128]{1,0:T(2,128)S(1)}, u32[]{:S(2)}, u32[]{:S(2)}) collective-permute-start(f32[2,128]{1,0:T(2,128)S(1)} %add.16), channel_id=1, source_target_pairs={{0,9},{1,8},{4,13},{5,12},{8,1},{9,0},{12,5},{13,4},{2,11},{3,10},... | collective-permute-start | bytes 3080 | tf_op jit(solution)/shard_map/ppermute | solution.py:41

commit v4 on v3

--- a/solution.py
+++ b/solution.py
@@ -8,9 +8,10 @@
 
 HALF = 32
 LANES = 128
-FORWARD_UNROLL = 8
-BACKWARD_UNROLL = 8
-VMEM = 16 * 2**20
+FORWARD_UNROLL = 24
+BACKWARD_UNROLL = 12
+CHUNK = 4
+VMEM = 24 * 2**20
 
 mask_slope = 4.0
 resist_steep = 4.0
@@ -22,9 +23,22 @@
 F32 = jnp.float32
 
 
+def stay(array):
+    return pltpu.with_memory_space_constraint(array, pltpu.HBM)
+
+
 def ring(axis, step):
     peers = lax.axis_size(axis)
     return [(i, (i + step) % peers) for i in range(peers)]
+
+
+def snake(step):
+    tiles, strips = lax.axis_size("tiles"), lax.axis_size("strip")
+    order = []
+    for tile in range(tiles):
+        levels = range(strips) if tile % 2 == 0 else reversed(range(strips))
+        order += [tile * strips + level for level in levels]
+    return [(device, order[(i + step) % len(order)]) for i, device in enumerate(order)]
 
 
 def partners(peers, other):
@@ -38,7 +52,7 @@
     both = (axis, "expo")
     if peers == 4:
         one, two, three = (
-            lax.ppermute(value, both, partners(peers, lambda i, d=d: (i + d) % peers)) for d in (1, 2, 3)
+            lax.ppermute(value, both, partners(peers, lambda i, d=d: i ^ d)) for d in (1, 2, 3)
         )
         return (value + two) + (one + three)
     reach = 1
@@ -64,18 +78,31 @@
         masks_ref[slot] = jnp.where(keep, one, zero).astype(BF16)
 
 
-def taps_kernel(weights_ref, col_ref, row_ref, out_ref):
+def taps_kernel(weights_hbm, col_hbm, row_hbm, out_ref, weights_ref, col_ref, row_ref, flat_ref, sems):
     kernels, _, taps = col_ref.shape
+    copies = [
+        pltpu.make_async_copy(source, target, sems.at[slot])
+        for slot, (source, target) in enumerate(
+            ((weights_hbm, weights_ref), (col_hbm, col_ref), (row_hbm, row_ref))
+        )
+    ]
+    for copy in copies:
+        copy.start()
     t, l = index_pair((taps, 2 * LANES))
     pick = jnp.where((l == t) | (l == LANES + taps - 1 - t), 1.0, 0.0).astype(BF16)
+    for copy in copies:
+        copy.wait()
     for k in range(kernels):
-        both = jnp.concatenate([col_ref[k].astype(F32), row_ref[k].astype(F32)], axis=0).astype(BF16)
-        out_ref[k, 0:4] = jnp.dot(both, pick, preferred_element_type=F32)
+        flat_ref[4 * k : 4 * k + 2] = col_ref[k].astype(F32)
+        flat_ref[4 * k + 2 : 4 * k + 4] = row_ref[k].astype(F32)
+    rows = jnp.dot(flat_ref[...].astype(BF16), pick, preferred_element_type=F32)
+    for k in range(kernels):
+        out_ref[k, 0:4] = rows[4 * k : 4 * k + 4]
         out_ref[k, 4:8] = jnp.full((4, 2 * LANES), weights_ref[k], F32)
 
 
 def prepare_kernel(
-    params_hbm, target_hbm, params_ref, mask_ref, code_ref, down_ref, up_ref, target_ref, sems
+    ends_ref, params_hbm, target_hbm, params_ref, mask_ref, code_ref, ahead_ref, behind_ref, target_ref, sems
 ):
     rows = params_ref.shape[0]
     wide = 2 * HALF
@@ -91,10 +118,15 @@
     code = (target_ref[...] + 1).astype(F32).astype(BF16)
     mask_ref[...] = mask
     code_ref[...] = code
-    down_ref[0:wide, :] = mask[rows - wide :]
-    down_ref[wide:, :] = code[rows - HALF :]
-    up_ref[0:wide, :] = mask[0:wide]
-    up_ref[wide:, :] = code[0:HALF]
+
+    def edges(down_ref, up_ref):
+        down_ref[0:wide, :] = mask[rows - wide :]
+        down_ref[wide:, :] = code[rows - HALF :]
+        up_ref[0:wide, :] = mask[0:wide]
+        up_ref[wide:, :] = code[0:HALF]
+
+    pl.when(ends_ref[4] == 0)(lambda: edges(ahead_ref, behind_ref))
+    pl.when(ends_ref[4] == 1)(lambda: edges(behind_ref, ahead_ref))
 
 
 def unless(end, values):
@@ -102,11 +134,14 @@
 
 
 def assemble_kernel(
-    ends_ref, mask_ref, code_ref, up_ref, down_ref, _, centre_ref, code_out_ref, *side_refs
+    ends_ref, mask_ref, code_ref, behind_ref, ahead_ref, _, centre_ref, code_out_ref, *side_refs
 ):
     rows, cols = mask_ref.shape
     wide = 2 * HALF
-    above, below = unless(ends_ref[2], up_ref[...]), unless(ends_ref[3], down_ref[...])
+    turn = ends_ref[4] == 1
+    behind, ahead = behind_ref[...].astype(F32), ahead_ref[...].astype(F32)
+    above = unless(ends_ref[2], jnp.where(turn, ahead, behind))
+    below = unless(ends_ref[3], jnp.where(turn, behind, ahead))
     tall = jnp.concatenate([above[0:wide], mask_ref[...].astype(F32), below[0:wide]], axis=0)
     turned = tall.T.astype(BF16)
     code = jnp.concatenate(
@@ -318,7 +353,11 @@
                 turned.append(pltpu.roll(spread, part * wide, 1, stride=1, stride_axis=0))
             both = jnp.where(b < wide, turned[0], turned[1])
             table_ref[:, at + 2 * LANES : at + 3 * LANES] = jnp.where(inside, both, 0.0).astype(BF16)
-        descent_ref[...] += jnp.dot(table_ref[...], source_ref[...], preferred_element_type=F32)
+            if unit % CHUNK == CHUNK - 1:
+                chunk = slice((unit + 1 - CHUNK) * 2 * span, (unit + 1) * 2 * span)
+                descent_ref[...] += jnp.dot(
+                    table_ref[:, chunk], source_ref[chunk, :], preferred_element_type=F32
+                )
         return carry
 
     lax.fori_loop(0, kernels // units, group, 0)
@@ -365,29 +404,40 @@
 
     plain, edge = array((rows, cols), BF16), array((wide + HALF, cols), BF16)
     full = array((rows, cols), F32)
-    params, mask_half, code, to_down, to_up = call(
+    sides, strips = lax.axis_size("col"), lax.axis_size("strip")
+    place, level, turn = lax.axis_index("col"), lax.axis_index("strip"), lax.axis_index("tiles") % 2
+    ends = jnp.stack([place == 0, place == sides - 1, level == 0, level == strips - 1, turn == 1]).astype(jnp.int32)
+    params, mask_half, code, ahead, behind = call(
         prepare_kernel,
         "prepare",
-        [hbm, hbm],
+        [smem, hbm, hbm],
         (full, plain, plain, edge, edge),
         scratch=[pltpu.VMEM((rows, cols), target.dtype), pltpu.SemaphoreType.DMA((2,))],
-    )(mask_params[0], target)
-    from_up = lax.ppermute(to_down, "strip", ring("strip", 1))
-    from_down = lax.ppermute(to_up, "strip", ring("strip", -1))
+    )(ends, stay(mask_params[0]), stay(target))
+    from_behind = lax.ppermute(ahead, ("tiles", "strip"), snake(1))
+    from_ahead = lax.ppermute(behind, ("tiles", "strip"), snake(-1))
     (tap_rows,) = call(
-        taps_kernel, "taps", [smem, vmem, vmem], (array((kernels, 8, 2 * LANES), F32),), flops=10**8
-    )(kernel_weights, col_taps, row_taps)
-
-    sides, strips = lax.axis_size("col"), lax.axis_size("strip")
-    place, level = lax.axis_index("col"), lax.axis_index("strip")
-    ends = jnp.stack([place == 0, place == sides - 1, level == 0, level == strips - 1]).astype(jnp.int32)
+        taps_kernel,
+        "taps",
+        [hbm] * 3,
+        (array((kernels, 8, 2 * LANES), F32),),
+        scratch=[
+            pltpu.SMEM(kernel_weights.shape, F32),
+            pltpu.VMEM(col_taps.shape, BF16),
+            pltpu.VMEM(row_taps.shape, BF16),
+            pltpu.VMEM((4 * kernels, taps), F32),
+            pltpu.SemaphoreType.DMA((3,)),
+        ],
+        flops=10**8,
+    )(stay(kernel_weights), stay(col_taps), stay(row_taps))
+
     side, turned = array((wide + HALF, long), BF16), array((cols, long), BF16)
     centre, code_turned, *messages = call(
         assemble_kernel,
         "assemble",
         [smem, vmem, vmem, vmem, vmem, pl.BlockSpec(memory_space=pl.ANY)],
         (turned, turned) + (side,) * (1 if sides == 2 else 2),
-    )(ends, mask_half, code, from_up, from_down, tap_rows)
+    )(ends, mask_half, code, from_behind, from_ahead, tap_rows)
     if sides == 2:
         before = after = lax.ppermute(messages[0], "col", ring("col", 1))
     else:

time: 42 us -> 39.3 us (0.936)
  local copies, waits for them, and re-layouts: 3.87 us -> 0.1 us
  waiting for transfers between devices: 11.2 us -> 13.4 us
  starting transfers between devices: 11.6 us -> 10.1 us
  Pallas kernels: 14.3 us -> 14.8 us
    unnamed x10 -> x0, local copies, waits for them, and re-layouts: 3.87 us -> none
    ppermute x5, waiting for transfers between devices: 4.29 us -> 6.24 us  [the longest x3 3.34 us: total_over(): lax.ppermute(value, both, partners(peers, lambda i, d=d: i ^ d))]
    pallas_call x2, Pallas kernels: 1.12 us -> 2.46 us  [the longest x1 1.56 us: shards(): call(prepare_kernel, 'prepare', [smem, hbm, hbm], (full, plain, plain, ed...]
    ppermute x5, starting transfers between devices: 8.16 us -> 6.99 us  [the longest x3 3.88 us: total_over(): lax.ppermute(value, both, partners(peers, lambda i, d=d: i ^ d))]
    pallas_call x1, Pallas kernels: 6.36 us -> 5.87 us  [shards(): call(forward_kernel, 'forward', [smem] + [vmem] * 4, (array((kernels, til...]
  transfers between devices with their start and end apart: 9 -> 9, of which waited for: 6 -> 9; matrix products, arithmetic and copies ran while one was open for 0% -> 0% of each run, Pallas kernels for 2% -> 2%
where the time goes in v4:
time: 39.3 us; the launch traced here: 39.1 us
  Pallas kernels  14.8 us (38%)
  waiting for transfers between devices  13.4 us (34%)
  starting transfers between devices  10.1 us (26%)
  between operations  0.71 us (2%)
    pallas_call x1, Pallas kernels, shards(): call(forward_kernel, 'forward', [smem] + [vmem] * 4, (array((kernels, til...  5.87 us
    pallas_call x1, Pallas kernels, shards(): call(backward_kernel, 'backward', [smem] + [vmem] * 8, (full, full, array...  5.09 us
    ppermute x3, starting transfers between devices, total_over(): lax.ppermute(value, both, partners(peers, lambda i, d=d: i ^ d))  3.88 us
    ppermute x3, waiting for transfers between devices, total_over(): lax.ppermute(value, both, partners(peers, lambda i, d=d: i ^ d))  3.34 us
    ppermute x1, starting transfers between devices, shards(): from_behind = lax.ppermute(ahead, ('tiles', 'strip'), snake(1))  3.1 us
    ppermute x1, waiting for transfers between devices, shards(): before = after = lax.ppermute(messages[0], 'col', ring('col', 1))  2.86 us
    ppermute x1, waiting for transfers between devices, shards(): from_ahead = lax.ppermute(behind, ('tiles', 'strip'), snake(-1))  2.08 us
    ppermute x1, waiting for transfers between devices, total_over(): lax.ppermute(value, both, partners(peers, lambda i, r=reach: i ^ r))  1.73 us
  transfers between devices with their start and end apart: 9, of which 9 were waited for; matrix products, arithmetic and copies ran while one was open for 0% of the time, Pallas kernels for 2%

profile of v4, /device:TPU:0, one launch (start us, length us, event | category | flops | bytes accessed | tf_op | source)
XLA Modules:
  0.0 39.1 jit_solution(8709123195355594840)
XLA Ops:
  0.6 0.1 stack.23
  0.8 1.6 %prepare.1 = (f32[256,128]{1,0:T(8,128)S(1)}, bf16[256,128]{1,0:T(8,128)(2,1)S(1)}, bf16[256,128]{1,0:T(8,128)(2,1)S(1)}, bf16[96,128]{1,0:T(8,128)(2,1)S(1)}, bf16[96,128]{1,0:T(8,128)(2,1)S(1)}) custom-call(s32[5]{0:T(128)S(1)} %convert_element_type.3.ends_ref, f32[256,128]{1,0:T(8,128)} %bitcast.9, s32[256,128]{1,0:T(8,128)} %target_hbm.1), custom_call_target="tpu_custom_call" | custom-call | flops 1000000 | bytes 1000000 | tf_op jit(solution)/shard_map/prepare/pallas_call | solution.py:410
  2.3 3.1 %collective-permute-start = (bf16[96,128]{1,0:T(8,128)(2,1)S(1)}, bf16[96,128]{1,0:T(8,128)(2,1)S(1)}, u32[]{:S(2)}, u32[]{:S(2)}) collective-permute-start(bf16[96,128]{1,0:T(8,128)(2,1)S(1)} %get-tuple-element.21), channel_id=1, source_target_pairs={{0,4},{4,8},{8,12},{12,28},{28,24},{24,20},{20,16},{16,0},{1,5},{5... | collective-permute-start | bytes 73736 | tf_op jit(solution)/shard_map/ppermute | solution.py:417
  5.4 0.0 collective-permute-start.1
  5.4 0.9 %taps.1._.taps_ref = f32[24,8,256]{2,1,0:T(8,128)S(1)} custom-call(f32[24]{0:T(128)} %weights_hbm.1, bf16[24,2,65]{2,1,0:T(2,128)(2,1)} %col_hbm.1, bf16[24,2,65]{2,1,0:T(2,128)(2,1)} %row_hbm.1), custom_call_target="tpu_custom_call" | custom-call | flops 100000000 | bytes 1000000 | tf_op jit(solution)/shard_map/taps/pallas_call | solution.py:419
  6.4 0.8 %collective-permute-done.behind_ref = bf16[96,128]{1,0:T(8,128)(2,1)S(1)} collective-permute-done((bf16[96,128]{1,0:T(8,128)(2,1)S(1)}, bf16[96,128]{1,0:T(8,128)(2,1)S(1)}, u32[]{:S(2)}, u32[]{:S(2)}) %collective-permute-start) | collective-permute-done | bytes 24608 | tf_op jit(solution)/shard_map/ppermute | solution.py:417
  7.2 2.1 %collective-permute-done.1.ahead_ref = bf16[96,128]{1,0:T(8,128)(2,1)S(1)} collective-permute-done((bf16[96,128]{1,0:T(8,128)(2,1)S(1)}, bf16[96,128]{1,0:T(8,128)(2,1)S(1)}, u32[]{:S(2)}, u32[]{:S(2)}) %collective-permute-start.1) | collective-permute-done | bytes 24608 | tf_op jit(solution)/shard_map/ppermute | solution.py:418
  9.3 0.7 %assemble.1 = (bf16[128,384]{1,0:T(8,128)(2,1)S(1)}, bf16[128,384]{1,0:T(8,128)(2,1)S(1)}, bf16[96,384]{1,0:T(8,128)(2,1)S(1)}) custom-call(s32[5]{0:T(128)S(1)} %convert_element_type.3.ends_ref, bf16[256,128]{1,0:T(8,128)(2,1)S(1)} %get-tuple-element.19.mask_ref, bf16[256,128]{1,0:T(8,128)(2,1)S(1)} %get-tuple-element.20.code_ref, ...), custom_call_target="tpu_custom_call" | custom-call | flops 1000000 | bytes 1000000 | tf_op jit(solution)/shard_map/assemble/pallas_call | solution.py:435
  10.0 1.6 %collective-permute-start.2 = (bf16[96,384]{1,0:T(8,128)(2,1)S(1)}, bf16[96,384]{1,0:T(8,128)(2,1)S(1)}, u32[]{:S(2)}, u32[]{:S(2)}) collective-permute-start(bf16[96,384]{1,0:T(8,128)(2,1)S(1)} %get-tuple-element.24), channel_id=1, source_target_pairs={{0,2},{2,0},{1,3},{3,1},{4,6},{6,4},{5,7},{7,5},{8,10},{10,8},{9,1... | collective-permute-start | bytes 221192 | tf_op jit(solution)/shard_map/ppermute | solution.py:442
  11.5 2.9 %collective-permute-done.2.before_ref.after_ref.code_before_ref.code_after_ref = bf16[96,384]{1,0:T(8,128)(2,1)S(1)} collective-permute-done((bf16[96,384]{1,0:T(8,128)(2,1)S(1)}, bf16[96,384]{1,0:T(8,128)(2,1)S(1)}, u32[]{:S(2)}, u32[]{:S(2)}) %collective-permute-start.2) | collective-permute-done | bytes 73760 | tf_op jit(solution)/shard_map/ppermute | solution.py:442
  14.4 5.9 %forward.1 = (bf16[24,3,192,256]{3,2,1,0:T(8,128)(2,1)S(1)}, f32[3,192,128]{2,1,0:T(8,128)S(1)}) custom-call(s32[5]{0:T(128)S(1)} %convert_element_type.3.ends_ref, bf16[128,384]{1,0:T(8,128)(2,1)S(1)} %get-tuple-element.23.centre_ref, bf16[96,384]{1,0:T(8,128)(2,1)S(1)} %collective-permute-done.2.before_ref.after_ref.code_before_ref.code_after_ref, ...), custom_call_target="tpu_custom_call" | custom-call | flops 1000000 | bytes 1000000 | tf_op jit(solution)/shard_map/forward/pallas_call | solution.py:449
  20.2 0.1 collective-permute-start.3
  20.3 1.6 %collective-permute-done.3.other_ref = f32[3,192,128]{2,1,0:T(8,128)S(1)} collective-permute-done((f32[3,192,128]{2,1,0:T(8,128)S(1)}, f32[3,192,128]{2,1,0:T(8,128)S(1)}, u32[]{:S(2)}, u32[]{:S(2)}) %collective-permute-start.3) | collective-permute-done | bytes 294944 | tf_op jit(solution)/shard_map/ppermute | solution.py:464
  21.9 5.1 %backward.1 = (f32[256,128]{1,0:T(8,128)S(1)}, f32[256,128]{1,0:T(8,128)}, f32[2,128]{1,0:T(2,128)S(1)}) custom-call(s32[5]{0:T(128)S(1)} %convert_element_type.3.ends_ref, f32[3,192,128]{2,1,0:T(8,128)S(1)} %get-tuple-element.25.own_ref, f32[3,192,128]{2,1,0:T(8,128)S(1)} %collective-permute-done.3.other_ref, ...), custom_call_target="tpu_custom_call" | custom-call | flops 1000000 | bytes 1000000 | tf_op jit(solution)/shard_map/backward/pallas_call | solution.py:466
  27.0 0.2 collective-permute-start.4
  27.2 1.0 %collective-permute-done.4 = f32[2,128]{1,0:T(2,128)S(1)} collective-permute-done((f32[2,128]{1,0:T(2,128)S(1)}, f32[2,128]{1,0:T(2,128)S(1)}, u32[]{:S(2)}, u32[]{:S(2)}) %collective-permute-start.4) | collective-permute-done | bytes 1056 | tf_op jit(solution)/shard_map/ppermute | solution.py:484
  28.2 1.3 %collective-permute-start.5 = (f32[2,128]{1,0:T(2,128)S(1)}, f32[2,128]{1,0:T(2,128)S(1)}, u32[]{:S(2)}, u32[]{:S(2)}) collective-permute-start(f32[2,128]{1,0:T(2,128)S(1)} %add.20), channel_id=1, source_target_pairs={{0,3},{1,2},{2,1},{3,0},{4,7},{5,6},{6,5},{7,4},{8,11},{9,10},{10,... | collective-permute-start | bytes 3080 | tf_op jit(solution)/shard_map/ppermute | solution.py:60
  29.5 1.7 %collective-permute-done.5 = f32[2,128]{1,0:T(2,128)S(1)} collective-permute-done((f32[2,128]{1,0:T(2,128)S(1)}, f32[2,128]{1,0:T(2,128)S(1)}, u32[]{:S(2)}, u32[]{:S(2)}) %collective-permute-start.5) | collective-permute-done | bytes 1056 | tf_op jit(solution)/shard_map/ppermute | solution.py:60
  31.2 3.3 %collective-permute-start.8 = (f32[2,128]{1,0:T(2,128)S(1)}, f32[2,128]{1,0:T(2,128)S(1)}, u32[]{:S(2)}, u32[]{:S(2)}) collective-permute-start(f32[2,128]{1,0:T(2,128)S(1)} %add.21), channel_id=1, source_target_pairs={{0,13},{1,12},{4,9},{5,8},{8,5},{9,4},{12,1},{13,0},{2,15},{3,14},... | collective-permute-start | bytes 3080 | tf_op jit(solution)/shard_map/ppermute | solution.py:55
  34.5 0.6 %collective-permute-start.6 = (f32[2,128]{1,0:T(2,128)S(1)}, f32[2,128]{1,0:T(2,128)S(1)}, u32[]{:S(2)}, u32[]{:S(2)}) collective-permute-start(f32[2,128]{1,0:T(2,128)S(1)} %add.21), channel_id=1, source_target_pairs={{0,9},{1,8},{4,13},{5,12},{8,1},{9,0},{12,5},{13,4},{2,11},{3,10},... | collective-permute-start | bytes 3080 | tf_op jit(solution)/shard_map/ppermute | solution.py:55
  35.1 0.9 %collective-permute-done.8 = f32[2,128]{1,0:T(2,128)S(1)} collective-permute-done((f32[2,128]{1,0:T(2,128)S(1)}, f32[2,128]{1,0:T(2,128)S(1)}, u32[]{:S(2)}, u32[]{:S(2)}) %collective-permute-start.8) | collective-permute-done | bytes 1056 | tf_op jit(solution)/shard_map/ppermute | solution.py:55
  36.0 1.5 %collective-permute-done.7 = f32[2,128]{1,0:T(2,128)S(1)} collective-permute-done((f32[2,128]{1,0:T(2,128)S(1)}, f32[2,128]{1,0:T(2,128)S(1)}, u32[]{:S(2)}, u32[]{:S(2)}) %collective-permute-start.7) | collective-permute-done | bytes 1056 | tf_op jit(solution)/shard_map/ppermute | solution.py:55
  37.5 0.9 %collective-permute-done.6 = f32[2,128]{1,0:T(2,128)S(1)} collective-permute-done((f32[2,128]{1,0:T(2,128)S(1)}, f32[2,128]{1,0:T(2,128)S(1)}, u32[]{:S(2)}, u32[]{:S(2)}) %collective-permute-start.6) | collective-permute-done | bytes 1056 | tf_op jit(solution)/shard_map/ppermute | solution.py:55
  38.5 0.7 %finish.1 = (f32[256,128]{1,0:T(8,128)}, f32[1,128]{1,0:T(1,128)}) custom-call(f32[256,128]{1,0:T(8,128)S(1)} %get-tuple-element.18.params_ref, f32[256,128]{1,0:T(8,128)S(1)} %get-tuple-element.28.gradient_ref, f32[2,128]{1,0:T(2,128)S(1)} %add_add_fusion.sums_ref), custom_call_target="tpu_custom_call" | custom-call | flops 1000000 | bytes 1000000 | tf_op jit(solution)/shard_map/finish/pallas_call | solution.py:488
  (5 shorter events, 0.0 us)
Async XLA Ops:
  2.3 4.9 %collective-permute-start = (bf16[96,128]{1,0:T(8,128)(2,1)S(1)}, bf16[96,128]{1,0:T(8,128)(2,1)S(1)}, u32[]{:S(2)}, u32[]{:S(2)}) collective-permute-start(bf16[96,128]{1,0:T(8,128)(2,1)S(1)} %get-tuple-element.21), channel_id=1, source_target_pairs={{0,4},{4,8},{8,12},{12,28},{28,24},{24,20},{20,16},{16,0},{1,5},{5... | collective-permute-start | bytes 73736 | tf_op jit(solution)/shard_map/ppermute | solution.py:417
  5.4 3.8 %collective-permute-start.1 = (bf16[96,128]{1,0:T(8,128)(2,1)S(1)}, bf16[96,128]{1,0:T(8,128)(2,1)S(1)}, u32[]{:S(2)}, u32[]{:S(2)}) collective-permute-start(bf16[96,128]{1,0:T(8,128)(2,1)S(1)} %get-tuple-element.22), channel_id=1, source_target_pairs={{0,16},{4,0},{8,4},{12,8},{28,12},{24,28},{20,24},{16,20},{1,17},{... | collective-permute-start | bytes 73736 | tf_op jit(solution)/shard_map/ppermute | solution.py:418
  10.0 4.4 %collective-permute-start.2 = (bf16[96,384]{1,0:T(8,128)(2,1)S(1)}, bf16[96,384]{1,0:T(8,128)(2,1)S(1)}, u32[]{:S(2)}, u32[]{:S(2)}) collective-permute-start(bf16[96,384]{1,0:T(8,128)(2,1)S(1)} %get-tuple-element.24), channel_id=1, source_target_pairs={{0,2},{2,0},{1,3},{3,1},{4,6},{6,4},{5,7},{7,5},{8,10},{10,8},{9,1... | collective-permute-start | bytes 221192 | tf_op jit(solution)/shard_map/ppermute | solution.py:442
  20.2 1.6 %collective-permute-start.3 = (f32[3,192,128]{2,1,0:T(8,128)S(1)}, f32[3,192,128]{2,1,0:T(8,128)S(1)}, u32[]{:S(2)}, u32[]{:S(2)}) collective-permute-start(f32[3,192,128]{2,1,0:T(8,128)S(1)} %get-tuple-element.25.own_ref), channel_id=1, source_target_pairs={{0,1},{1,0},{2,3},{3,2},{4,5},{5,4},{6,7},{7,6},{8,9},{9,8},{10,11... | collective-permute-start | bytes 884744 | tf_op jit(solution)/shard_map/ppermute | solution.py:464
  27.0 1.2 %collective-permute-start.4 = (f32[2,128]{1,0:T(2,128)S(1)}, f32[2,128]{1,0:T(2,128)S(1)}, u32[]{:S(2)}, u32[]{:S(2)}) collective-permute-start(f32[2,128]{1,0:T(2,128)S(1)} %get-tuple-element.29), channel_id=1, source_target_pairs={{0,1},{1,0},{2,3},{3,2},{4,5},{5,4},{6,7},{7,6},{8,9},{9,8},{10,11... | collective-permute-start | bytes 3080 | tf_op jit(solution)/shard_map/ppermute | solution.py:484
  28.2 3.0 %collective-permute-start.5 = (f32[2,128]{1,0:T(2,128)S(1)}, f32[2,128]{1,0:T(2,128)S(1)}, u32[]{:S(2)}, u32[]{:S(2)}) collective-permute-start(f32[2,128]{1,0:T(2,128)S(1)} %add.20), channel_id=1, source_target_pairs={{0,3},{1,2},{2,1},{3,0},{4,7},{5,6},{6,5},{7,4},{8,11},{9,10},{10,... | collective-permute-start | bytes 3080 | tf_op jit(solution)/shard_map/ppermute | solution.py:60
  31.2 4.8 %collective-permute-start.8 = (f32[2,128]{1,0:T(2,128)S(1)}, f32[2,128]{1,0:T(2,128)S(1)}, u32[]{:S(2)}, u32[]{:S(2)}) collective-permute-start(f32[2,128]{1,0:T(2,128)S(1)} %add.21), channel_id=1, source_target_pairs={{0,13},{1,12},{4,9},{5,8},{8,5},{9,4},{12,1},{13,0},{2,15},{3,14},... | collective-permute-start | bytes 3080 | tf_op jit(solution)/shard_map/ppermute | solution.py:55
  34.5 3.0 %collective-permute-start.7 = (f32[2,128]{1,0:T(2,128)S(1)}, f32[2,128]{1,0:T(2,128)S(1)}, u32[]{:S(2)}, u32[]{:S(2)}) collective-permute-start(f32[2,128]{1,0:T(2,128)S(1)} %add.21), channel_id=1, source_target_pairs={{0,5},{1,4},{4,1},{5,0},{8,13},{9,12},{12,9},{13,8},{2,7},{3,6},{6... | collective-permute-start | bytes 3080 | tf_op jit(solution)/shard_map/ppermute | solution.py:55
  34.5 3.9 %collective-permute-start.6 = (f32[2,128]{1,0:T(2,128)S(1)}, f32[2,128]{1,0:T(2,128)S(1)}, u32[]{:S(2)}, u32[]{:S(2)}) collective-permute-start(f32[2,128]{1,0:T(2,128)S(1)} %add.21), channel_id=1, source_target_pairs={{0,9},{1,8},{4,13},{5,12},{8,1},{9,0},{12,5},{13,4},{2,11},{3,10},... | collective-permute-start | bytes 3080 | tf_op jit(solution)/shard_map/ppermute | solution.py:55

commit v5 on v4

--- a/solution.py
+++ b/solution.py
@@ -102,7 +102,7 @@
 
 
 def prepare_kernel(
-    ends_ref, params_hbm, target_hbm, params_ref, mask_ref, code_ref, ahead_ref, behind_ref, target_ref, sems
+    params_hbm, target_hbm, params_ref, mask_ref, code_ref, ahead_ref, behind_ref, target_ref, sems
 ):
     rows = params_ref.shape[0]
     wide = 2 * HALF
@@ -125,23 +125,35 @@
         up_ref[0:wide, :] = mask[0:wide]
         up_ref[wide:, :] = code[0:HALF]
 
-    pl.when(ends_ref[4] == 0)(lambda: edges(ahead_ref, behind_ref))
-    pl.when(ends_ref[4] == 1)(lambda: edges(behind_ref, ahead_ref))
+    pl.when(jnp.logical_not(turned_tile()))(lambda: edges(ahead_ref, behind_ref))
+    pl.when(turned_tile())(lambda: edges(behind_ref, ahead_ref))
 
 
 def unless(end, values):
-    return jnp.where(end == 1, 0.0, values.astype(F32))
+    return jnp.where(end, 0.0, values.astype(F32))
+
+
+def at_start(axis):
+    return lax.axis_index(axis) == 0
+
+
+def at_end(axis):
+    return lax.axis_index(axis) == lax.axis_size(axis) - 1
+
+
+def turned_tile():
+    return lax.axis_index("tiles") % 2 == 1
 
 
 def assemble_kernel(
-    ends_ref, mask_ref, code_ref, behind_ref, ahead_ref, _, centre_ref, code_out_ref, *side_refs
+    mask_ref, code_ref, behind_ref, ahead_ref, _, centre_ref, code_out_ref, *side_refs
 ):
     rows, cols = mask_ref.shape
     wide = 2 * HALF
-    turn = ends_ref[4] == 1
+    turn = turned_tile()
     behind, ahead = behind_ref[...].astype(F32), ahead_ref[...].astype(F32)
-    above = unless(ends_ref[2], jnp.where(turn, ahead, behind))
-    below = unless(ends_ref[3], jnp.where(turn, behind, ahead))
+    above = unless(at_start("strip"), jnp.where(turn, ahead, behind))
+    below = unless(at_end("strip"), jnp.where(turn, behind, ahead))
     tall = jnp.concatenate([above[0:wide], mask_ref[...].astype(F32), below[0:wide]], axis=0)
     turned = tall.T.astype(BF16)
     code = jnp.concatenate(
@@ -163,12 +175,11 @@
         right(side_refs[0])
         left(side_refs[1])
     else:
-        pl.when(ends_ref[0] == 1)(lambda: right(side_refs[0]))
-        pl.when(ends_ref[0] == 0)(lambda: left(side_refs[0]))
+        pl.when(at_start("col"))(lambda: right(side_refs[0]))
+        pl.when(at_end("col"))(lambda: left(side_refs[0]))
 
 
 def forward_kernel(
-    ends_ref,
     centre_ref,
     before_ref,
     after_ref,
@@ -192,9 +203,9 @@
 
     mask = jnp.concatenate(
         [
-            unless(ends_ref[0], before_ref[0:wide, :]).astype(BF16),
+            unless(at_start("col"), before_ref[0:wide, :]).astype(BF16),
             centre_ref[...],
-            unless(ends_ref[1], after_ref[0:wide, :]).astype(BF16),
+            unless(at_end("col"), after_ref[0:wide, :]).astype(BF16),
         ],
         axis=0,
     )
@@ -256,7 +267,6 @@
 
 
 def backward_kernel(
-    ends_ref,
     own_ref,
     other_ref,
     code_ref,
@@ -289,9 +299,9 @@
         lanes = slice(t * LANES, (t + 1) * LANES)
         code = jnp.concatenate(
             [
-                unless(ends_ref[0], code_before_ref[wide:, lanes]),
+                unless(at_start("col"), code_before_ref[wide:, lanes]),
                 code_ref[:, lanes].astype(F32),
-                unless(ends_ref[1], code_after_ref[wide:, lanes]),
+                unless(at_end("col"), code_after_ref[wide:, lanes]),
             ],
             axis=0,
         )
@@ -385,7 +395,6 @@
     units, back_units = FORWARD_UNROLL, BACKWARD_UNROLL
     if cols != LANES or rows % LANES or taps != wide + 1 or kernels % units or kernels % back_units:
         raise ValueError("block shape")
-    smem = pl.BlockSpec(memory_space=pltpu.SMEM)
     vmem = pl.BlockSpec(memory_space=pltpu.VMEM)
     hbm = pl.BlockSpec(memory_space=pltpu.HBM)
     array = jax.ShapeDtypeStruct
@@ -405,15 +414,13 @@
     plain, edge = array((rows, cols), BF16), array((wide + HALF, cols), BF16)
     full = array((rows, cols), F32)
     sides, strips = lax.axis_size("col"), lax.axis_size("strip")
-    place, level, turn = lax.axis_index("col"), lax.axis_index("strip"), lax.axis_index("tiles") % 2
-    ends = jnp.stack([place == 0, place == sides - 1, level == 0, level == strips - 1, turn == 1]).astype(jnp.int32)
     params, mask_half, code, ahead, behind = call(
         prepare_kernel,
         "prepare",
-        [smem, hbm, hbm],
+        [hbm, hbm],
         (full, plain, plain, edge, edge),
         scratch=[pltpu.VMEM((rows, cols), target.dtype), pltpu.SemaphoreType.DMA((2,))],
-    )(ends, stay(mask_params[0]), stay(target))
+    )(stay(mask_params[0]), stay(target))
     from_behind = lax.ppermute(ahead, ("tiles", "strip"), snake(1))
     from_ahead = lax.ppermute(behind, ("tiles", "strip"), snake(-1))
     (tap_rows,) = call(
@@ -435,9 +442,9 @@
     centre, code_turned, *messages = call(
         assemble_kernel,
         "assemble",
-        [smem, vmem, vmem, vmem, vmem, pl.BlockSpec(memory_space=pl.ANY)],
+        [vmem] * 4 + [pl.BlockSpec(memory_space=pl.ANY)],
         (turned, turned) + (side,) * (1 if sides == 2 else 2),
-    )(ends, mask_half, code, from_behind, from_ahead, tap_rows)
+    )(mask_half, code, from_behind, from_ahead, tap_rows)
     if sides == 2:
         before = after = lax.ppermute(messages[0], "col", ring("col", 1))
     else:
@@ -449,7 +456,7 @@
     field, intensity = call(
         forward_kernel,
         "forward",
-        [smem] + [vmem] * 4,
+        [vmem] * 4,
         (array((kernels, tiles, span, 2 * LANES), BF16), array(plane, F32)),
         scratch=[
             pltpu.VMEM((LANES, (cols // wide + 1) * long), BF16),
@@ -459,14 +466,14 @@
             pltpu.VMEM((units, tiles * span, 2 * LANES), BF16),
         ],
         grant=VMEM,
-    )(ends, centre, before, after, tap_rows)
+    )(centre, before, after, tap_rows)
 
     other = lax.ppermute(intensity, "expo", [(0, 1), (1, 0)])
 
     gradient, resist, sums = call(
         backward_kernel,
         "backward",
-        [smem] + [vmem] * 8,
+        [vmem] * 8,
         (full, full, array((2, LANES), F32)),
         out_specs=[vmem, hbm, vmem],
         scratch=[
@@ -479,7 +486,7 @@
             pltpu.SemaphoreType.DMA,
         ],
         grant=VMEM,
-    )(ends, intensity, other, code_turned, before, after, params, field, tap_rows)
+    )(intensity, other, code_turned, before, after, params, field, tap_rows)
 
     sums = sums + lax.ppermute(sums, "expo", [(0, 1), (1, 0)])
     for axis in ("col", "strip"):

time: 39.3 us -> 37.1 us (0.944)
  Pallas kernels: 14.8 us -> 12.7 us
    pallas_call x4, Pallas kernels: 13.2 us -> 11.1 us  [the longest x1 5.32 us: shards(): call(forward_kernel, 'forward', [vmem] * 4, (array((kernels, tiles, span,...]
where the time goes in v5:
time: 37.1 us; the launch traced here: 36.9 us
  waiting for transfers between devices  13.4 us (36%)
  Pallas kernels  12.7 us (34%)
  starting transfers between devices  10.1 us (27%)
  between operations  0.69 us (2%)
    pallas_call x1, Pallas kernels, shards(): call(forward_kernel, 'forward', [vmem] * 4, (array((kernels, tiles, span,...  5.32 us
    pallas_call x1, Pallas kernels, shards(): call(backward_kernel, 'backward', [vmem] * 8, (full, full, array((2, LANE...  4.6 us
    ppermute x3, starting transfers between devices, total_over(): lax.ppermute(value, both, partners(peers, lambda i, d=d: i ^ d))  3.88 us
    ppermute x3, waiting for transfers between devices, total_over(): lax.ppermute(value, both, partners(peers, lambda i, d=d: i ^ d))  3.35 us
    ppermute x1, starting transfers between devices, shards(): from_behind = lax.ppermute(ahead, ('tiles', 'strip'), snake(1))  3.1 us
    ppermute x1, waiting for transfers between devices, shards(): before = after = lax.ppermute(messages[0], 'col', ring('col', 1))  2.86 us
    ppermute x1, waiting for transfers between devices, shards(): from_ahead = lax.ppermute(behind, ('tiles', 'strip'), snake(-1))  2.07 us
    ppermute x1, waiting for transfers between devices, total_over(): lax.ppermute(value, both, partners(peers, lambda i, r=reach: i ^ r))  1.73 us
  transfers between devices with their start and end apart: 9, of which 9 were waited for; matrix products, arithmetic and copies ran while one was open for 0% of the time, Pallas kernels for 2%

profile of v5, /device:TPU:0, one launch (start us, length us, event | category | flops | bytes accessed | tf_op | source)
XLA Modules:
  0.0 36.9 jit_solution(10210133763750420040)
XLA Ops:
  0.6 1.0 %prepare.1 = (f32[256,128]{1,0:T(8,128)S(1)}, bf16[256,128]{1,0:T(8,128)(2,1)S(1)}, bf16[256,128]{1,0:T(8,128)(2,1)S(1)}, bf16[96,128]{1,0:T(8,128)(2,1)S(1)}, bf16[96,128]{1,0:T(8,128)(2,1)S(1)}) custom-call(f32[256,128]{1,0:T(8,128)} %bitcast.4, s32[256,128]{1,0:T(8,128)} %target_hbm.1), custom_call_target="tpu_custom_call" | custom-call | flops 1000000 | bytes 1000000 | tf_op jit(solution)/shard_map/prepare/pallas_call | solution.py:417
  1.7 3.1 %collective-permute-start = (bf16[96,128]{1,0:T(8,128)(2,1)S(1)}, bf16[96,128]{1,0:T(8,128)(2,1)S(1)}, u32[]{:S(2)}, u32[]{:S(2)}) collective-permute-start(bf16[96,128]{1,0:T(8,128)(2,1)S(1)} %get-tuple-element.21), channel_id=1, source_target_pairs={{0,4},{4,8},{8,12},{12,28},{28,24},{24,20},{20,16},{16,0},{1,5},{5... | collective-permute-start | bytes 73736 | tf_op jit(solution)/shard_map/ppermute | solution.py:424
  4.8 0.0 collective-permute-start.1
  4.8 0.9 %taps.1._.taps_ref = f32[24,8,256]{2,1,0:T(8,128)S(1)} custom-call(f32[24]{0:T(128)} %weights_hbm.1, bf16[24,2,65]{2,1,0:T(2,128)(2,1)} %col_hbm.1, bf16[24,2,65]{2,1,0:T(2,128)(2,1)} %row_hbm.1), custom_call_target="tpu_custom_call" | custom-call | flops 100000000 | bytes 1000000 | tf_op jit(solution)/shard_map/taps/pallas_call | solution.py:426
  5.7 0.8 %collective-permute-done.behind_ref = bf16[96,128]{1,0:T(8,128)(2,1)S(1)} collective-permute-done((bf16[96,128]{1,0:T(8,128)(2,1)S(1)}, bf16[96,128]{1,0:T(8,128)(2,1)S(1)}, u32[]{:S(2)}, u32[]{:S(2)}) %collective-permute-start) | collective-permute-done | bytes 24608 | tf_op jit(solution)/shard_map/ppermute | solution.py:424
  6.5 2.1 %collective-permute-done.1.ahead_ref = bf16[96,128]{1,0:T(8,128)(2,1)S(1)} collective-permute-done((bf16[96,128]{1,0:T(8,128)(2,1)S(1)}, bf16[96,128]{1,0:T(8,128)(2,1)S(1)}, u32[]{:S(2)}, u32[]{:S(2)}) %collective-permute-start.1) | collective-permute-done | bytes 24608 | tf_op jit(solution)/shard_map/ppermute | solution.py:425
  8.6 0.2 assemble.1
  8.7 1.6 %collective-permute-start.2 = (bf16[96,384]{1,0:T(8,128)(2,1)S(1)}, bf16[96,384]{1,0:T(8,128)(2,1)S(1)}, u32[]{:S(2)}, u32[]{:S(2)}) collective-permute-start(bf16[96,384]{1,0:T(8,128)(2,1)S(1)} %get-tuple-element.24), channel_id=1, source_target_pairs={{0,2},{2,0},{1,3},{3,1},{4,6},{6,4},{5,7},{7,5},{8,10},{10,8},{9,1... | collective-permute-start | bytes 221192 | tf_op jit(solution)/shard_map/ppermute | solution.py:449
  10.3 2.9 %collective-permute-done.2.before_ref.after_ref.code_before_ref.code_after_ref = bf16[96,384]{1,0:T(8,128)(2,1)S(1)} collective-permute-done((bf16[96,384]{1,0:T(8,128)(2,1)S(1)}, bf16[96,384]{1,0:T(8,128)(2,1)S(1)}, u32[]{:S(2)}, u32[]{:S(2)}) %collective-permute-start.2) | collective-permute-done | bytes 73760 | tf_op jit(solution)/shard_map/ppermute | solution.py:449
  13.2 5.3 %forward.1 = (bf16[24,3,192,256]{3,2,1,0:T(8,128)(2,1)S(1)}, f32[3,192,128]{2,1,0:T(8,128)S(1)}) custom-call(bf16[128,384]{1,0:T(8,128)(2,1)S(1)} %get-tuple-element.23.centre_ref, bf16[96,384]{1,0:T(8,128)(2,1)S(1)} %collective-permute-done.2.before_ref.after_ref.code_before_ref.code_after_ref, ...), custom_call_target="tpu_custom_call" | custom-call | flops 1000000 | bytes 1000000 | tf_op jit(solution)/shard_map/forward/pallas_call | solution.py:456
  18.5 0.1 collective-permute-start.3
  18.6 1.6 %collective-permute-done.3.other_ref = f32[3,192,128]{2,1,0:T(8,128)S(1)} collective-permute-done((f32[3,192,128]{2,1,0:T(8,128)S(1)}, f32[3,192,128]{2,1,0:T(8,128)S(1)}, u32[]{:S(2)}, u32[]{:S(2)}) %collective-permute-start.3) | collective-permute-done | bytes 294944 | tf_op jit(solution)/shard_map/ppermute | solution.py:471
  20.1 4.6 %backward.1 = (f32[256,128]{1,0:T(8,128)S(1)}, f32[256,128]{1,0:T(8,128)}, f32[2,128]{1,0:T(2,128)S(1)}) custom-call(f32[3,192,128]{2,1,0:T(8,128)S(1)} %get-tuple-element.25.own_ref, f32[3,192,128]{2,1,0:T(8,128)S(1)} %collective-permute-done.3.other_ref, bf16[128,384]{1,0:T(8,128)(2,1)S(1)} %get-tuple-element.26.code_ref, ...), custom_call_target="tpu_custom_call" | custom-call | flops 1000000 | bytes 1000000 | tf_op jit(solution)/shard_map/backward/pallas_call | solution.py:473
  24.8 0.2 collective-permute-start.4
  25.0 1.0 %collective-permute-done.4 = f32[2,128]{1,0:T(2,128)S(1)} collective-permute-done((f32[2,128]{1,0:T(2,128)S(1)}, f32[2,128]{1,0:T(2,128)S(1)}, u32[]{:S(2)}, u32[]{:S(2)}) %collective-permute-start.4) | collective-permute-done | bytes 1056 | tf_op jit(solution)/shard_map/ppermute | solution.py:491
  26.0 1.3 %collective-permute-start.5 = (f32[2,128]{1,0:T(2,128)S(1)}, f32[2,128]{1,0:T(2,128)S(1)}, u32[]{:S(2)}, u32[]{:S(2)}) collective-permute-start(f32[2,128]{1,0:T(2,128)S(1)} %add.15), channel_id=1, source_target_pairs={{0,3},{1,2},{2,1},{3,0},{4,7},{5,6},{6,5},{7,4},{8,11},{9,10},{10,... | collective-permute-start | bytes 3080 | tf_op jit(solution)/shard_map/ppermute | solution.py:60
  27.3 1.7 %collective-permute-done.5 = f32[2,128]{1,0:T(2,128)S(1)} collective-permute-done((f32[2,128]{1,0:T(2,128)S(1)}, f32[2,128]{1,0:T(2,128)S(1)}, u32[]{:S(2)}, u32[]{:S(2)}) %collective-permute-start.5) | collective-permute-done | bytes 1056 | tf_op jit(solution)/shard_map/ppermute | solution.py:60
  29.0 3.3 %collective-permute-start.8 = (f32[2,128]{1,0:T(2,128)S(1)}, f32[2,128]{1,0:T(2,128)S(1)}, u32[]{:S(2)}, u32[]{:S(2)}) collective-permute-start(f32[2,128]{1,0:T(2,128)S(1)} %add.16), channel_id=1, source_target_pairs={{0,13},{1,12},{4,9},{5,8},{8,5},{9,4},{12,1},{13,0},{2,15},{3,14},... | collective-permute-start | bytes 3080 | tf_op jit(solution)/shard_map/ppermute | solution.py:55
  32.3 0.0 collective-permute-start.7
  32.3 0.6 %collective-permute-start.6 = (f32[2,128]{1,0:T(2,128)S(1)}, f32[2,128]{1,0:T(2,128)S(1)}, u32[]{:S(2)}, u32[]{:S(2)}) collective-permute-start(f32[2,128]{1,0:T(2,128)S(1)} %add.16), channel_id=1, source_target_pairs={{0,9},{1,8},{4,13},{5,12},{8,1},{9,0},{12,5},{13,4},{2,11},{3,10},... | collective-permute-start | bytes 3080 | tf_op jit(solution)/shard_map/ppermute | solution.py:55
  32.9 0.9 %collective-permute-done.8 = f32[2,128]{1,0:T(2,128)S(1)} collective-permute-done((f32[2,128]{1,0:T(2,128)S(1)}, f32[2,128]{1,0:T(2,128)S(1)}, u32[]{:S(2)}, u32[]{:S(2)}) %collective-permute-start.8) | collective-permute-done | bytes 1056 | tf_op jit(solution)/shard_map/ppermute | solution.py:55
  33.8 1.5 %collective-permute-done.7 = f32[2,128]{1,0:T(2,128)S(1)} collective-permute-done((f32[2,128]{1,0:T(2,128)S(1)}, f32[2,128]{1,0:T(2,128)S(1)}, u32[]{:S(2)}, u32[]{:S(2)}) %collective-permute-start.7) | collective-permute-done | bytes 1056 | tf_op jit(solution)/shard_map/ppermute | solution.py:55
  35.3 0.9 %collective-permute-done.6 = f32[2,128]{1,0:T(2,128)S(1)} collective-permute-done((f32[2,128]{1,0:T(2,128)S(1)}, f32[2,128]{1,0:T(2,128)S(1)}, u32[]{:S(2)}, u32[]{:S(2)}) %collective-permute-start.6) | collective-permute-done | bytes 1056 | tf_op jit(solution)/shard_map/ppermute | solution.py:55
  36.2 0.7 %finish.1 = (f32[256,128]{1,0:T(8,128)}, f32[1,128]{1,0:T(1,128)}) custom-call(f32[256,128]{1,0:T(8,128)S(1)} %get-tuple-element.18.params_ref, f32[256,128]{1,0:T(8,128)S(1)} %get-tuple-element.28.gradient_ref, f32[2,128]{1,0:T(2,128)S(1)} %add_add_fusion.sums_ref), custom_call_target="tpu_custom_call" | custom-call | flops 1000000 | bytes 1000000 | tf_op jit(solution)/shard_map/finish/pallas_call | solution.py:495
  (3 shorter events, 0.0 us)
Async XLA Ops:
  1.7 4.9 %collective-permute-start = (bf16[96,128]{1,0:T(8,128)(2,1)S(1)}, bf16[96,128]{1,0:T(8,128)(2,1)S(1)}, u32[]{:S(2)}, u32[]{:S(2)}) collective-permute-start(bf16[96,128]{1,0:T(8,128)(2,1)S(1)} %get-tuple-element.21), channel_id=1, source_target_pairs={{0,4},{4,8},{8,12},{12,28},{28,24},{24,20},{20,16},{16,0},{1,5},{5... | collective-permute-start | bytes 73736 | tf_op jit(solution)/shard_map/ppermute | solution.py:424
  4.8 3.8 %collective-permute-start.1 = (bf16[96,128]{1,0:T(8,128)(2,1)S(1)}, bf16[96,128]{1,0:T(8,128)(2,1)S(1)}, u32[]{:S(2)}, u32[]{:S(2)}) collective-permute-start(bf16[96,128]{1,0:T(8,128)(2,1)S(1)} %get-tuple-element.22), channel_id=1, source_target_pairs={{0,16},{4,0},{8,4},{12,8},{28,12},{24,28},{20,24},{16,20},{1,17},{... | collective-permute-start | bytes 73736 | tf_op jit(solution)/shard_map/ppermute | solution.py:425
  8.7 4.4 %collective-permute-start.2 = (bf16[96,384]{1,0:T(8,128)(2,1)S(1)}, bf16[96,384]{1,0:T(8,128)(2,1)S(1)}, u32[]{:S(2)}, u32[]{:S(2)}) collective-permute-start(bf16[96,384]{1,0:T(8,128)(2,1)S(1)} %get-tuple-element.24), channel_id=1, source_target_pairs={{0,2},{2,0},{1,3},{3,1},{4,6},{6,4},{5,7},{7,5},{8,10},{10,8},{9,1... | collective-permute-start | bytes 221192 | tf_op jit(solution)/shard_map/ppermute | solution.py:449
  18.5 1.6 %collective-permute-start.3 = (f32[3,192,128]{2,1,0:T(8,128)S(1)}, f32[3,192,128]{2,1,0:T(8,128)S(1)}, u32[]{:S(2)}, u32[]{:S(2)}) collective-permute-start(f32[3,192,128]{2,1,0:T(8,128)S(1)} %get-tuple-element.25.own_ref), channel_id=1, source_target_pairs={{0,1},{1,0},{2,3},{3,2},{4,5},{5,4},{6,7},{7,6},{8,9},{9,8},{10,11... | collective-permute-start | bytes 884744 | tf_op jit(solution)/shard_map/ppermute | solution.py:471
  24.8 1.2 %collective-permute-start.4 = (f32[2,128]{1,0:T(2,128)S(1)}, f32[2,128]{1,0:T(2,128)S(1)}, u32[]{:S(2)}, u32[]{:S(2)}) collective-permute-start(f32[2,128]{1,0:T(2,128)S(1)} %get-tuple-element.29), channel_id=1, source_target_pairs={{0,1},{1,0},{2,3},{3,2},{4,5},{5,4},{6,7},{7,6},{8,9},{9,8},{10,11... | collective-permute-start | bytes 3080 | tf_op jit(solution)/shard_map/ppermute | solution.py:491
  26.0 3.0 %collective-permute-start.5 = (f32[2,128]{1,0:T(2,128)S(1)}, f32[2,128]{1,0:T(2,128)S(1)}, u32[]{:S(2)}, u32[]{:S(2)}) collective-permute-start(f32[2,128]{1,0:T(2,128)S(1)} %add.15), channel_id=1, source_target_pairs={{0,3},{1,2},{2,1},{3,0},{4,7},{5,6},{6,5},{7,4},{8,11},{9,10},{10,... | collective-permute-start | bytes 3080 | tf_op jit(solution)/shard_map/ppermute | solution.py:60
  29.0 4.8 %collective-permute-start.8 = (f32[2,128]{1,0:T(2,128)S(1)}, f32[2,128]{1,0:T(2,128)S(1)}, u32[]{:S(2)}, u32[]{:S(2)}) collective-permute-start(f32[2,128]{1,0:T(2,128)S(1)} %add.16), channel_id=1, source_target_pairs={{0,13},{1,12},{4,9},{5,8},{8,5},{9,4},{12,1},{13,0},{2,15},{3,14},... | collective-permute-start | bytes 3080 | tf_op jit(solution)/shard_map/ppermute | solution.py:55
  32.3 3.0 %collective-permute-start.7 = (f32[2,128]{1,0:T(2,128)S(1)}, f32[2,128]{1,0:T(2,128)S(1)}, u32[]{:S(2)}, u32[]{:S(2)}) collective-permute-start(f32[2,128]{1,0:T(2,128)S(1)} %add.16), channel_id=1, source_target_pairs={{0,5},{1,4},{4,1},{5,0},{8,13},{9,12},{12,9},{13,8},{2,7},{3,6},{6... | collective-permute-start | bytes 3080 | tf_op jit(solution)/shard_map/ppermute | solution.py:55
  32.3 3.9 %collective-permute-start.6 = (f32[2,128]{1,0:T(2,128)S(1)}, f32[2,128]{1,0:T(2,128)S(1)}, u32[]{:S(2)}, u32[]{:S(2)}) collective-permute-start(f32[2,128]{1,0:T(2,128)S(1)} %add.16), channel_id=1, source_target_pairs={{0,9},{1,8},{4,13},{5,12},{8,1},{9,0},{12,5},{13,4},{2,11},{3,10},... | collective-permute-start | bytes 3080 | tf_op jit(solution)/shard_map/ppermute | solution.py:55

commit v6 on v5

--- a/solution.py
+++ b/solution.py
@@ -8,7 +8,6 @@
 
 HALF = 32
 LANES = 128
-FORWARD_UNROLL = 24
 BACKWARD_UNROLL = 12
 CHUNK = 4
 VMEM = 24 * 2**20
@@ -179,91 +178,76 @@
         pl.when(at_end("col"))(lambda: left(side_refs[0]))
 
 
-def forward_kernel(
-    centre_ref,
-    before_ref,
-    after_ref,
-    taps_ref,
-    field_ref,
-    intensity_ref,
-    mask_ref,
-    total_ref,
-    masks_ref,
-    table_ref,
-    columns_ref,
-):
+def correlate(taps_ref, source_ref, field_ref, total_ref, masks_ref, table_ref, columns_ref):
     kernels = taps_ref.shape[0]
-    units = columns_ref.shape[0]
-    cols = centre_ref.shape[0]
+    tiles, span = field_ref.shape[1:3]
     wide = 2 * HALF
-    long = centre_ref.shape[1]
-    tiles = long // LANES
-    blocks = cols // wide + 1
-    span = cols + wide
-
-    mask = jnp.concatenate(
-        [
-            unless(at_start("col"), before_ref[0:wide, :]).astype(BF16),
-            centre_ref[...],
-            unless(at_end("col"), after_ref[0:wide, :]).astype(BF16),
-        ],
-        axis=0,
-    )
-    for block in range(blocks):
-        mask_ref[:, block * long : (block + 1) * long] = mask[block * wide : block * wide + LANES]
+    long = tiles * LANES
     total_ref[...] = jnp.zeros_like(total_ref)
     write_masks(masks_ref)
-
-    def group(step, carry):
-        for unit in range(units):
-            for part in range(2):
-                row = taps_ref[step * units + unit, part : part + 1, 0:LANES]
-                base = circulant(row, 0)[0:wide]
-                at = (unit * 2 + part) * wide
-                table_ref[at : at + wide, :] = base * masks_ref[0, 0:wide]
-        columns = jnp.dot(table_ref[...], mask_ref[...], preferred_element_type=F32).astype(BF16)
-        for unit in range(units):
-            for part in range(2):
-                at = (unit * 2 + part) * wide
-                for block in range(blocks):
-                    for t in range(tiles):
-                        lane = block * long + t * LANES
-                        to = t * span + block * wide
-                        columns_ref[unit, to : to + wide, part * LANES : (part + 1) * LANES] = columns[
-                            at : at + wide, lane : lane + LANES
-                        ]
-        for unit in range(units):
-            kernel = step * units + unit
-            near, far = [], []
-            for part in range(2):
-                base = circulant(taps_ref[kernel, 2 + part : 3 + part, LANES:], LANES // 2)
-                near.append(base * masks_ref[2])
-                far.append(base * masks_ref[3])
-            near = [
-                jnp.concatenate([near[0], near[1]], axis=1),
-                jnp.concatenate([-near[1], near[0]], axis=1),
-            ]
-            far = [
-                jnp.concatenate([far[0], far[1]], axis=1),
-                jnp.concatenate([-far[1], far[0]], axis=1),
-            ]
-            weight = taps_ref[kernel, 4:5, :]
-            edge = (tiles - 1) * span
-            window = jnp.concatenate([columns_ref[unit, 0:edge], columns_ref[unit, span:]], axis=1)
-            inner = jnp.dot(window, jnp.concatenate(near + far, axis=0), preferred_element_type=F32)
-            outer = jnp.dot(
-                columns_ref[unit, edge:], jnp.concatenate(near, axis=0), preferred_element_type=F32
-            )
-            for t in range(tiles):
-                part = inner[t * span : (t + 1) * span] if t + 1 < tiles else outer
-                scaled = weight * part
-                field_ref[kernel, t] = scaled.astype(field_ref.dtype)
-                total_ref[t] += scaled * part
-        return carry
-
-    lax.fori_loop(0, kernels // units, group, 0)
-    for t in range(tiles):
+    for kernel in range(kernels):
+        for part in range(2):
+            base = circulant(taps_ref[kernel, part : part + 1, 0:LANES], 0)[0:wide]
+            at = (kernel * 2 + part) * wide
+            table_ref[at : at + wide, :] = base * masks_ref[0, 0:wide]
+    columns = jnp.dot(table_ref[...], source_ref[...], preferred_element_type=F32).astype(BF16)
+    for kernel in range(kernels):
+        for part in range(2):
+            at = (kernel * 2 + part) * wide
+            for block in range(span // wide):
+                for t in range(tiles):
+                    lane = block * long + t * LANES
+                    to = t * span + block * wide
+                    columns_ref[kernel, to : to + wide, part * LANES : (part + 1) * LANES] = columns[
+                        at : at + wide, lane : lane + LANES
+                    ]
+    edge = (tiles - 1) * span
+    for kernel in range(kernels):
+        near, far = [], []
+        for part in range(2):
+            base = circulant(taps_ref[kernel, 2 + part : 3 + part, LANES:], LANES // 2)
+            near.append(base * masks_ref[2])
+            far.append(base * masks_ref[3])
+        near = [
+            jnp.concatenate([near[0], near[1]], axis=1),
+            jnp.concatenate([-near[1], near[0]], axis=1),
+        ]
+        far = [
+            jnp.concatenate([far[0], far[1]], axis=1),
+            jnp.concatenate([-far[1], far[0]], axis=1),
+        ]
+        weight = taps_ref[kernel, 4:5, :]
+        window = jnp.concatenate([columns_ref[kernel, 0:edge], columns_ref[kernel, span:]], axis=1)
+        inner = jnp.dot(window, jnp.concatenate(near + far, axis=0), preferred_element_type=F32)
+        outer = jnp.dot(columns_ref[kernel, edge:], jnp.concatenate(near, axis=0), preferred_element_type=F32)
+        for t in range(tiles):
+            part = inner[t * span : (t + 1) * span] if t + 1 < tiles else outer
+            scaled = weight * part
+            field_ref[kernel, t] = scaled.astype(field_ref.dtype)
+            total_ref[t] += scaled * part
+
+
+def middle_kernel(centre_ref, taps_ref, field_ref, intensity_ref, total_ref, *scratch):
+    correlate(taps_ref, centre_ref, field_ref, total_ref, *scratch)
+    for t in range(total_ref.shape[0]):
         intensity_ref[t] = total_ref[t, :, 0:LANES] + total_ref[t, :, LANES:]
+
+
+def side_kernel(
+    centre_ref, before_ref, after_ref, taps_ref, middle_ref, field_ref, intensity_ref, total_ref, source_ref, *scratch
+):
+    wide = 2 * HALF
+    cols, long = centre_ref.shape
+    source_ref[0:wide, 0:long] = unless(at_start("col"), before_ref[0:wide, :]).astype(BF16)
+    source_ref[wide:, 0:long] = centre_ref[0:wide, :]
+    source_ref[0:wide, long:] = centre_ref[cols - wide :, :]
+    source_ref[wide:, long:] = unless(at_end("col"), after_ref[0:wide, :]).astype(BF16)
+    correlate(taps_ref, source_ref, field_ref, total_ref, *scratch)
+    for t in range(total_ref.shape[0]):
+        intensity = total_ref[t, :, 0:LANES] + total_ref[t, :, LANES:]
+        intensity_ref[t, 0:wide] = intensity[0:wide]
+        intensity_ref[t, wide : 2 * wide] = middle_ref[t]
+        intensity_ref[t, 2 * wide :] = intensity[wide:]
 
 
 def backward_kernel(
@@ -273,7 +257,8 @@
     code_before_ref,
     code_after_ref,
     params_ref,
-    field_ref,
+    middle_ref,
+    side_ref,
     taps_ref,
     gradient_ref,
     resist_hbm,
@@ -342,7 +327,13 @@
                 ],
                 axis=0,
             )
-            products = [slope_ref[t] * field_ref[kernel, t] for t in range(tiles)]
+            products = [
+                slope_ref[t]
+                * jnp.concatenate(
+                    [side_ref[kernel, t, 0:wide], middle_ref[kernel, t], side_ref[kernel, t, wide:]], axis=0
+                )
+                for t in range(tiles)
+            ]
             window = jnp.concatenate(
                 [jnp.concatenate(products[:-1], axis=0), jnp.concatenate(products[1:], axis=0)], axis=1
             )
@@ -392,8 +383,8 @@
     wide = 2 * HALF
     tiles = rows // LANES + 1
     long, span = tiles * LANES, cols + wide
-    units, back_units = FORWARD_UNROLL, BACKWARD_UNROLL
-    if cols != LANES or rows % LANES or taps != wide + 1 or kernels % units or kernels % back_units:
+    back_units = BACKWARD_UNROLL
+    if cols != LANES or rows % LANES or taps != wide + 1 or kernels % back_units:
         raise ValueError("block shape")
     vmem = pl.BlockSpec(memory_space=pltpu.VMEM)
     hbm = pl.BlockSpec(memory_space=pltpu.HBM)
@@ -452,28 +443,43 @@
         after = lax.ppermute(messages[1], "col", ring("col", -1))
 
     masks = pltpu.VMEM((4, LANES, LANES), BF16)
+
+    def part(width):
+        fields = array((kernels, tiles, width, 2 * LANES), BF16)
+        scratch = [
+            masks,
+            pltpu.VMEM((kernels * 2 * wide, LANES), BF16),
+            pltpu.VMEM((kernels, tiles * width, 2 * LANES), BF16),
+        ]
+        return fields, pltpu.VMEM((tiles, width, 2 * LANES), F32), scratch
+
+    fields, total, scratch = part(wide)
+    middle, middle_intensity = call(
+        middle_kernel,
+        "middle",
+        [vmem] * 2,
+        (fields, array((tiles, wide, LANES), F32)),
+        scratch=[total] + scratch,
+        grant=VMEM,
+        flops=4 * 10**9,
+    )(centre, tap_rows)
     plane = (tiles, span, LANES)
-    field, intensity = call(
-        forward_kernel,
-        "forward",
-        [vmem] * 4,
-        (array((kernels, tiles, span, 2 * LANES), BF16), array(plane, F32)),
-        scratch=[
-            pltpu.VMEM((LANES, (cols // wide + 1) * long), BF16),
-            pltpu.VMEM((tiles, span, 2 * LANES), F32),
-            masks,
-            pltpu.VMEM((units * 2 * wide, LANES), BF16),
-            pltpu.VMEM((units, tiles * span, 2 * LANES), BF16),
-        ],
+    fields, total, scratch = part(2 * wide)
+    sides_field, intensity = call(
+        side_kernel,
+        "side",
+        [vmem] * 5,
+        (fields, array(plane, F32)),
+        scratch=[total, pltpu.VMEM((LANES, 2 * long), BF16)] + scratch,
         grant=VMEM,
-    )(centre, before, after, tap_rows)
+    )(centre, before, after, tap_rows, middle_intensity)
 
     other = lax.ppermute(intensity, "expo", [(0, 1), (1, 0)])
 
     gradient, resist, sums = call(
         backward_kernel,
         "backward",
-        [vmem] * 8,
+        [vmem] * 9,
         (full, full, array((2, LANES), F32)),
         out_specs=[vmem, hbm, vmem],
         scratch=[
@@ -486,7 +492,7 @@
             pltpu.SemaphoreType.DMA,
         ],
         grant=VMEM,
-    )(intensity, other, code_turned, before, after, params, field, tap_rows)
+    )(intensity, other, code_turned, before, after, params, middle, sides_field, tap_rows)
 
     sums = sums + lax.ppermute(sums, "expo", [(0, 1), (1, 0)])
     for axis in ("col", "strip"):

time: 37.1 us -> 35.6 us (0.960)
  waiting for transfers between devices: 13.4 us -> 11.2 us
  Pallas kernels: 12.7 us -> 13.5 us
    ppermute x1, waiting for transfers between devices: 2.86 us -> 0.61 us  [shards(): before = after = lax.ppermute(messages[0], 'col', ring('col', 1))]
    pallas_call x2 -> x3, Pallas kernels: 9.92 us -> 10.7 us  [the longest x1 4.61 us: shards(): call(backward_kernel, 'backward', [vmem] * 9, (full, full, array((2, LANE...]
  transfers between devices with their start and end apart: 9 -> 9, of which waited for: 9 -> 9; matrix products, arithmetic and copies ran while one was open for 0% -> 0% of each run, Pallas kernels for 2% -> 9%
where the time goes in v6:
time: 35.6 us; the launch traced here: 35.5 us
  Pallas kernels  13.5 us (38%)
  waiting for transfers between devices  11.2 us (31%)
  starting transfers between devices  10.1 us (28%)
  between operations  0.69 us (2%)
    pallas_call x1, Pallas kernels, shards(): call(backward_kernel, 'backward', [vmem] * 9, (full, full, array((2, LANE...  4.61 us
    ppermute x3, starting transfers between devices, total_over(): lax.ppermute(value, both, partners(peers, lambda i, d=d: i ^ d))  3.88 us
    pallas_call x1, Pallas kernels, shards(): call(side_kernel, 'side', [vmem] * 5, (fields, array(plane, F32)), scratc...  3.87 us
    ppermute x3, waiting for transfers between devices, total_over(): lax.ppermute(value, both, partners(peers, lambda i, d=d: i ^ d))  3.33 us
    ppermute x1, starting transfers between devices, shards(): from_behind = lax.ppermute(ahead, ('tiles', 'strip'), snake(1))  3.1 us
    pallas_call x1, Pallas kernels, shards(): call(middle_kernel, 'middle', [vmem] * 2, (fields, array((tiles, wide, LA...  2.25 us
    ppermute x1, waiting for transfers between devices, shards(): from_ahead = lax.ppermute(behind, ('tiles', 'strip'), snake(-1))  2.07 us
    ppermute x1, waiting for transfers between devices, total_over(): lax.ppermute(value, both, partners(peers, lambda i, r=reach: i ^ r))  1.73 us
  transfers between devices with their start and end apart: 9, of which 9 were waited for; matrix products, arithmetic and copies ran while one was open for 0% of the time, Pallas kernels for 9%

profile of v6, /device:TPU:0, one launch (start us, length us, event | category | flops | bytes accessed | tf_op | source)
XLA Modules:
  0.0 35.5 jit_solution(2791258026406479124)
XLA Ops:
  0.6 1.0 %prepare.1 = (f32[256,128]{1,0:T(8,128)S(1)}, bf16[256,128]{1,0:T(8,128)(2,1)S(1)}, bf16[256,128]{1,0:T(8,128)(2,1)S(1)}, bf16[96,128]{1,0:T(8,128)(2,1)S(1)}, bf16[96,128]{1,0:T(8,128)(2,1)S(1)}) custom-call(f32[256,128]{1,0:T(8,128)} %bitcast.4, s32[256,128]{1,0:T(8,128)} %target_hbm.1), custom_call_target="tpu_custom_call" | custom-call | flops 1000000 | bytes 1000000 | tf_op jit(solution)/shard_map/prepare/pallas_call | solution.py:408
  1.7 3.1 %collective-permute-start = (bf16[96,128]{1,0:T(8,128)(2,1)S(1)}, bf16[96,128]{1,0:T(8,128)(2,1)S(1)}, u32[]{:S(2)}, u32[]{:S(2)}) collective-permute-start(bf16[96,128]{1,0:T(8,128)(2,1)S(1)} %get-tuple-element.23), channel_id=1, source_target_pairs={{0,4},{4,8},{8,12},{12,28},{28,24},{24,20},{20,16},{16,0},{1,5},{5... | collective-permute-start | bytes 73736 | tf_op jit(solution)/shard_map/ppermute | solution.py:415
  4.8 0.0 collective-permute-start.1
  4.8 0.9 %taps.1._.taps_ref = f32[24,8,256]{2,1,0:T(8,128)S(1)} custom-call(f32[24]{0:T(128)} %weights_hbm.1, bf16[24,2,65]{2,1,0:T(2,128)(2,1)} %col_hbm.1, bf16[24,2,65]{2,1,0:T(2,128)(2,1)} %row_hbm.1), custom_call_target="tpu_custom_call" | custom-call | flops 100000000 | bytes 1000000 | tf_op jit(solution)/shard_map/taps/pallas_call | solution.py:417
  5.7 0.8 %collective-permute-done.behind_ref = bf16[96,128]{1,0:T(8,128)(2,1)S(1)} collective-permute-done((bf16[96,128]{1,0:T(8,128)(2,1)S(1)}, bf16[96,128]{1,0:T(8,128)(2,1)S(1)}, u32[]{:S(2)}, u32[]{:S(2)}) %collective-permute-start) | collective-permute-done | bytes 24608 | tf_op jit(solution)/shard_map/ppermute | solution.py:415
  6.5 2.1 %collective-permute-done.1.ahead_ref = bf16[96,128]{1,0:T(8,128)(2,1)S(1)} collective-permute-done((bf16[96,128]{1,0:T(8,128)(2,1)S(1)}, bf16[96,128]{1,0:T(8,128)(2,1)S(1)}, u32[]{:S(2)}, u32[]{:S(2)}) %collective-permute-start.1) | collective-permute-done | bytes 24608 | tf_op jit(solution)/shard_map/ppermute | solution.py:416
  8.6 0.2 assemble.1
  8.7 1.6 %collective-permute-start.2 = (bf16[96,384]{1,0:T(8,128)(2,1)S(1)}, bf16[96,384]{1,0:T(8,128)(2,1)S(1)}, u32[]{:S(2)}, u32[]{:S(2)}) collective-permute-start(bf16[96,384]{1,0:T(8,128)(2,1)S(1)} %get-tuple-element.26), channel_id=1, source_target_pairs={{0,2},{2,0},{1,3},{3,1},{4,6},{6,4},{5,7},{7,5},{8,10},{10,8},{9,1... | collective-permute-start | bytes 221192 | tf_op jit(solution)/shard_map/ppermute | solution.py:440
  10.3 2.2 %middle.1 = (bf16[24,3,64,256]{3,2,1,0:T(8,128)(2,1)S(1)}, f32[3,64,128]{2,1,0:T(8,128)S(1)}) custom-call(bf16[128,384]{1,0:T(8,128)(2,1)S(1)} %get-tuple-element.25.centre_ref, f32[24,8,256]{2,1,0:T(8,128)S(1)} %taps.1._.taps_ref), custom_call_target="tpu_custom_call" | custom-call | flops 4000000000 | bytes 1000000 | tf_op jit(solution)/shard_map/middle/pallas_call | solution.py:457
  12.6 0.6 %collective-permute-done.2.before_ref.after_ref.code_before_ref.code_after_ref = bf16[96,384]{1,0:T(8,128)(2,1)S(1)} collective-permute-done((bf16[96,384]{1,0:T(8,128)(2,1)S(1)}, bf16[96,384]{1,0:T(8,128)(2,1)S(1)}, u32[]{:S(2)}, u32[]{:S(2)}) %collective-permute-start.2) | collective-permute-done | bytes 73760 | tf_op jit(solution)/shard_map/ppermute | solution.py:440
  13.2 3.9 %side.1 = (bf16[24,3,128,256]{3,2,1,0:T(8,128)(2,1)S(1)}, f32[3,192,128]{2,1,0:T(8,128)S(1)}) custom-call(bf16[128,384]{1,0:T(8,128)(2,1)S(1)} %get-tuple-element.25.centre_ref, bf16[96,384]{1,0:T(8,128)(2,1)S(1)} %collective-permute-done.2.before_ref.after_ref.code_before_ref.code_after_ref, ...), custom_call_target="tpu_custom_call" | custom-call | flops 1000000 | bytes 1000000 | tf_op jit(solution)/shard_map/side/pallas_call | solution.py:468
  17.0 0.1 collective-permute-start.3
  17.1 1.6 %collective-permute-done.3.other_ref = f32[3,192,128]{2,1,0:T(8,128)S(1)} collective-permute-done((f32[3,192,128]{2,1,0:T(8,128)S(1)}, f32[3,192,128]{2,1,0:T(8,128)S(1)}, u32[]{:S(2)}, u32[]{:S(2)}) %collective-permute-start.3) | collective-permute-done | bytes 294944 | tf_op jit(solution)/shard_map/ppermute | solution.py:477
  18.7 4.6 %backward.1 = (f32[256,128]{1,0:T(8,128)S(1)}, f32[256,128]{1,0:T(8,128)}, f32[2,128]{1,0:T(2,128)S(1)}) custom-call(f32[3,192,128]{2,1,0:T(8,128)S(1)} %get-tuple-element.28.own_ref, f32[3,192,128]{2,1,0:T(8,128)S(1)} %collective-permute-done.3.other_ref, bf16[128,384]{1,0:T(8,128)(2,1)S(1)} %get-tuple-element.29.code_ref, ...), custom_call_target="tpu_custom_call" | custom-call | flops 1000000 | bytes 1000000 | tf_op jit(solution)/shard_map/backward/pallas_call | solution.py:479
  23.3 0.2 collective-permute-start.4
  23.5 1.0 %collective-permute-done.4 = f32[2,128]{1,0:T(2,128)S(1)} collective-permute-done((f32[2,128]{1,0:T(2,128)S(1)}, f32[2,128]{1,0:T(2,128)S(1)}, u32[]{:S(2)}, u32[]{:S(2)}) %collective-permute-start.4) | collective-permute-done | bytes 1056 | tf_op jit(solution)/shard_map/ppermute | solution.py:497
  24.5 1.3 %collective-permute-start.5 = (f32[2,128]{1,0:T(2,128)S(1)}, f32[2,128]{1,0:T(2,128)S(1)}, u32[]{:S(2)}, u32[]{:S(2)}) collective-permute-start(f32[2,128]{1,0:T(2,128)S(1)} %add.15), channel_id=1, source_target_pairs={{0,3},{1,2},{2,1},{3,0},{4,7},{5,6},{6,5},{7,4},{8,11},{9,10},{10,... | collective-permute-start | bytes 3080 | tf_op jit(solution)/shard_map/ppermute | solution.py:59
  25.8 1.7 %collective-permute-done.5 = f32[2,128]{1,0:T(2,128)S(1)} collective-permute-done((f32[2,128]{1,0:T(2,128)S(1)}, f32[2,128]{1,0:T(2,128)S(1)}, u32[]{:S(2)}, u32[]{:S(2)}) %collective-permute-start.5) | collective-permute-done | bytes 1056 | tf_op jit(solution)/shard_map/ppermute | solution.py:59
  27.5 3.3 %collective-permute-start.8 = (f32[2,128]{1,0:T(2,128)S(1)}, f32[2,128]{1,0:T(2,128)S(1)}, u32[]{:S(2)}, u32[]{:S(2)}) collective-permute-start(f32[2,128]{1,0:T(2,128)S(1)} %add.16), channel_id=1, source_target_pairs={{0,13},{1,12},{4,9},{5,8},{8,5},{9,4},{12,1},{13,0},{2,15},{3,14},... | collective-permute-start | bytes 3080 | tf_op jit(solution)/shard_map/ppermute | solution.py:54
  30.9 0.6 %collective-permute-start.6 = (f32[2,128]{1,0:T(2,128)S(1)}, f32[2,128]{1,0:T(2,128)S(1)}, u32[]{:S(2)}, u32[]{:S(2)}) collective-permute-start(f32[2,128]{1,0:T(2,128)S(1)} %add.16), channel_id=1, source_target_pairs={{0,9},{1,8},{4,13},{5,12},{8,1},{9,0},{12,5},{13,4},{2,11},{3,10},... | collective-permute-start | bytes 3080 | tf_op jit(solution)/shard_map/ppermute | solution.py:54
  31.4 0.9 %collective-permute-done.8 = f32[2,128]{1,0:T(2,128)S(1)} collective-permute-done((f32[2,128]{1,0:T(2,128)S(1)}, f32[2,128]{1,0:T(2,128)S(1)}, u32[]{:S(2)}, u32[]{:S(2)}) %collective-permute-start.8) | collective-permute-done | bytes 1056 | tf_op jit(solution)/shard_map/ppermute | solution.py:54
  32.3 1.5 %collective-permute-done.7 = f32[2,128]{1,0:T(2,128)S(1)} collective-permute-done((f32[2,128]{1,0:T(2,128)S(1)}, f32[2,128]{1,0:T(2,128)S(1)}, u32[]{:S(2)}, u32[]{:S(2)}) %collective-permute-start.7) | collective-permute-done | bytes 1056 | tf_op jit(solution)/shard_map/ppermute | solution.py:54
  33.9 0.9 %collective-permute-done.6 = f32[2,128]{1,0:T(2,128)S(1)} collective-permute-done((f32[2,128]{1,0:T(2,128)S(1)}, f32[2,128]{1,0:T(2,128)S(1)}, u32[]{:S(2)}, u32[]{:S(2)}) %collective-permute-start.6) | collective-permute-done | bytes 1056 | tf_op jit(solution)/shard_map/ppermute | solution.py:54
  34.8 0.7 %finish.1 = (f32[256,128]{1,0:T(8,128)}, f32[1,128]{1,0:T(1,128)}) custom-call(f32[256,128]{1,0:T(8,128)S(1)} %get-tuple-element.20.params_ref, f32[256,128]{1,0:T(8,128)S(1)} %get-tuple-element.32.gradient_ref, f32[2,128]{1,0:T(2,128)S(1)} %add_add_fusion.sums_ref), custom_call_target="tpu_custom_call" | custom-call | flops 1000000 | bytes 1000000 | tf_op jit(solution)/shard_map/finish/pallas_call | solution.py:501
  (4 shorter events, 0.0 us)
Async XLA Ops:
  1.7 4.9 %collective-permute-start = (bf16[96,128]{1,0:T(8,128)(2,1)S(1)}, bf16[96,128]{1,0:T(8,128)(2,1)S(1)}, u32[]{:S(2)}, u32[]{:S(2)}) collective-permute-start(bf16[96,128]{1,0:T(8,128)(2,1)S(1)} %get-tuple-element.23), channel_id=1, source_target_pairs={{0,4},{4,8},{8,12},{12,28},{28,24},{24,20},{20,16},{16,0},{1,5},{5... | collective-permute-start | bytes 73736 | tf_op jit(solution)/shard_map/ppermute | solution.py:415
  4.8 3.8 %collective-permute-start.1 = (bf16[96,128]{1,0:T(8,128)(2,1)S(1)}, bf16[96,128]{1,0:T(8,128)(2,1)S(1)}, u32[]{:S(2)}, u32[]{:S(2)}) collective-permute-start(bf16[96,128]{1,0:T(8,128)(2,1)S(1)} %get-tuple-element.24), channel_id=1, source_target_pairs={{0,16},{4,0},{8,4},{12,8},{28,12},{24,28},{20,24},{16,20},{1,17},{... | collective-permute-start | bytes 73736 | tf_op jit(solution)/shard_map/ppermute | solution.py:416
  8.7 4.4 %collective-permute-start.2 = (bf16[96,384]{1,0:T(8,128)(2,1)S(1)}, bf16[96,384]{1,0:T(8,128)(2,1)S(1)}, u32[]{:S(2)}, u32[]{:S(2)}) collective-permute-start(bf16[96,384]{1,0:T(8,128)(2,1)S(1)} %get-tuple-element.26), channel_id=1, source_target_pairs={{0,2},{2,0},{1,3},{3,1},{4,6},{6,4},{5,7},{7,5},{8,10},{10,8},{9,1... | collective-permute-start | bytes 221192 | tf_op jit(solution)/shard_map/ppermute | solution.py:440
  17.0 1.6 %collective-permute-start.3 = (f32[3,192,128]{2,1,0:T(8,128)S(1)}, f32[3,192,128]{2,1,0:T(8,128)S(1)}, u32[]{:S(2)}, u32[]{:S(2)}) collective-permute-start(f32[3,192,128]{2,1,0:T(8,128)S(1)} %get-tuple-element.28.own_ref), channel_id=1, source_target_pairs={{0,1},{1,0},{2,3},{3,2},{4,5},{5,4},{6,7},{7,6},{8,9},{9,8},{10,11... | collective-permute-start | bytes 884744 | tf_op jit(solution)/shard_map/ppermute | solution.py:477
  23.3 1.2 %collective-permute-start.4 = (f32[2,128]{1,0:T(2,128)S(1)}, f32[2,128]{1,0:T(2,128)S(1)}, u32[]{:S(2)}, u32[]{:S(2)}) collective-permute-start(f32[2,128]{1,0:T(2,128)S(1)} %get-tuple-element.33), channel_id=1, source_target_pairs={{0,1},{1,0},{2,3},{3,2},{4,5},{5,4},{6,7},{7,6},{8,9},{9,8},{10,11... | collective-permute-start | bytes 3080 | tf_op jit(solution)/shard_map/ppermute | solution.py:497
  24.5 3.0 %collective-permute-start.5 = (f32[2,128]{1,0:T(2,128)S(1)}, f32[2,128]{1,0:T(2,128)S(1)}, u32[]{:S(2)}, u32[]{:S(2)}) collective-permute-start(f32[2,128]{1,0:T(2,128)S(1)} %add.15), channel_id=1, source_target_pairs={{0,3},{1,2},{2,1},{3,0},{4,7},{5,6},{6,5},{7,4},{8,11},{9,10},{10,... | collective-permute-start | bytes 3080 | tf_op jit(solution)/shard_map/ppermute | solution.py:59
  27.5 4.8 %collective-permute-start.8 = (f32[2,128]{1,0:T(2,128)S(1)}, f32[2,128]{1,0:T(2,128)S(1)}, u32[]{:S(2)}, u32[]{:S(2)}) collective-permute-start(f32[2,128]{1,0:T(2,128)S(1)} %add.16), channel_id=1, source_target_pairs={{0,13},{1,12},{4,9},{5,8},{8,5},{9,4},{12,1},{13,0},{2,15},{3,14},... | collective-permute-start | bytes 3080 | tf_op jit(solution)/shard_map/ppermute | solution.py:54
  30.9 3.0 %collective-permute-start.7 = (f32[2,128]{1,0:T(2,128)S(1)}, f32[2,128]{1,0:T(2,128)S(1)}, u32[]{:S(2)}, u32[]{:S(2)}) collective-permute-start(f32[2,128]{1,0:T(2,128)S(1)} %add.16), channel_id=1, source_target_pairs={{0,5},{1,4},{4,1},{5,0},{8,13},{9,12},{12,9},{13,8},{2,7},{3,6},{6... | collective-permute-start | bytes 3080 | tf_op jit(solution)/shard_map/ppermute | solution.py:54
  30.9 3.9 %collective-permute-start.6 = (f32[2,128]{1,0:T(2,128)S(1)}, f32[2,128]{1,0:T(2,128)S(1)}, u32[]{:S(2)}, u32[]{:S(2)}) collective-permute-start(f32[2,128]{1,0:T(2,128)S(1)} %add.16), channel_id=1, source_target_pairs={{0,9},{1,8},{4,13},{5,12},{8,1},{9,0},{12,5},{13,4},{2,11},{3,10},... | collective-permute-start | bytes 3080 | tf_op jit(solution)/shard_map/ppermute | solution.py:54

commit v7 on v6

--- a/solution.py
+++ b/solution.py
@@ -9,7 +9,7 @@
 HALF = 32
 LANES = 128
 BACKWARD_UNROLL = 12
-CHUNK = 4
+CHUNK = 6
 VMEM = 24 * 2**20
 
 mask_slope = 4.0
@@ -49,11 +49,6 @@
     if peers & (peers - 1):
         return lax.psum(value, axis)
     both = (axis, "expo")
-    if peers == 4:
-        one, two, three = (
-            lax.ppermute(value, both, partners(peers, lambda i, d=d: i ^ d)) for d in (1, 2, 3)
-        )
-        return (value + two) + (one + three)
     reach = 1
     while reach < peers:
         value = value + lax.ppermute(value, both, partners(peers, lambda i, r=reach: i ^ r))
@@ -77,12 +72,66 @@
         masks_ref[slot] = jnp.where(keep, one, zero).astype(BF16)
 
 
-def taps_kernel(weights_hbm, col_hbm, row_hbm, out_ref, weights_ref, col_ref, row_ref, flat_ref, sems):
+def mask_of(params):
+    return jax.nn.sigmoid(mask_slope * params).astype(BF16)
+
+
+def code_of(target):
+    return (target + 1).astype(F32).astype(BF16)
+
+
+def edges_kernel(params_hbm, target_hbm, ahead_ref, behind_ref, params_ref, target_ref, sems):
+    rows = params_hbm.shape[0]
+    wide = 2 * HALF
+    copies = [
+        pltpu.make_async_copy(source.at[pl.ds(start, size)], target.at[slot], sems.at[sem, slot])
+        for sem, (source, target, size) in enumerate(
+            ((params_hbm, params_ref, wide), (target_hbm, target_ref, HALF))
+        )
+        for slot, start in enumerate((0, rows - size))
+    ]
+    for copy in copies:
+        copy.start()
+    for copy in copies:
+        copy.wait()
+
+    def fill(refs):
+        for slot, ref in enumerate(refs):
+            ref[0:wide, :] = mask_of(params_ref[slot])
+            ref[wide:, :] = code_of(target_ref[slot])
+
+    pl.when(jnp.logical_not(turned_tile()))(lambda: fill((behind_ref, ahead_ref)))
+    pl.when(turned_tile())(lambda: fill((ahead_ref, behind_ref)))
+
+
+def load_kernel(
+    params_hbm,
+    target_hbm,
+    weights_hbm,
+    col_hbm,
+    row_hbm,
+    params_ref,
+    mask_ref,
+    code_ref,
+    taps_ref,
+    target_ref,
+    weights_ref,
+    col_ref,
+    row_ref,
+    flat_ref,
+    sems,
+):
     kernels, _, taps = col_ref.shape
     copies = [
         pltpu.make_async_copy(source, target, sems.at[slot])
         for slot, (source, target) in enumerate(
-            ((weights_hbm, weights_ref), (col_hbm, col_ref), (row_hbm, row_ref))
+            (
+                (weights_hbm, weights_ref),
+                (col_hbm, col_ref),
+                (row_hbm, row_ref),
+                (params_hbm, params_ref),
+                (target_hbm, target_ref),
+            )
         )
     ]
     for copy in copies:
@@ -96,36 +145,10 @@
         flat_ref[4 * k + 2 : 4 * k + 4] = row_ref[k].astype(F32)
     rows = jnp.dot(flat_ref[...].astype(BF16), pick, preferred_element_type=F32)
     for k in range(kernels):
-        out_ref[k, 0:4] = rows[4 * k : 4 * k + 4]
-        out_ref[k, 4:8] = jnp.full((4, 2 * LANES), weights_ref[k], F32)
-
-
-def prepare_kernel(
-    params_hbm, target_hbm, params_ref, mask_ref, code_ref, ahead_ref, behind_ref, target_ref, sems
-):
-    rows = params_ref.shape[0]
-    wide = 2 * HALF
-    copies = [
-        pltpu.make_async_copy(params_hbm, params_ref, sems.at[0]),
-        pltpu.make_async_copy(target_hbm, target_ref, sems.at[1]),
-    ]
-    for copy in copies:
-        copy.start()
-    for copy in copies:
-        copy.wait()
-    mask = jax.nn.sigmoid(mask_slope * params_ref[...]).astype(BF16)
-    code = (target_ref[...] + 1).astype(F32).astype(BF16)
-    mask_ref[...] = mask
-    code_ref[...] = code
-
-    def edges(down_ref, up_ref):
-        down_ref[0:wide, :] = mask[rows - wide :]
-        down_ref[wide:, :] = code[rows - HALF :]
-        up_ref[0:wide, :] = mask[0:wide]
-        up_ref[wide:, :] = code[0:HALF]
-
-    pl.when(jnp.logical_not(turned_tile()))(lambda: edges(ahead_ref, behind_ref))
-    pl.when(turned_tile())(lambda: edges(behind_ref, ahead_ref))
+        taps_ref[k, 0:4] = rows[4 * k : 4 * k + 4]
+        taps_ref[k, 4:8] = jnp.full((4, 2 * LANES), weights_ref[k], F32)
+    mask_ref[...] = mask_of(params_ref[...])
+    code_ref[...] = code_of(target_ref[...])
 
 
 def unless(end, values):
@@ -145,7 +168,7 @@
 
 
 def assemble_kernel(
-    mask_ref, code_ref, behind_ref, ahead_ref, _, centre_ref, code_out_ref, *side_refs
+    mask_ref, code_ref, behind_ref, ahead_ref, centre_ref, code_out_ref, *side_refs
 ):
     rows, cols = mask_ref.shape
     wide = 2 * HALF
@@ -405,37 +428,43 @@
     plain, edge = array((rows, cols), BF16), array((wide + HALF, cols), BF16)
     full = array((rows, cols), F32)
     sides, strips = lax.axis_size("col"), lax.axis_size("strip")
-    params, mask_half, code, ahead, behind = call(
-        prepare_kernel,
-        "prepare",
+    mine, goal = stay(mask_params[0]), stay(target)
+    ahead, behind = call(
+        edges_kernel,
+        "edges",
         [hbm, hbm],
-        (full, plain, plain, edge, edge),
-        scratch=[pltpu.VMEM((rows, cols), target.dtype), pltpu.SemaphoreType.DMA((2,))],
-    )(stay(mask_params[0]), stay(target))
+        (edge, edge),
+        scratch=[
+            pltpu.VMEM((2, wide, cols), F32),
+            pltpu.VMEM((2, HALF, cols), target.dtype),
+            pltpu.SemaphoreType.DMA((2, 2)),
+        ],
+    )(mine, goal)
     from_behind = lax.ppermute(ahead, ("tiles", "strip"), snake(1))
     from_ahead = lax.ppermute(behind, ("tiles", "strip"), snake(-1))
-    (tap_rows,) = call(
-        taps_kernel,
-        "taps",
-        [hbm] * 3,
-        (array((kernels, 8, 2 * LANES), F32),),
+    params, mask_half, code, tap_rows = call(
+        load_kernel,
+        "load",
+        [hbm] * 5,
+        (full, plain, plain, array((kernels, 8, 2 * LANES), F32)),
         scratch=[
+            pltpu.VMEM((rows, cols), target.dtype),
             pltpu.SMEM(kernel_weights.shape, F32),
             pltpu.VMEM(col_taps.shape, BF16),
             pltpu.VMEM(row_taps.shape, BF16),
             pltpu.VMEM((4 * kernels, taps), F32),
-            pltpu.SemaphoreType.DMA((3,)),
+            pltpu.SemaphoreType.DMA((5,)),
         ],
         flops=10**8,
-    )(stay(kernel_weights), stay(col_taps), stay(row_taps))
+    )(mine, goal, stay(kernel_weights), stay(col_taps), stay(row_taps))
 
     side, turned = array((wide + HALF, long), BF16), array((cols, long), BF16)
     centre, code_turned, *messages = call(
         assemble_kernel,
         "assemble",
-        [vmem] * 4 + [pl.BlockSpec(memory_space=pl.ANY)],
+        [vmem] * 4,
         (turned, turned) + (side,) * (1 if sides == 2 else 2),
-    )(mask_half, code, from_behind, from_ahead, tap_rows)
+    )(mask_half, code, from_behind, from_ahead)
     if sides == 2:
         before = after = lax.ppermute(messages[0], "col", ring("col", 1))
     else:

time: 35.6 us -> 35.1 us (0.986)
  waiting for transfers between devices: 11.2 us -> 10.7 us
    ppermute x3 -> x0, starting transfers between devices: 3.88 us -> none  [total_over(): lax.ppermute(value, both, partners(peers, lambda i, d=d: i ^ d))]
    ppermute x1 -> x3, starting transfers between devices: 1.26 us -> 4.99 us  [total_over(): lax.ppermute(value, both, partners(peers, lambda i, r=reach: i ^ r))]
    ppermute x3 -> x0, waiting for transfers between devices: 3.33 us -> none  [total_over(): lax.ppermute(value, both, partners(peers, lambda i, d=d: i ^ d))]
    ppermute x1 -> x3, waiting for transfers between devices: 1.73 us -> 4.91 us  [total_over(): lax.ppermute(value, both, partners(peers, lambda i, r=reach: i ^ r))]
  transfers between devices with their start and end apart: 9 -> 8, of which waited for: 9 -> 8; matrix products, arithmetic and copies ran while one was open for 0% -> 0% of each run, Pallas kernels for 9% -> 10%
where the time goes in v7:
time: 35.1 us; the launch traced here: 34.9 us
  Pallas kernels  13.6 us (39%)
  waiting for transfers between devices  10.7 us (30%)
  starting transfers between devices  9.93 us (28%)
  between operations  0.69 us (2%)
    ppermute x3, starting transfers between devices, total_over(): lax.ppermute(value, both, partners(peers, lambda i, r=reach: i ^ r))  4.99 us
    ppermute x3, waiting for transfers between devices, total_over(): lax.ppermute(value, both, partners(peers, lambda i, r=reach: i ^ r))  4.91 us
    pallas_call x1, Pallas kernels, shards(): call(backward_kernel, 'backward', [vmem] * 9, (full, full, array((2, LANE...  4.55 us
    pallas_call x1, Pallas kernels, shards(): call(side_kernel, 'side', [vmem] * 5, (fields, array(plane, F32)), scratc...  3.87 us
    ppermute x1, starting transfers between devices, shards(): from_behind = lax.ppermute(ahead, ('tiles', 'strip'), snake(1))  3.1 us
    pallas_call x1, Pallas kernels, shards(): call(middle_kernel, 'middle', [vmem] * 2, (fields, array((tiles, wide, LA...  2.24 us
    ppermute x1, waiting for transfers between devices, shards(): from_ahead = lax.ppermute(behind, ('tiles', 'strip'), snake(-1))  2.08 us
    ppermute x1, waiting for transfers between devices, shards(): other = lax.ppermute(intensity, 'expo', [(0, 1), (1, 0)])  1.57 us
  transfers between devices with their start and end apart: 8, of which 8 were waited for; matrix products, arithmetic and copies ran while one was open for 0% of the time, Pallas kernels for 10%

profile of v7, /device:TPU:0, one launch (start us, length us, event | category | flops | bytes accessed | tf_op | source)
XLA Modules:
  0.0 34.9 jit_solution(18078876113149566946)
XLA Ops:
  0.6 0.8 %edges.1 = (bf16[96,128]{1,0:T(8,128)(2,1)S(1)}, bf16[96,128]{1,0:T(8,128)(2,1)S(1)}) custom-call(f32[256,128]{1,0:T(8,128)} %bitcast.4, s32[256,128]{1,0:T(8,128)} %target_hbm.3), custom_call_target="tpu_custom_call" | custom-call | flops 1000000 | bytes 1000000 | tf_op jit(solution)/shard_map/edges/pallas_call | solution.py:432
  1.5 3.1 %collective-permute-start = (bf16[96,128]{1,0:T(8,128)(2,1)S(1)}, bf16[96,128]{1,0:T(8,128)(2,1)S(1)}, u32[]{:S(2)}, u32[]{:S(2)}) collective-permute-start(bf16[96,128]{1,0:T(8,128)(2,1)S(1)} %get-tuple-element.24), channel_id=1, source_target_pairs={{0,4},{4,8},{8,12},{12,28},{28,24},{24,20},{20,16},{16,0},{1,5},{5... | collective-permute-start | bytes 73736 | tf_op jit(solution)/shard_map/ppermute | solution.py:443
  4.6 0.0 collective-permute-start.1
  4.6 1.2 %load.1 = (f32[256,128]{1,0:T(8,128)S(1)}, bf16[256,128]{1,0:T(8,128)(2,1)S(1)}, bf16[256,128]{1,0:T(8,128)(2,1)S(1)}, f32[24,8,256]{2,1,0:T(8,128)S(1)}) custom-call(f32[256,128]{1,0:T(8,128)} %bitcast.5, s32[256,128]{1,0:T(8,128)} %target_hbm.3, f32[24]{0:T(128)} %weights_hbm.1, bf16[24,2,65]{2,1,0:T(2,128)(2,1)} %col_hbm.1, bf16[24,2,65]{2,1,0:T(2,128)(2,1)} %row_hbm.1), custom_call_target="tpu_custom_call" | custom-call | flops 100000000 | bytes 1000000 | tf_op jit(solution)/shard_map/load/pallas_call | solution.py:445
  5.8 0.5 %collective-permute-done.behind_ref = bf16[96,128]{1,0:T(8,128)(2,1)S(1)} collective-permute-done((bf16[96,128]{1,0:T(8,128)(2,1)S(1)}, bf16[96,128]{1,0:T(8,128)(2,1)S(1)}, u32[]{:S(2)}, u32[]{:S(2)}) %collective-permute-start) | collective-permute-done | bytes 24608 | tf_op jit(solution)/shard_map/ppermute | solution.py:443
  6.3 2.1 %collective-permute-done.1.ahead_ref = bf16[96,128]{1,0:T(8,128)(2,1)S(1)} collective-permute-done((bf16[96,128]{1,0:T(8,128)(2,1)S(1)}, bf16[96,128]{1,0:T(8,128)(2,1)S(1)}, u32[]{:S(2)}, u32[]{:S(2)}) %collective-permute-start.1) | collective-permute-done | bytes 24608 | tf_op jit(solution)/shard_map/ppermute | solution.py:444
  8.4 0.2 assemble.1
  8.6 1.6 %collective-permute-start.2 = (bf16[96,384]{1,0:T(8,128)(2,1)S(1)}, bf16[96,384]{1,0:T(8,128)(2,1)S(1)}, u32[]{:S(2)}, u32[]{:S(2)}) collective-permute-start(bf16[96,384]{1,0:T(8,128)(2,1)S(1)} %get-tuple-element.27), channel_id=1, source_target_pairs={{0,2},{2,0},{1,3},{3,1},{4,6},{6,4},{5,7},{7,5},{8,10},{10,8},{9,1... | collective-permute-start | bytes 221192 | tf_op jit(solution)/shard_map/ppermute | solution.py:469
  10.1 2.2 %middle.1 = (bf16[24,3,64,256]{3,2,1,0:T(8,128)(2,1)S(1)}, f32[3,64,128]{2,1,0:T(8,128)S(1)}) custom-call(bf16[128,384]{1,0:T(8,128)(2,1)S(1)} %get-tuple-element.26.centre_ref, f32[24,8,256]{2,1,0:T(8,128)S(1)} %get-tuple-element.28.taps_ref), custom_call_target="tpu_custom_call" | custom-call | flops 4000000000 | bytes 1000000 | tf_op jit(solution)/shard_map/middle/pallas_call | solution.py:486
  12.4 0.6 %collective-permute-done.2.before_ref.after_ref.code_before_ref.code_after_ref = bf16[96,384]{1,0:T(8,128)(2,1)S(1)} collective-permute-done((bf16[96,384]{1,0:T(8,128)(2,1)S(1)}, bf16[96,384]{1,0:T(8,128)(2,1)S(1)}, u32[]{:S(2)}, u32[]{:S(2)}) %collective-permute-start.2) | collective-permute-done | bytes 73760 | tf_op jit(solution)/shard_map/ppermute | solution.py:469
  13.0 3.9 %side.1 = (bf16[24,3,128,256]{3,2,1,0:T(8,128)(2,1)S(1)}, f32[3,192,128]{2,1,0:T(8,128)S(1)}) custom-call(bf16[128,384]{1,0:T(8,128)(2,1)S(1)} %get-tuple-element.26.centre_ref, bf16[96,384]{1,0:T(8,128)(2,1)S(1)} %collective-permute-done.2.before_ref.after_ref.code_before_ref.code_after_ref, ...), custom_call_target="tpu_custom_call" | custom-call | flops 1000000 | bytes 1000000 | tf_op jit(solution)/shard_map/side/pallas_call | solution.py:497
  16.9 0.1 collective-permute-start.3
  16.9 1.6 %collective-permute-done.3.other_ref = f32[3,192,128]{2,1,0:T(8,128)S(1)} collective-permute-done((f32[3,192,128]{2,1,0:T(8,128)S(1)}, f32[3,192,128]{2,1,0:T(8,128)S(1)}, u32[]{:S(2)}, u32[]{:S(2)}) %collective-permute-start.3) | collective-permute-done | bytes 294944 | tf_op jit(solution)/shard_map/ppermute | solution.py:506
  18.5 4.5 %backward.1 = (f32[256,128]{1,0:T(8,128)S(1)}, f32[256,128]{1,0:T(8,128)}, f32[2,128]{1,0:T(2,128)S(1)}) custom-call(f32[3,192,128]{2,1,0:T(8,128)S(1)} %get-tuple-element.30.own_ref, f32[3,192,128]{2,1,0:T(8,128)S(1)} %collective-permute-done.3.other_ref, bf16[128,384]{1,0:T(8,128)(2,1)S(1)} %get-tuple-element.31.code_ref, ...), custom_call_target="tpu_custom_call" | custom-call | flops 1000000 | bytes 1000000 | tf_op jit(solution)/shard_map/backward/pallas_call | solution.py:508
  23.1 0.2 collective-permute-start.4
  23.3 1.0 %collective-permute-done.4 = f32[2,128]{1,0:T(2,128)S(1)} collective-permute-done((f32[2,128]{1,0:T(2,128)S(1)}, f32[2,128]{1,0:T(2,128)S(1)}, u32[]{:S(2)}, u32[]{:S(2)}) %collective-permute-start.4) | collective-permute-done | bytes 1056 | tf_op jit(solution)/shard_map/ppermute | solution.py:526
  24.3 1.2 %collective-permute-start.5 = (f32[2,128]{1,0:T(2,128)S(1)}, f32[2,128]{1,0:T(2,128)S(1)}, u32[]{:S(2)}, u32[]{:S(2)}) collective-permute-start(f32[2,128]{1,0:T(2,128)S(1)} %add.12), channel_id=1, source_target_pairs={{0,3},{1,2},{2,1},{3,0},{4,7},{5,6},{6,5},{7,4},{8,11},{9,10},{10,... | collective-permute-start | bytes 3080 | tf_op jit(solution)/shard_map/ppermute | solution.py:54
  25.5 1.7 %collective-permute-done.5 = f32[2,128]{1,0:T(2,128)S(1)} collective-permute-done((f32[2,128]{1,0:T(2,128)S(1)}, f32[2,128]{1,0:T(2,128)S(1)}, u32[]{:S(2)}, u32[]{:S(2)}) %collective-permute-start.5) | collective-permute-done | bytes 1056 | tf_op jit(solution)/shard_map/ppermute | solution.py:54
  27.3 1.4 %collective-permute-start.6 = (f32[2,128]{1,0:T(2,128)S(1)}, f32[2,128]{1,0:T(2,128)S(1)}, u32[]{:S(2)}, u32[]{:S(2)}) collective-permute-start(f32[2,128]{1,0:T(2,128)S(1)} %add.13), channel_id=1, source_target_pairs={{0,5},{1,4},{4,1},{5,0},{8,13},{9,12},{12,9},{13,8},{2,7},{3,6},{6... | collective-permute-start | bytes 3080 | tf_op jit(solution)/shard_map/ppermute | solution.py:54
  28.6 1.6 %collective-permute-done.6 = f32[2,128]{1,0:T(2,128)S(1)} collective-permute-done((f32[2,128]{1,0:T(2,128)S(1)}, f32[2,128]{1,0:T(2,128)S(1)}, u32[]{:S(2)}, u32[]{:S(2)}) %collective-permute-start.6) | collective-permute-done | bytes 1056 | tf_op jit(solution)/shard_map/ppermute | solution.py:54
  30.3 2.4 %collective-permute-start.7 = (f32[2,128]{1,0:T(2,128)S(1)}, f32[2,128]{1,0:T(2,128)S(1)}, u32[]{:S(2)}, u32[]{:S(2)}) collective-permute-start(f32[2,128]{1,0:T(2,128)S(1)} %add.14), channel_id=1, source_target_pairs={{0,9},{1,8},{4,13},{5,12},{8,1},{9,0},{12,5},{13,4},{2,11},{3,10},... | collective-permute-start | bytes 3080 | tf_op jit(solution)/shard_map/ppermute | solution.py:54
  32.7 1.5 %collective-permute-done.7 = f32[2,128]{1,0:T(2,128)S(1)} collective-permute-done((f32[2,128]{1,0:T(2,128)S(1)}, f32[2,128]{1,0:T(2,128)S(1)}, u32[]{:S(2)}, u32[]{:S(2)}) %collective-permute-start.7) | collective-permute-done | bytes 1056 | tf_op jit(solution)/shard_map/ppermute | solution.py:54
  34.2 0.7 %finish.1 = (f32[256,128]{1,0:T(8,128)}, f32[1,128]{1,0:T(1,128)}) custom-call(f32[256,128]{1,0:T(8,128)S(1)} %get-tuple-element.21.params_ref, f32[256,128]{1,0:T(8,128)S(1)} %get-tuple-element.34.gradient_ref, f32[2,128]{1,0:T(2,128)S(1)} %add.15.sums_ref), custom_call_target="tpu_custom_call" | custom-call | flops 1000000 | bytes 1000000 | tf_op jit(solution)/shard_map/finish/pallas_call | solution.py:530
  (4 shorter events, 0.0 us)
Async XLA Ops:
  1.5 4.9 %collective-permute-start = (bf16[96,128]{1,0:T(8,128)(2,1)S(1)}, bf16[96,128]{1,0:T(8,128)(2,1)S(1)}, u32[]{:S(2)}, u32[]{:S(2)}) collective-permute-start(bf16[96,128]{1,0:T(8,128)(2,1)S(1)} %get-tuple-element.24), channel_id=1, source_target_pairs={{0,4},{4,8},{8,12},{12,28},{28,24},{24,20},{20,16},{16,0},{1,5},{5... | collective-permute-start | bytes 73736 | tf_op jit(solution)/shard_map/ppermute | solution.py:443
  4.6 3.8 %collective-permute-start.1 = (bf16[96,128]{1,0:T(8,128)(2,1)S(1)}, bf16[96,128]{1,0:T(8,128)(2,1)S(1)}, u32[]{:S(2)}, u32[]{:S(2)}) collective-permute-start(bf16[96,128]{1,0:T(8,128)(2,1)S(1)} %get-tuple-element.25), channel_id=1, source_target_pairs={{0,16},{4,0},{8,4},{12,8},{28,12},{24,28},{20,24},{16,20},{1,17},{... | collective-permute-start | bytes 73736 | tf_op jit(solution)/shard_map/ppermute | solution.py:444
  8.6 4.4 %collective-permute-start.2 = (bf16[96,384]{1,0:T(8,128)(2,1)S(1)}, bf16[96,384]{1,0:T(8,128)(2,1)S(1)}, u32[]{:S(2)}, u32[]{:S(2)}) collective-permute-start(bf16[96,384]{1,0:T(8,128)(2,1)S(1)} %get-tuple-element.27), channel_id=1, source_target_pairs={{0,2},{2,0},{1,3},{3,1},{4,6},{6,4},{5,7},{7,5},{8,10},{10,8},{9,1... | collective-permute-start | bytes 221192 | tf_op jit(solution)/shard_map/ppermute | solution.py:469
  16.9 1.6 %collective-permute-start.3 = (f32[3,192,128]{2,1,0:T(8,128)S(1)}, f32[3,192,128]{2,1,0:T(8,128)S(1)}, u32[]{:S(2)}, u32[]{:S(2)}) collective-permute-start(f32[3,192,128]{2,1,0:T(8,128)S(1)} %get-tuple-element.30.own_ref), channel_id=1, source_target_pairs={{0,1},{1,0},{2,3},{3,2},{4,5},{5,4},{6,7},{7,6},{8,9},{9,8},{10,11... | collective-permute-start | bytes 884744 | tf_op jit(solution)/shard_map/ppermute | solution.py:506
  23.1 1.2 %collective-permute-start.4 = (f32[2,128]{1,0:T(2,128)S(1)}, f32[2,128]{1,0:T(2,128)S(1)}, u32[]{:S(2)}, u32[]{:S(2)}) collective-permute-start(f32[2,128]{1,0:T(2,128)S(1)} %get-tuple-element.35), channel_id=1, source_target_pairs={{0,1},{1,0},{2,3},{3,2},{4,5},{5,4},{6,7},{7,6},{8,9},{9,8},{10,11... | collective-permute-start | bytes 3080 | tf_op jit(solution)/shard_map/ppermute | solution.py:526
  24.3 3.0 %collective-permute-start.5 = (f32[2,128]{1,0:T(2,128)S(1)}, f32[2,128]{1,0:T(2,128)S(1)}, u32[]{:S(2)}, u32[]{:S(2)}) collective-permute-start(f32[2,128]{1,0:T(2,128)S(1)} %add.12), channel_id=1, source_target_pairs={{0,3},{1,2},{2,1},{3,0},{4,7},{5,6},{6,5},{7,4},{8,11},{9,10},{10,... | collective-permute-start | bytes 3080 | tf_op jit(solution)/shard_map/ppermute | solution.py:54
  27.3 3.0 %collective-permute-start.6 = (f32[2,128]{1,0:T(2,128)S(1)}, f32[2,128]{1,0:T(2,128)S(1)}, u32[]{:S(2)}, u32[]{:S(2)}) collective-permute-start(f32[2,128]{1,0:T(2,128)S(1)} %add.13), channel_id=1, source_target_pairs={{0,5},{1,4},{4,1},{5,0},{8,13},{9,12},{12,9},{13,8},{2,7},{3,6},{6... | collective-permute-start | bytes 3080 | tf_op jit(solution)/shard_map/ppermute | solution.py:54
  30.3 3.9 %collective-permute-start.7 = (f32[2,128]{1,0:T(2,128)S(1)}, f32[2,128]{1,0:T(2,128)S(1)}, u32[]{:S(2)}, u32[]{:S(2)}) collective-permute-start(f32[2,128]{1,0:T(2,128)S(1)} %add.14), channel_id=1, source_target_pairs={{0,9},{1,8},{4,13},{5,12},{8,1},{9,0},{12,5},{13,4},{2,11},{3,10},... | collective-permute-start | bytes 3080 | tf_op jit(solution)/shard_map/ppermute | solution.py:54

commit v8 on v7

--- a/solution.py
+++ b/solution.py
@@ -114,11 +114,14 @@
     mask_ref,
     code_ref,
     taps_ref,
+    near_ref,
+    row_table_ref,
     target_ref,
     weights_ref,
     col_ref,
     row_ref,
     flat_ref,
+    masks_ref,
     sems,
 ):
     kernels, _, taps = col_ref.shape
@@ -149,6 +152,21 @@
         taps_ref[k, 4:8] = jnp.full((4, 2 * LANES), weights_ref[k], F32)
     mask_ref[...] = mask_of(params_ref[...])
     code_ref[...] = code_of(target_ref[...])
+    write_masks(masks_ref)
+    wide = taps - 1
+    for k in range(kernels):
+        for part in range(2):
+            at = (2 * k + part) * wide
+            base = circulant(taps_ref[k, part : part + 1, 0:LANES], 0)[0:wide]
+            near_ref[at : at + wide, :] = base * masks_ref[0, 0:wide]
+        for half in range(2):
+            zero, one = (
+                circulant(taps_ref[k, 2 + part : 3 + part, LANES:], LANES // 2) * masks_ref[2 + half]
+                for part in range(2)
+            )
+            at = half * 2 * LANES
+            row_table_ref[k, at : at + LANES] = jnp.concatenate([zero, one], axis=1)
+            row_table_ref[k, at + LANES : at + 2 * LANES] = jnp.concatenate([-one, zero], axis=1)
 
 
 def unless(end, values):
@@ -201,19 +219,14 @@
         pl.when(at_end("col"))(lambda: left(side_refs[0]))
 
 
-def correlate(taps_ref, source_ref, field_ref, total_ref, masks_ref, table_ref, columns_ref):
+def correlate(tables, source_ref, field_ref, total_ref, columns_ref):
+    taps_ref, near_ref, row_table_ref = tables
     kernels = taps_ref.shape[0]
     tiles, span = field_ref.shape[1:3]
     wide = 2 * HALF
     long = tiles * LANES
     total_ref[...] = jnp.zeros_like(total_ref)
-    write_masks(masks_ref)
-    for kernel in range(kernels):
-        for part in range(2):
-            base = circulant(taps_ref[kernel, part : part + 1, 0:LANES], 0)[0:wide]
-            at = (kernel * 2 + part) * wide
-            table_ref[at : at + wide, :] = base * masks_ref[0, 0:wide]
-    columns = jnp.dot(table_ref[...], source_ref[...], preferred_element_type=F32).astype(BF16)
+    columns = jnp.dot(near_ref[...], source_ref[...], preferred_element_type=F32).astype(BF16)
     for kernel in range(kernels):
         for part in range(2):
             at = (kernel * 2 + part) * wide
@@ -226,23 +239,12 @@
                     ]
     edge = (tiles - 1) * span
     for kernel in range(kernels):
-        near, far = [], []
-        for part in range(2):
-            base = circulant(taps_ref[kernel, 2 + part : 3 + part, LANES:], LANES // 2)
-            near.append(base * masks_ref[2])
-            far.append(base * masks_ref[3])
-        near = [
-            jnp.concatenate([near[0], near[1]], axis=1),
-            jnp.concatenate([-near[1], near[0]], axis=1),
-        ]
-        far = [
-            jnp.concatenate([far[0], far[1]], axis=1),
-            jnp.concatenate([-far[1], far[0]], axis=1),
-        ]
         weight = taps_ref[kernel, 4:5, :]
         window = jnp.concatenate([columns_ref[kernel, 0:edge], columns_ref[kernel, span:]], axis=1)
-        inner = jnp.dot(window, jnp.concatenate(near + far, axis=0), preferred_element_type=F32)
-        outer = jnp.dot(columns_ref[kernel, edge:], jnp.concatenate(near, axis=0), preferred_element_type=F32)
+        inner = jnp.dot(window, row_table_ref[kernel], preferred_element_type=F32)
+        outer = jnp.dot(
+            columns_ref[kernel, edge:], row_table_ref[kernel, 0 : 2 * LANES], preferred_element_type=F32
+        )
         for t in range(tiles):
             part = inner[t * span : (t + 1) * span] if t + 1 < tiles else outer
             scaled = weight * part
@@ -250,14 +252,55 @@
             total_ref[t] += scaled * part
 
 
-def middle_kernel(centre_ref, taps_ref, field_ref, intensity_ref, total_ref, *scratch):
-    correlate(taps_ref, centre_ref, field_ref, total_ref, *scratch)
+def back_tables_kernel(taps_ref, _, row_table_ref, col_table_ref, masks_ref):
+    kernels = taps_ref.shape[0]
+    wide = 2 * HALF
+    each = 3 * LANES
+    write_masks(masks_ref)
+    a, b = index_pair((LANES, LANES))
+    inside = jnp.where(b < wide, b, b - wide) < a
+    for kernel in range(kernels):
+        for half in range(2):
+            zero, one = (
+                circulant(taps_ref[kernel, 2 + part : 3 + part, 0:LANES], LANES // 2) * masks_ref[2 + half]
+                for part in range(2)
+            )
+            at = half * 2 * LANES
+            row_table_ref[kernel, at : at + LANES] = jnp.concatenate([zero, -one], axis=1)
+            row_table_ref[kernel, at + LANES : at + 2 * LANES] = jnp.concatenate([one, zero], axis=1)
+        turned = []
+        group, at = kernel // CHUNK, kernel % CHUNK * each
+        for part in range(2):
+            row = taps_ref[kernel, part : part + 1, LANES:]
+            to = slice(at + part * LANES, at + (part + 1) * LANES)
+            col_table_ref[group, :, to] = circulant(row, 0) * masks_ref[0]
+            spread = jnp.broadcast_to(row, (LANES, LANES))
+            turned.append(pltpu.roll(spread, part * wide, 1, stride=1, stride_axis=0))
+        both = jnp.where(b < wide, turned[0], turned[1])
+        col_table_ref[group, :, at + 2 * LANES : at + each] = jnp.where(inside, both, 0.0).astype(BF16)
+
+
+def middle_kernel(
+    centre_ref, taps_ref, near_ref, row_table_ref, field_ref, intensity_ref, total_ref, columns_ref
+):
+    correlate((taps_ref, near_ref, row_table_ref), centre_ref, field_ref, total_ref, columns_ref)
     for t in range(total_ref.shape[0]):
         intensity_ref[t] = total_ref[t, :, 0:LANES] + total_ref[t, :, LANES:]
 
 
 def side_kernel(
-    centre_ref, before_ref, after_ref, taps_ref, middle_ref, field_ref, intensity_ref, total_ref, source_ref, *scratch
+    centre_ref,
+    before_ref,
+    after_ref,
+    middle_ref,
+    taps_ref,
+    near_ref,
+    row_table_ref,
+    field_ref,
+    intensity_ref,
+    total_ref,
+    source_ref,
+    columns_ref,
 ):
     wide = 2 * HALF
     cols, long = centre_ref.shape
@@ -265,7 +308,7 @@
     source_ref[wide:, 0:long] = centre_ref[0:wide, :]
     source_ref[0:wide, long:] = centre_ref[cols - wide :, :]
     source_ref[wide:, long:] = unless(at_end("col"), after_ref[0:wide, :]).astype(BF16)
-    correlate(taps_ref, source_ref, field_ref, total_ref, *scratch)
+    correlate((taps_ref, near_ref, row_table_ref), source_ref, field_ref, total_ref, columns_ref)
     for t in range(total_ref.shape[0]):
         intensity = total_ref[t, :, 0:LANES] + total_ref[t, :, LANES:]
         intensity_ref[t, 0:wide] = intensity[0:wide]
@@ -282,25 +325,24 @@
     params_ref,
     middle_ref,
     side_ref,
-    taps_ref,
+    row_table_ref,
+    col_table_ref,
     gradient_ref,
     resist_hbm,
     sums_ref,
     slope_ref,
     descent_ref,
     resist_ref,
-    masks_ref,
-    table_ref,
     source_ref,
     sem,
 ):
-    kernels = taps_ref.shape[0]
+    kernels = row_table_ref.shape[0]
     cols = code_ref.shape[0]
     wide = 2 * HALF
     tiles = own_ref.shape[0]
     span = cols + wide
     rows = (tiles - 1) * LANES
-    units = table_ref.shape[1] // (2 * span)
+    units = source_ref.shape[0] // (2 * span)
 
     resists, loss = [], 0.0
     for t in range(tiles):
@@ -329,27 +371,10 @@
     copy = pltpu.make_async_copy(resist_ref, resist_hbm, sem)
     copy.start()
     descent_ref[...] = jnp.zeros_like(descent_ref)
-    write_masks(masks_ref)
 
     def group(step, carry):
-        a, b = index_pair((LANES, LANES))
-        inside = jnp.where(b < wide, b, b - wide) < a
         for unit in range(units):
             kernel = step * units + unit
-            near, far = [], []
-            for part in range(2):
-                base = circulant(taps_ref[kernel, 2 + part : 3 + part, 0:LANES], LANES // 2)
-                near.append(base * masks_ref[2])
-                far.append(base * masks_ref[3])
-            table = jnp.concatenate(
-                [
-                    jnp.concatenate([near[0], -near[1]], axis=1),
-                    jnp.concatenate([near[1], near[0]], axis=1),
-                    jnp.concatenate([far[0], -far[1]], axis=1),
-                    jnp.concatenate([far[1], far[0]], axis=1),
-                ],
-                axis=0,
-            )
             products = [
                 slope_ref[t]
                 * jnp.concatenate(
@@ -360,7 +385,7 @@
             window = jnp.concatenate(
                 [jnp.concatenate(products[:-1], axis=0), jnp.concatenate(products[1:], axis=0)], axis=1
             )
-            returned = jnp.dot(window, table, preferred_element_type=F32).astype(BF16)
+            returned = jnp.dot(window, row_table_ref[kernel], preferred_element_type=F32).astype(BF16)
             at = unit * 2 * span
             for t in range(tiles - 1):
                 to = slice(t * LANES, (t + 1) * LANES)
@@ -369,18 +394,10 @@
                     source_ref[at + part * cols : at + (part + 1) * cols, to] = piece[0:cols]
                     tail = at + 2 * cols + part * wide
                     source_ref[tail : tail + wide, to] = piece[cols:]
-            turned = []
-            for part in range(2):
-                row = taps_ref[kernel, part : part + 1, LANES:]
-                table_ref[:, at + part * LANES : at + (part + 1) * LANES] = circulant(row, 0) * masks_ref[0]
-                spread = jnp.broadcast_to(row, (LANES, LANES))
-                turned.append(pltpu.roll(spread, part * wide, 1, stride=1, stride_axis=0))
-            both = jnp.where(b < wide, turned[0], turned[1])
-            table_ref[:, at + 2 * LANES : at + 3 * LANES] = jnp.where(inside, both, 0.0).astype(BF16)
             if unit % CHUNK == CHUNK - 1:
                 chunk = slice((unit + 1 - CHUNK) * 2 * span, (unit + 1) * 2 * span)
                 descent_ref[...] += jnp.dot(
-                    table_ref[:, chunk], source_ref[chunk, :], preferred_element_type=F32
+                    col_table_ref[step * (units // CHUNK) + unit // CHUNK], source_ref[chunk, :], preferred_element_type=F32
                 )
         return carry
 
@@ -442,17 +459,20 @@
     )(mine, goal)
     from_behind = lax.ppermute(ahead, ("tiles", "strip"), snake(1))
     from_ahead = lax.ppermute(behind, ("tiles", "strip"), snake(-1))
-    params, mask_half, code, tap_rows = call(
+    masks = pltpu.VMEM((4, LANES, LANES), BF16)
+    row_tables = array((kernels, 4 * LANES, 2 * LANES), BF16)
+    params, mask_half, code, *tables = call(
         load_kernel,
         "load",
         [hbm] * 5,
-        (full, plain, plain, array((kernels, 8, 2 * LANES), F32)),
+        (full, plain, plain, array((kernels, 8, 2 * LANES), F32), array((kernels * 2 * wide, LANES), BF16), row_tables),
         scratch=[
             pltpu.VMEM((rows, cols), target.dtype),
             pltpu.SMEM(kernel_weights.shape, F32),
             pltpu.VMEM(col_taps.shape, BF16),
             pltpu.VMEM(row_taps.shape, BF16),
             pltpu.VMEM((4 * kernels, taps), F32),
+            masks,
             pltpu.SemaphoreType.DMA((5,)),
         ],
         flops=10**8,
@@ -471,57 +491,57 @@
         before = lax.ppermute(messages[0], "col", ring("col", 1))
         after = lax.ppermute(messages[1], "col", ring("col", -1))
 
-    masks = pltpu.VMEM((4, LANES, LANES), BF16)
-
     def part(width):
         fields = array((kernels, tiles, width, 2 * LANES), BF16)
-        scratch = [
-            masks,
-            pltpu.VMEM((kernels * 2 * wide, LANES), BF16),
-            pltpu.VMEM((kernels, tiles * width, 2 * LANES), BF16),
-        ]
-        return fields, pltpu.VMEM((tiles, width, 2 * LANES), F32), scratch
-
-    fields, total, scratch = part(wide)
+        columns = pltpu.VMEM((kernels, tiles * width, 2 * LANES), BF16)
+        return fields, pltpu.VMEM((tiles, width, 2 * LANES), F32), columns
+
+    fields, total, columns = part(wide)
     middle, middle_intensity = call(
         middle_kernel,
         "middle",
-        [vmem] * 2,
+        [vmem] * 4,
         (fields, array((tiles, wide, LANES), F32)),
-        scratch=[total] + scratch,
+        scratch=[total, columns],
         grant=VMEM,
         flops=4 * 10**9,
-    )(centre, tap_rows)
+    )(centre, *tables)
     plane = (tiles, span, LANES)
-    fields, total, scratch = part(2 * wide)
+    fields, total, columns = part(2 * wide)
     sides_field, intensity = call(
         side_kernel,
         "side",
-        [vmem] * 5,
+        [vmem] * 7,
         (fields, array(plane, F32)),
-        scratch=[total, pltpu.VMEM((LANES, 2 * long), BF16)] + scratch,
+        scratch=[total, pltpu.VMEM((LANES, 2 * long), BF16), columns],
         grant=VMEM,
-    )(centre, before, after, tap_rows, middle_intensity)
+    )(centre, before, after, middle_intensity, *tables)
 
     other = lax.ppermute(intensity, "expo", [(0, 1), (1, 0)])
+    back_tables = call(
+        back_tables_kernel,
+        "back_tables",
+        [vmem, pl.BlockSpec(memory_space=pl.ANY)],
+        (row_tables, array((kernels // CHUNK, cols, CHUNK * 2 * span), BF16)),
+        scratch=[masks],
+        flops=10**9,
+    )(tables[0], intensity)
 
     gradient, resist, sums = call(
         backward_kernel,
         "backward",
-        [vmem] * 9,
+        [vmem] * 10,
         (full, full, array((2, LANES), F32)),
         out_specs=[vmem, hbm, vmem],
         scratch=[
             pltpu.VMEM((tiles, span, 2 * LANES), BF16),
             pltpu.VMEM((cols, rows), F32),
             pltpu.VMEM((rows, cols), F32),
-            masks,
-            pltpu.VMEM((cols, back_units * 2 * span), BF16),
             pltpu.VMEM((back_units * 2 * span, rows), BF16),
             pltpu.SemaphoreType.DMA,
         ],
         grant=VMEM,
-    )(intensity, other, code_turned, before, after, params, middle, sides_field, tap_rows)
+    )(intensity, other, code_turned, before, after, params, middle, sides_field, *back_tables)
 
     sums = sums + lax.ppermute(sums, "expo", [(0, 1), (1, 0)])
     for axis in ("col", "strip"):

time: 35.1 us -> 34.9 us (level)
  waiting for transfers between devices: 10.7 us -> 8 us
  Pallas kernels: 13.6 us -> 15.7 us
  starting transfers between devices: 9.93 us -> 10.3 us
    ppermute x1, waiting for transfers between devices: 1.57 us -> 0.27 us  [shards(): other = lax.ppermute(intensity, 'expo', [(0, 1), (1, 0)])]
    pallas_call x1, Pallas kernels: 1.23 us -> 2.33 us  [shards(): call(load_kernel, 'load', [hbm] * 5, (full, plain, plain, array((kernels,...]
    pallas_call x3 -> x4, Pallas kernels: 10.7 us -> 11.7 us  [the longest x1 4.38 us: shards(): call(backward_kernel, 'backward', [vmem] * 10, (full, full, array((2, LAN...]
    ppermute x1, waiting for transfers between devices: 2.08 us -> 1.47 us  [shards(): from_ahead = lax.ppermute(behind, ('tiles', 'strip'), snake(-1))]
    ppermute x1, waiting for transfers between devices: 0.51 us -> 0.01 us  [shards(): from_behind = lax.ppermute(ahead, ('tiles', 'strip'), snake(1))]
  transfers between devices with their start and end apart: 8 -> 8, of which waited for: 8 -> 7; matrix products, arithmetic and copies ran while one was open for 0% -> 0% of each run, Pallas kernels for 10% -> 17%
where the time goes in v8:
time: 34.9 us; the launch traced here: 34.7 us
  Pallas kernels  15.7 us (45%)
  starting transfers between devices  10.3 us (30%)
  waiting for transfers between devices  8 us (23%)
  between operations  0.71 us (2%)
    ppermute x3, starting transfers between devices, total_over(): lax.ppermute(value, both, partners(peers, lambda i, r=reach: i ^ r))  5.21 us
    ppermute x3, waiting for transfers between devices, total_over(): lax.ppermute(value, both, partners(peers, lambda i, r=reach: i ^ r))  4.69 us
    pallas_call x1, Pallas kernels, shards(): call(backward_kernel, 'backward', [vmem] * 10, (full, full, array((2, LAN...  4.38 us
    pallas_call x1, Pallas kernels, shards(): call(side_kernel, 'side', [vmem] * 7, (fields, array(plane, F32)), scratc...  3.79 us
    ppermute x1, starting transfers between devices, shards(): from_behind = lax.ppermute(ahead, ('tiles', 'strip'), snake(1))  3.1 us
    pallas_call x1, Pallas kernels, shards(): call(load_kernel, 'load', [hbm] * 5, (full, plain, plain, array((kernels,...  2.33 us
    pallas_call x1, Pallas kernels, shards(): call(middle_kernel, 'middle', [vmem] * 4, (fields, array((tiles, wide, LA...  2.21 us
    ppermute x1, starting transfers between devices, shards(): before = after = lax.ppermute(messages[0], 'col', ring('col', 1))  1.56 us
  transfers between devices with their start and end apart: 8, of which 7 were waited for; matrix products, arithmetic and copies ran while one was open for 0% of the time, Pallas kernels for 17%

profile of v8, /device:TPU:0, one launch (start us, length us, event | category | flops | bytes accessed | tf_op | source)
XLA Modules:
  0.0 34.7 jit_solution(742243066307468441)
XLA Ops:
  0.6 0.8 %edges.1 = (bf16[96,128]{1,0:T(8,128)(2,1)S(1)}, bf16[96,128]{1,0:T(8,128)(2,1)S(1)}) custom-call(f32[256,128]{1,0:T(8,128)} %bitcast.4, s32[256,128]{1,0:T(8,128)} %target_hbm.3), custom_call_target="tpu_custom_call" | custom-call | flops 1000000 | bytes 1000000 | tf_op jit(solution)/shard_map/edges/pallas_call | solution.py:449
  1.5 3.1 %collective-permute-start = (bf16[96,128]{1,0:T(8,128)(2,1)S(1)}, bf16[96,128]{1,0:T(8,128)(2,1)S(1)}, u32[]{:S(2)}, u32[]{:S(2)}) collective-permute-start(bf16[96,128]{1,0:T(8,128)(2,1)S(1)} %get-tuple-element.28), channel_id=1, source_target_pairs={{0,4},{4,8},{8,12},{12,28},{28,24},{24,20},{20,16},{16,0},{1,5},{5... | collective-permute-start | bytes 73736 | tf_op jit(solution)/shard_map/ppermute | solution.py:460
  4.6 0.0 collective-permute-start.1
  4.6 2.3 %load.1 = (f32[256,128]{1,0:T(8,128)S(1)}, bf16[256,128]{1,0:T(8,128)(2,1)S(1)}, bf16[256,128]{1,0:T(8,128)(2,1)S(1)}, f32[24,8,256]{2,1,0:T(8,128)S(1)}, bf16[3...) custom-call(f32[256,128]{1,0:T(8,128)} %bitcast.5, s32[256,128]{1,0:T(8,128)} %target_hbm.3, f32[24]{0:T(128)} %weights_hbm.1, ...), custom_call_target="tpu_custom_call" | custom-call | flops 100000000 | bytes 1000000 | tf_op jit(solution)/shard_map/load/pallas_call | solution.py:464
  6.9 0.0 collective-permute-done.behind_ref
  6.9 1.5 %collective-permute-done.1.ahead_ref = bf16[96,128]{1,0:T(8,128)(2,1)S(1)} collective-permute-done((bf16[96,128]{1,0:T(8,128)(2,1)S(1)}, bf16[96,128]{1,0:T(8,128)(2,1)S(1)}, u32[]{:S(2)}, u32[]{:S(2)}) %collective-permute-start.1) | collective-permute-done | bytes 24608 | tf_op jit(solution)/shard_map/ppermute | solution.py:461
  8.4 0.2 assemble.1
  8.6 1.6 %collective-permute-start.2 = (bf16[96,384]{1,0:T(8,128)(2,1)S(1)}, bf16[96,384]{1,0:T(8,128)(2,1)S(1)}, u32[]{:S(2)}, u32[]{:S(2)}) collective-permute-start(bf16[96,384]{1,0:T(8,128)(2,1)S(1)} %get-tuple-element.31), channel_id=1, source_target_pairs={{0,2},{2,0},{1,3},{3,1},{4,6},{6,4},{5,7},{7,5},{8,10},{10,8},{9,1... | collective-permute-start | bytes 221192 | tf_op jit(solution)/shard_map/ppermute | solution.py:489
  10.1 2.2 %middle.1 = (bf16[24,3,64,256]{3,2,1,0:T(8,128)(2,1)S(1)}, f32[3,64,128]{2,1,0:T(8,128)S(1)}) custom-call(bf16[128,384]{1,0:T(8,128)(2,1)S(1)} %get-tuple-element.30.centre_ref, f32[24,8,256]{2,1,0:T(8,128)S(1)} %get-tuple-element.32.taps_ref, bf16[3072,128]{1,0:T(8,128)(2,1)S(1)} %get-tuple-element.33.near_ref, ...), custom_call_target="tpu_custom_call" | custom-call | flops 4000000000 | bytes 1000000 | tf_op jit(solution)/shard_map/middle/pallas_call | solution.py:500
  12.3 0.6 %collective-permute-done.2.before_ref.after_ref.code_before_ref.code_after_ref = bf16[96,384]{1,0:T(8,128)(2,1)S(1)} collective-permute-done((bf16[96,384]{1,0:T(8,128)(2,1)S(1)}, bf16[96,384]{1,0:T(8,128)(2,1)S(1)}, u32[]{:S(2)}, u32[]{:S(2)}) %collective-permute-start.2) | collective-permute-done | bytes 73760 | tf_op jit(solution)/shard_map/ppermute | solution.py:489
  13.0 3.8 %side.1 = (bf16[24,3,128,256]{3,2,1,0:T(8,128)(2,1)S(1)}, f32[3,192,128]{2,1,0:T(8,128)S(1)}) custom-call(bf16[128,384]{1,0:T(8,128)(2,1)S(1)} %get-tuple-element.30.centre_ref, bf16[96,384]{1,0:T(8,128)(2,1)S(1)} %collective-permute-done.2.before_ref.after_ref.code_before_ref.code_after_ref, ...), custom_call_target="tpu_custom_call" | custom-call | flops 1000000 | bytes 1000000 | tf_op jit(solution)/shard_map/side/pallas_call | solution.py:511
  16.8 0.1 collective-permute-start.3
  16.9 1.3 %back_tables.1 = (bf16[24,512,256]{2,1,0:T(8,128)(2,1)S(1)}, bf16[4,128,2304]{2,1,0:T(8,128)(2,1)S(1)}) custom-call(f32[24,8,256]{2,1,0:T(8,128)S(1)} %get-tuple-element.32.taps_ref, f32[3,192,128]{2,1,0:T(8,128)S(1)} %get-tuple-element.36._.own_ref), custom_call_target="tpu_custom_call" | custom-call | flops 1000000000 | bytes 1000000 | tf_op jit(solution)/shard_map/back_tables/pallas_call | solution.py:521
  18.2 0.3 collective-permute-done.3.other_ref
  18.4 4.4 %backward.1 = (f32[256,128]{1,0:T(8,128)S(1)}, f32[256,128]{1,0:T(8,128)}, f32[2,128]{1,0:T(2,128)S(1)}) custom-call(f32[3,192,128]{2,1,0:T(8,128)S(1)} %get-tuple-element.36._.own_ref, f32[3,192,128]{2,1,0:T(8,128)S(1)} %collective-permute-done.3.other_ref, bf16[128,384]{1,0:T(8,128)(2,1)S(1)} %get-tuple-element.37.code_ref, ...), custom_call_target="tpu_custom_call" | custom-call | flops 1000000 | bytes 1000000 | tf_op jit(solution)/shard_map/backward/pallas_call | solution.py:530
  22.8 0.3 collective-permute-start.4
  23.1 0.9 %collective-permute-done.4 = f32[2,128]{1,0:T(2,128)S(1)} collective-permute-done((f32[2,128]{1,0:T(2,128)S(1)}, f32[2,128]{1,0:T(2,128)S(1)}, u32[]{:S(2)}, u32[]{:S(2)}) %collective-permute-start.4) | collective-permute-done | bytes 1056 | tf_op jit(solution)/shard_map/ppermute | solution.py:546
  24.1 1.3 %collective-permute-start.5 = (f32[2,128]{1,0:T(2,128)S(1)}, f32[2,128]{1,0:T(2,128)S(1)}, u32[]{:S(2)}, u32[]{:S(2)}) collective-permute-start(f32[2,128]{1,0:T(2,128)S(1)} %add.12), channel_id=1, source_target_pairs={{0,3},{1,2},{2,1},{3,0},{4,7},{5,6},{6,5},{7,4},{8,11},{9,10},{10,... | collective-permute-start | bytes 3080 | tf_op jit(solution)/shard_map/ppermute | solution.py:54
  25.4 1.7 %collective-permute-done.5 = f32[2,128]{1,0:T(2,128)S(1)} collective-permute-done((f32[2,128]{1,0:T(2,128)S(1)}, f32[2,128]{1,0:T(2,128)S(1)}, u32[]{:S(2)}, u32[]{:S(2)}) %collective-permute-start.5) | collective-permute-done | bytes 1056 | tf_op jit(solution)/shard_map/ppermute | solution.py:54
  27.1 1.4 %collective-permute-start.6 = (f32[2,128]{1,0:T(2,128)S(1)}, f32[2,128]{1,0:T(2,128)S(1)}, u32[]{:S(2)}, u32[]{:S(2)}) collective-permute-start(f32[2,128]{1,0:T(2,128)S(1)} %add.13), channel_id=1, source_target_pairs={{0,5},{1,4},{4,1},{5,0},{8,13},{9,12},{12,9},{13,8},{2,7},{3,6},{6... | collective-permute-start | bytes 3080 | tf_op jit(solution)/shard_map/ppermute | solution.py:54
  28.5 1.6 %collective-permute-done.6 = f32[2,128]{1,0:T(2,128)S(1)} collective-permute-done((f32[2,128]{1,0:T(2,128)S(1)}, f32[2,128]{1,0:T(2,128)S(1)}, u32[]{:S(2)}, u32[]{:S(2)}) %collective-permute-start.6) | collective-permute-done | bytes 1056 | tf_op jit(solution)/shard_map/ppermute | solution.py:54
  30.1 2.4 %collective-permute-start.7 = (f32[2,128]{1,0:T(2,128)S(1)}, f32[2,128]{1,0:T(2,128)S(1)}, u32[]{:S(2)}, u32[]{:S(2)}) collective-permute-start(f32[2,128]{1,0:T(2,128)S(1)} %add.14), channel_id=1, source_target_pairs={{0,9},{1,8},{4,13},{5,12},{8,1},{9,0},{12,5},{13,4},{2,11},{3,10},... | collective-permute-start | bytes 3080 | tf_op jit(solution)/shard_map/ppermute | solution.py:54
  32.5 1.5 %collective-permute-done.7 = f32[2,128]{1,0:T(2,128)S(1)} collective-permute-done((f32[2,128]{1,0:T(2,128)S(1)}, f32[2,128]{1,0:T(2,128)S(1)}, u32[]{:S(2)}, u32[]{:S(2)}) %collective-permute-start.7) | collective-permute-done | bytes 1056 | tf_op jit(solution)/shard_map/ppermute | solution.py:54
  34.0 0.7 %finish.1 = (f32[256,128]{1,0:T(8,128)}, f32[1,128]{1,0:T(1,128)}) custom-call(f32[256,128]{1,0:T(8,128)S(1)} %get-tuple-element.25.params_ref, f32[256,128]{1,0:T(8,128)S(1)} %get-tuple-element.42.gradient_ref, f32[2,128]{1,0:T(2,128)S(1)} %add.15.sums_ref), custom_call_target="tpu_custom_call" | custom-call | flops 1000000 | bytes 1000000 | tf_op jit(solution)/shard_map/finish/pallas_call | solution.py:550
  (4 shorter events, 0.0 us)
Async XLA Ops:
  1.5 5.5 %collective-permute-start = (bf16[96,128]{1,0:T(8,128)(2,1)S(1)}, bf16[96,128]{1,0:T(8,128)(2,1)S(1)}, u32[]{:S(2)}, u32[]{:S(2)}) collective-permute-start(bf16[96,128]{1,0:T(8,128)(2,1)S(1)} %get-tuple-element.28), channel_id=1, source_target_pairs={{0,4},{4,8},{8,12},{12,28},{28,24},{24,20},{20,16},{16,0},{1,5},{5... | collective-permute-start | bytes 73736 | tf_op jit(solution)/shard_map/ppermute | solution.py:460
  4.6 3.8 %collective-permute-start.1 = (bf16[96,128]{1,0:T(8,128)(2,1)S(1)}, bf16[96,128]{1,0:T(8,128)(2,1)S(1)}, u32[]{:S(2)}, u32[]{:S(2)}) collective-permute-start(bf16[96,128]{1,0:T(8,128)(2,1)S(1)} %get-tuple-element.29), channel_id=1, source_target_pairs={{0,16},{4,0},{8,4},{12,8},{28,12},{24,28},{20,24},{16,20},{1,17},{... | collective-permute-start | bytes 73736 | tf_op jit(solution)/shard_map/ppermute | solution.py:461
  8.6 4.4 %collective-permute-start.2 = (bf16[96,384]{1,0:T(8,128)(2,1)S(1)}, bf16[96,384]{1,0:T(8,128)(2,1)S(1)}, u32[]{:S(2)}, u32[]{:S(2)}) collective-permute-start(bf16[96,384]{1,0:T(8,128)(2,1)S(1)} %get-tuple-element.31), channel_id=1, source_target_pairs={{0,2},{2,0},{1,3},{3,1},{4,6},{6,4},{5,7},{7,5},{8,10},{10,8},{9,1... | collective-permute-start | bytes 221192 | tf_op jit(solution)/shard_map/ppermute | solution.py:489
  16.8 1.6 %collective-permute-start.3 = (f32[3,192,128]{2,1,0:T(8,128)S(1)}, f32[3,192,128]{2,1,0:T(8,128)S(1)}, u32[]{:S(2)}, u32[]{:S(2)}) collective-permute-start(f32[3,192,128]{2,1,0:T(8,128)S(1)} %get-tuple-element.36._.own_ref), channel_id=1, source_target_pairs={{0,1},{1,0},{2,3},{3,2},{4,5},{5,4},{6,7},{7,6},{8,9},{9,8},{10,11... | collective-permute-start | bytes 884744 | tf_op jit(solution)/shard_map/ppermute | solution.py:520
  22.8 1.2 %collective-permute-start.4 = (f32[2,128]{1,0:T(2,128)S(1)}, f32[2,128]{1,0:T(2,128)S(1)}, u32[]{:S(2)}, u32[]{:S(2)}) collective-permute-start(f32[2,128]{1,0:T(2,128)S(1)} %get-tuple-element.43), channel_id=1, source_target_pairs={{0,1},{1,0},{2,3},{3,2},{4,5},{5,4},{6,7},{7,6},{8,9},{9,8},{10,11... | collective-permute-start | bytes 3080 | tf_op jit(solution)/shard_map/ppermute | solution.py:546
  24.1 3.0 %collective-permute-start.5 = (f32[2,128]{1,0:T(2,128)S(1)}, f32[2,128]{1,0:T(2,128)S(1)}, u32[]{:S(2)}, u32[]{:S(2)}) collective-permute-start(f32[2,128]{1,0:T(2,128)S(1)} %add.12), channel_id=1, source_target_pairs={{0,3},{1,2},{2,1},{3,0},{4,7},{5,6},{6,5},{7,4},{8,11},{9,10},{10,... | collective-permute-start | bytes 3080 | tf_op jit(solution)/shard_map/ppermute | solution.py:54
  27.1 3.0 %collective-permute-start.6 = (f32[2,128]{1,0:T(2,128)S(1)}, f32[2,128]{1,0:T(2,128)S(1)}, u32[]{:S(2)}, u32[]{:S(2)}) collective-permute-start(f32[2,128]{1,0:T(2,128)S(1)} %add.13), channel_id=1, source_target_pairs={{0,5},{1,4},{4,1},{5,0},{8,13},{9,12},{12,9},{13,8},{2,7},{3,6},{6... | collective-permute-start | bytes 3080 | tf_op jit(solution)/shard_map/ppermute | solution.py:54
  30.1 3.9 %collective-permute-start.7 = (f32[2,128]{1,0:T(2,128)S(1)}, f32[2,128]{1,0:T(2,128)S(1)}, u32[]{:S(2)}, u32[]{:S(2)}) collective-permute-start(f32[2,128]{1,0:T(2,128)S(1)} %add.14), channel_id=1, source_target_pairs={{0,9},{1,8},{4,13},{5,12},{8,1},{9,0},{12,5},{13,4},{2,11},{3,10},... | collective-permute-start | bytes 3080 | tf_op jit(solution)/shard_map/ppermute | solution.py:54

commit v9 on v8

--- a/solution.py
+++ b/solution.py
@@ -252,8 +252,22 @@
             total_ref[t] += scaled * part
 
 
-def back_tables_kernel(taps_ref, _, row_table_ref, col_table_ref, masks_ref):
+def back_tables_kernel(
+    taps_ref, code_ref, code_before_ref, code_after_ref, _, row_table_ref, col_table_ref, goal_ref, factor_ref, masks_ref
+):
     kernels = taps_ref.shape[0]
+    for t in range(goal_ref.shape[0]):
+        lanes = slice(t * LANES, (t + 1) * LANES)
+        code = jnp.concatenate(
+            [
+                unless(at_start("col"), code_before_ref[2 * HALF :, lanes]),
+                code_ref[:, lanes].astype(F32),
+                unless(at_end("col"), code_after_ref[2 * HALF :, lanes]),
+            ],
+            axis=0,
+        )
+        goal_ref[t] = code - 1.0
+        factor_ref[t] = jnp.where(code > 0.5, 4.0 * resist_steep, 0.0)
     wide = 2 * HALF
     each = 3 * LANES
     write_masks(masks_ref)
@@ -319,9 +333,8 @@
 def backward_kernel(
     own_ref,
     other_ref,
-    code_ref,
-    code_before_ref,
-    code_after_ref,
+    goal_ref,
+    factor_ref,
     params_ref,
     middle_ref,
     side_ref,
@@ -337,7 +350,7 @@
     sem,
 ):
     kernels = row_table_ref.shape[0]
-    cols = code_ref.shape[0]
+    cols = gradient_ref.shape[1]
     wide = 2 * HALF
     tiles = own_ref.shape[0]
     span = cols + wide
@@ -346,20 +359,10 @@
 
     resists, loss = [], 0.0
     for t in range(tiles):
-        lanes = slice(t * LANES, (t + 1) * LANES)
-        code = jnp.concatenate(
-            [
-                unless(at_start("col"), code_before_ref[wide:, lanes]),
-                code_ref[:, lanes].astype(F32),
-                unless(at_end("col"), code_after_ref[wide:, lanes]),
-            ],
-            axis=0,
-        )
         summed = own_ref[t] + other_ref[t]
         resist = jax.nn.sigmoid(resist_steep * (summed - resist_level))
-        mismatch = resist - (code - 1.0)
-        slope = 4.0 * mismatch * resist_steep * resist * (1.0 - resist)
-        slope = jnp.where(code > 0.5, slope, 0.0).astype(BF16)
+        mismatch = resist - goal_ref[t]
+        slope = (mismatch * resist * (1.0 - resist) * factor_ref[t]).astype(BF16)
         slope_ref[t] = jnp.concatenate([slope, slope], axis=1)
         resists.append(resist[HALF : HALF + cols])
         mine = mismatch[HALF : HALF + cols]
@@ -518,19 +521,24 @@
     )(centre, before, after, middle_intensity, *tables)
 
     other = lax.ppermute(intensity, "expo", [(0, 1), (1, 0)])
-    back_tables = call(
+    row_table, col_table, goal, factor = call(
         back_tables_kernel,
         "back_tables",
-        [vmem, pl.BlockSpec(memory_space=pl.ANY)],
-        (row_tables, array((kernels // CHUNK, cols, CHUNK * 2 * span), BF16)),
+        [vmem] * 4 + [pl.BlockSpec(memory_space=pl.ANY)],
+        (
+            row_tables,
+            array((kernels // CHUNK, cols, CHUNK * 2 * span), BF16),
+            array(plane, F32),
+            array(plane, F32),
+        ),
         scratch=[masks],
         flops=10**9,
-    )(tables[0], intensity)
+    )(tables[0], code_turned, before, after, intensity)
 
     gradient, resist, sums = call(
         backward_kernel,
         "backward",
-        [vmem] * 10,
+        [vmem] * 9,
         (full, full, array((2, LANES), F32)),
         out_specs=[vmem, hbm, vmem],
         scratch=[
@@ -541,7 +549,7 @@
             pltpu.SemaphoreType.DMA,
         ],
         grant=VMEM,
-    )(intensity, other, code_turned, before, after, params, middle, sides_field, *back_tables)
+    )(intensity, other, goal, factor, params, middle, sides_field, row_table, col_table)
 
     sums = sums + lax.ppermute(sums, "expo", [(0, 1), (1, 0)])
     for axis in ("col", "strip"):

time: 34.9 us -> 34.8 us (level)
  no operation moved by 1% of the time
where the time goes in v9:
time: 34.8 us; the launch traced here: 34.5 us
  Pallas kernels  15.6 us (45%)
  starting transfers between devices  10.5 us (30%)
  waiting for transfers between devices  7.73 us (22%)
  between operations  0.71 us (2%)
    ppermute x3, starting transfers between devices, total_over(): lax.ppermute(value, both, partners(peers, lambda i, r=reach: i ^ r))  5.37 us
    ppermute x3, waiting for transfers between devices, total_over(): lax.ppermute(value, both, partners(peers, lambda i, r=reach: i ^ r))  4.53 us
    pallas_call x1, Pallas kernels, shards(): call(backward_kernel, 'backward', [vmem] * 9, (full, full, array((2, LANE...  4.25 us
    pallas_call x1, Pallas kernels, shards(): call(side_kernel, 'side', [vmem] * 7, (fields, array(plane, F32)), scratc...  3.79 us
    ppermute x1, starting transfers between devices, shards(): from_behind = lax.ppermute(ahead, ('tiles', 'strip'), snake(1))  3.1 us
    pallas_call x1, Pallas kernels, shards(): call(load_kernel, 'load', [hbm] * 5, (full, plain, plain, array((kernels,...  2.33 us
    pallas_call x1, Pallas kernels, shards(): call(middle_kernel, 'middle', [vmem] * 4, (fields, array((tiles, wide, LA...  2.21 us
    ppermute x1, starting transfers between devices, shards(): before = after = lax.ppermute(messages[0], 'col', ring('col', 1))  1.56 us
  transfers between devices with their start and end apart: 8, of which 7 were waited for; matrix products, arithmetic and copies ran while one was open for 0% of the time, Pallas kernels for 17%

profile of v9, /device:TPU:0, one launch (start us, length us, event | category | flops | bytes accessed | tf_op | source)
XLA Modules:
  0.0 34.5 jit_solution(13106240856666414734)
XLA Ops:
  0.6 0.8 %edges.1 = (bf16[96,128]{1,0:T(8,128)(2,1)S(1)}, bf16[96,128]{1,0:T(8,128)(2,1)S(1)}) custom-call(f32[256,128]{1,0:T(8,128)} %bitcast.4, s32[256,128]{1,0:T(8,128)} %target_hbm.3), custom_call_target="tpu_custom_call" | custom-call | flops 1000000 | bytes 1000000 | tf_op jit(solution)/shard_map/edges/pallas_call | solution.py:452
  1.5 3.1 %collective-permute-start = (bf16[96,128]{1,0:T(8,128)(2,1)S(1)}, bf16[96,128]{1,0:T(8,128)(2,1)S(1)}, u32[]{:S(2)}, u32[]{:S(2)}) collective-permute-start(bf16[96,128]{1,0:T(8,128)(2,1)S(1)} %get-tuple-element.30), channel_id=1, source_target_pairs={{0,4},{4,8},{8,12},{12,28},{28,24},{24,20},{20,16},{16,0},{1,5},{5... | collective-permute-start | bytes 73736 | tf_op jit(solution)/shard_map/ppermute | solution.py:463
  4.6 0.0 collective-permute-start.1
  4.6 2.3 %load.1 = (f32[256,128]{1,0:T(8,128)S(1)}, bf16[256,128]{1,0:T(8,128)(2,1)S(1)}, bf16[256,128]{1,0:T(8,128)(2,1)S(1)}, f32[24,8,256]{2,1,0:T(8,128)S(1)}, bf16[3...) custom-call(f32[256,128]{1,0:T(8,128)} %bitcast.5, s32[256,128]{1,0:T(8,128)} %target_hbm.3, f32[24]{0:T(128)} %weights_hbm.1, ...), custom_call_target="tpu_custom_call" | custom-call | flops 100000000 | bytes 1000000 | tf_op jit(solution)/shard_map/load/pallas_call | solution.py:467
  6.9 0.0 collective-permute-done.behind_ref
  6.9 1.5 %collective-permute-done.1.ahead_ref = bf16[96,128]{1,0:T(8,128)(2,1)S(1)} collective-permute-done((bf16[96,128]{1,0:T(8,128)(2,1)S(1)}, bf16[96,128]{1,0:T(8,128)(2,1)S(1)}, u32[]{:S(2)}, u32[]{:S(2)}) %collective-permute-start.1) | collective-permute-done | bytes 24608 | tf_op jit(solution)/shard_map/ppermute | solution.py:464
  8.4 0.2 assemble.1
  8.6 1.6 %collective-permute-start.2 = (bf16[96,384]{1,0:T(8,128)(2,1)S(1)}, bf16[96,384]{1,0:T(8,128)(2,1)S(1)}, u32[]{:S(2)}, u32[]{:S(2)}) collective-permute-start(bf16[96,384]{1,0:T(8,128)(2,1)S(1)} %get-tuple-element.33), channel_id=1, source_target_pairs={{0,2},{2,0},{1,3},{3,1},{4,6},{6,4},{5,7},{7,5},{8,10},{10,8},{9,1... | collective-permute-start | bytes 221192 | tf_op jit(solution)/shard_map/ppermute | solution.py:492
  10.1 2.2 %middle.1 = (bf16[24,3,64,256]{3,2,1,0:T(8,128)(2,1)S(1)}, f32[3,64,128]{2,1,0:T(8,128)S(1)}) custom-call(bf16[128,384]{1,0:T(8,128)(2,1)S(1)} %get-tuple-element.32.centre_ref, f32[24,8,256]{2,1,0:T(8,128)S(1)} %get-tuple-element.34.taps_ref, bf16[3072,128]{1,0:T(8,128)(2,1)S(1)} %get-tuple-element.35.near_ref, ...), custom_call_target="tpu_custom_call" | custom-call | flops 4000000000 | bytes 1000000 | tf_op jit(solution)/shard_map/middle/pallas_call | solution.py:503
  12.3 0.6 %collective-permute-done.2.before_ref.after_ref.code_before_ref.code_after_ref = bf16[96,384]{1,0:T(8,128)(2,1)S(1)} collective-permute-done((bf16[96,384]{1,0:T(8,128)(2,1)S(1)}, bf16[96,384]{1,0:T(8,128)(2,1)S(1)}, u32[]{:S(2)}, u32[]{:S(2)}) %collective-permute-start.2) | collective-permute-done | bytes 73760 | tf_op jit(solution)/shard_map/ppermute | solution.py:492
  13.0 3.8 %side.1 = (bf16[24,3,128,256]{3,2,1,0:T(8,128)(2,1)S(1)}, f32[3,192,128]{2,1,0:T(8,128)S(1)}) custom-call(bf16[128,384]{1,0:T(8,128)(2,1)S(1)} %get-tuple-element.32.centre_ref, bf16[96,384]{1,0:T(8,128)(2,1)S(1)} %collective-permute-done.2.before_ref.after_ref.code_before_ref.code_after_ref, ...), custom_call_target="tpu_custom_call" | custom-call | flops 1000000 | bytes 1000000 | tf_op jit(solution)/shard_map/side/pallas_call | solution.py:514
  16.8 0.1 collective-permute-start.3
  16.9 1.3 %back_tables.1 = (bf16[24,512,256]{2,1,0:T(8,128)(2,1)S(1)}, bf16[4,128,2304]{2,1,0:T(8,128)(2,1)S(1)}, f32[3,192,128]{2,1,0:T(8,128)S(1)}, f32[3,192,128]{2,1,0:T(8,128)S(1)}) custom-call(f32[24,8,256]{2,1,0:T(8,128)S(1)} %get-tuple-element.34.taps_ref, bf16[128,384]{1,0:T(8,128)(2,1)S(1)} %get-tuple-element.39.code_ref, ...), custom_call_target="tpu_custom_call" | custom-call | flops 1000000000 | bytes 1000000 | tf_op jit(solution)/shard_map/back_tables/pallas_call | solution.py:524
  18.2 0.2 collective-permute-done.3.other_ref
  18.4 4.3 %backward.1 = (f32[256,128]{1,0:T(8,128)S(1)}, f32[256,128]{1,0:T(8,128)}, f32[2,128]{1,0:T(2,128)S(1)}) custom-call(f32[3,192,128]{2,1,0:T(8,128)S(1)} %get-tuple-element.38._.own_ref, f32[3,192,128]{2,1,0:T(8,128)S(1)} %collective-permute-done.3.other_ref, f32[3,192,128]{2,1,0:T(8,128)S(1)} %get-tuple-element.40.goal_ref, ...), custom_call_target="tpu_custom_call" | custom-call | flops 1000000 | bytes 1000000 | tf_op jit(solution)/shard_map/backward/pallas_call | solution.py:538
  22.7 0.4 %collective-permute-start.4 = (f32[2,128]{1,0:T(2,128)S(1)}, f32[2,128]{1,0:T(2,128)S(1)}, u32[]{:S(2)}, u32[]{:S(2)}) collective-permute-start(f32[2,128]{1,0:T(2,128)S(1)} %get-tuple-element.47), channel_id=1, source_target_pairs={{0,1},{1,0},{2,3},{3,2},{4,5},{5,4},{6,7},{7,6},{8,9},{9,8},{10,11... | collective-permute-start | bytes 3080 | tf_op jit(solution)/shard_map/ppermute | solution.py:554
  23.0 0.9 %collective-permute-done.4 = f32[2,128]{1,0:T(2,128)S(1)} collective-permute-done((f32[2,128]{1,0:T(2,128)S(1)}, f32[2,128]{1,0:T(2,128)S(1)}, u32[]{:S(2)}, u32[]{:S(2)}) %collective-permute-start.4) | collective-permute-done | bytes 1056 | tf_op jit(solution)/shard_map/ppermute | solution.py:554
  23.9 1.4 %collective-permute-start.5 = (f32[2,128]{1,0:T(2,128)S(1)}, f32[2,128]{1,0:T(2,128)S(1)}, u32[]{:S(2)}, u32[]{:S(2)}) collective-permute-start(f32[2,128]{1,0:T(2,128)S(1)} %add.12), channel_id=1, source_target_pairs={{0,3},{1,2},{2,1},{3,0},{4,7},{5,6},{6,5},{7,4},{8,11},{9,10},{10,... | collective-permute-start | bytes 3080 | tf_op jit(solution)/shard_map/ppermute | solution.py:54
  25.3 1.6 %collective-permute-done.5 = f32[2,128]{1,0:T(2,128)S(1)} collective-permute-done((f32[2,128]{1,0:T(2,128)S(1)}, f32[2,128]{1,0:T(2,128)S(1)}, u32[]{:S(2)}, u32[]{:S(2)}) %collective-permute-start.5) | collective-permute-done | bytes 1056 | tf_op jit(solution)/shard_map/ppermute | solution.py:54
  26.9 1.5 %collective-permute-start.6 = (f32[2,128]{1,0:T(2,128)S(1)}, f32[2,128]{1,0:T(2,128)S(1)}, u32[]{:S(2)}, u32[]{:S(2)}) collective-permute-start(f32[2,128]{1,0:T(2,128)S(1)} %add.13), channel_id=1, source_target_pairs={{0,5},{1,4},{4,1},{5,0},{8,13},{9,12},{12,9},{13,8},{2,7},{3,6},{6... | collective-permute-start | bytes 3080 | tf_op jit(solution)/shard_map/ppermute | solution.py:54
  28.4 1.5 %collective-permute-done.6 = f32[2,128]{1,0:T(2,128)S(1)} collective-permute-done((f32[2,128]{1,0:T(2,128)S(1)}, f32[2,128]{1,0:T(2,128)S(1)}, u32[]{:S(2)}, u32[]{:S(2)}) %collective-permute-start.6) | collective-permute-done | bytes 1056 | tf_op jit(solution)/shard_map/ppermute | solution.py:54
  29.9 2.5 %collective-permute-start.7 = (f32[2,128]{1,0:T(2,128)S(1)}, f32[2,128]{1,0:T(2,128)S(1)}, u32[]{:S(2)}, u32[]{:S(2)}) collective-permute-start(f32[2,128]{1,0:T(2,128)S(1)} %add.14), channel_id=1, source_target_pairs={{0,9},{1,8},{4,13},{5,12},{8,1},{9,0},{12,5},{13,4},{2,11},{3,10},... | collective-permute-start | bytes 3080 | tf_op jit(solution)/shard_map/ppermute | solution.py:54
  32.4 1.4 %collective-permute-done.7 = f32[2,128]{1,0:T(2,128)S(1)} collective-permute-done((f32[2,128]{1,0:T(2,128)S(1)}, f32[2,128]{1,0:T(2,128)S(1)}, u32[]{:S(2)}, u32[]{:S(2)}) %collective-permute-start.7) | collective-permute-done | bytes 1056 | tf_op jit(solution)/shard_map/ppermute | solution.py:54
  33.8 0.7 %finish.1 = (f32[256,128]{1,0:T(8,128)}, f32[1,128]{1,0:T(1,128)}) custom-call(f32[256,128]{1,0:T(8,128)S(1)} %get-tuple-element.27.params_ref, f32[256,128]{1,0:T(8,128)S(1)} %get-tuple-element.46.gradient_ref, f32[2,128]{1,0:T(2,128)S(1)} %add.15.sums_ref), custom_call_target="tpu_custom_call" | custom-call | flops 1000000 | bytes 1000000 | tf_op jit(solution)/shard_map/finish/pallas_call | solution.py:558
  (4 shorter events, 0.0 us)
Async XLA Ops:
  1.5 5.5 %collective-permute-start = (bf16[96,128]{1,0:T(8,128)(2,1)S(1)}, bf16[96,128]{1,0:T(8,128)(2,1)S(1)}, u32[]{:S(2)}, u32[]{:S(2)}) collective-permute-start(bf16[96,128]{1,0:T(8,128)(2,1)S(1)} %get-tuple-element.30), channel_id=1, source_target_pairs={{0,4},{4,8},{8,12},{12,28},{28,24},{24,20},{20,16},{16,0},{1,5},{5... | collective-permute-start | bytes 73736 | tf_op jit(solution)/shard_map/ppermute | solution.py:463
  4.6 3.8 %collective-permute-start.1 = (bf16[96,128]{1,0:T(8,128)(2,1)S(1)}, bf16[96,128]{1,0:T(8,128)(2,1)S(1)}, u32[]{:S(2)}, u32[]{:S(2)}) collective-permute-start(bf16[96,128]{1,0:T(8,128)(2,1)S(1)} %get-tuple-element.31), channel_id=1, source_target_pairs={{0,16},{4,0},{8,4},{12,8},{28,12},{24,28},{20,24},{16,20},{1,17},{... | collective-permute-start | bytes 73736 | tf_op jit(solution)/shard_map/ppermute | solution.py:464
  8.6 4.4 %collective-permute-start.2 = (bf16[96,384]{1,0:T(8,128)(2,1)S(1)}, bf16[96,384]{1,0:T(8,128)(2,1)S(1)}, u32[]{:S(2)}, u32[]{:S(2)}) collective-permute-start(bf16[96,384]{1,0:T(8,128)(2,1)S(1)} %get-tuple-element.33), channel_id=1, source_target_pairs={{0,2},{2,0},{1,3},{3,1},{4,6},{6,4},{5,7},{7,5},{8,10},{10,8},{9,1... | collective-permute-start | bytes 221192 | tf_op jit(solution)/shard_map/ppermute | solution.py:492
  16.8 1.6 %collective-permute-start.3 = (f32[3,192,128]{2,1,0:T(8,128)S(1)}, f32[3,192,128]{2,1,0:T(8,128)S(1)}, u32[]{:S(2)}, u32[]{:S(2)}) collective-permute-start(f32[3,192,128]{2,1,0:T(8,128)S(1)} %get-tuple-element.38._.own_ref), channel_id=1, source_target_pairs={{0,1},{1,0},{2,3},{3,2},{4,5},{5,4},{6,7},{7,6},{8,9},{9,8},{10,11... | collective-permute-start | bytes 884744 | tf_op jit(solution)/shard_map/ppermute | solution.py:523
  22.7 1.2 %collective-permute-start.4 = (f32[2,128]{1,0:T(2,128)S(1)}, f32[2,128]{1,0:T(2,128)S(1)}, u32[]{:S(2)}, u32[]{:S(2)}) collective-permute-start(f32[2,128]{1,0:T(2,128)S(1)} %get-tuple-element.47), channel_id=1, source_target_pairs={{0,1},{1,0},{2,3},{3,2},{4,5},{5,4},{6,7},{7,6},{8,9},{9,8},{10,11... | collective-permute-start | bytes 3080 | tf_op jit(solution)/shard_map/ppermute | solution.py:554
  23.9 3.0 %collective-permute-start.5 = (f32[2,128]{1,0:T(2,128)S(1)}, f32[2,128]{1,0:T(2,128)S(1)}, u32[]{:S(2)}, u32[]{:S(2)}) collective-permute-start(f32[2,128]{1,0:T(2,128)S(1)} %add.12), channel_id=1, source_target_pairs={{0,3},{1,2},{2,1},{3,0},{4,7},{5,6},{6,5},{7,4},{8,11},{9,10},{10,... | collective-permute-start | bytes 3080 | tf_op jit(solution)/shard_map/ppermute | solution.py:54
  26.9 3.0 %collective-permute-start.6 = (f32[2,128]{1,0:T(2,128)S(1)}, f32[2,128]{1,0:T(2,128)S(1)}, u32[]{:S(2)}, u32[]{:S(2)}) collective-permute-start(f32[2,128]{1,0:T(2,128)S(1)} %add.13), channel_id=1, source_target_pairs={{0,5},{1,4},{4,1},{5,0},{8,13},{9,12},{12,9},{13,8},{2,7},{3,6},{6... | collective-permute-start | bytes 3080 | tf_op jit(solution)/shard_map/ppermute | solution.py:54
  29.9 3.9 %collective-permute-start.7 = (f32[2,128]{1,0:T(2,128)S(1)}, f32[2,128]{1,0:T(2,128)S(1)}, u32[]{:S(2)}, u32[]{:S(2)}) collective-permute-start(f32[2,128]{1,0:T(2,128)S(1)} %add.14), channel_id=1, source_target_pairs={{0,9},{1,8},{4,13},{5,12},{8,1},{9,0},{12,5},{13,4},{2,11},{3,10},... | collective-permute-start | bytes 3080 | tf_op jit(solution)/shard_map/ppermute | solution.py:54

commit v10 on v9

--- a/solution.py
+++ b/solution.py
@@ -9,7 +9,8 @@
 HALF = 32
 LANES = 128
 BACKWARD_UNROLL = 12
-CHUNK = 6
+GROUPS = 2
+CHUNK = 12
 VMEM = 24 * 2**20
 
 mask_slope = 4.0
@@ -226,30 +227,34 @@
     wide = 2 * HALF
     long = tiles * LANES
     total_ref[...] = jnp.zeros_like(total_ref)
-    columns = jnp.dot(near_ref[...], source_ref[...], preferred_element_type=F32).astype(BF16)
-    for kernel in range(kernels):
-        for part in range(2):
-            at = (kernel * 2 + part) * wide
-            for block in range(span // wide):
-                for t in range(tiles):
-                    lane = block * long + t * LANES
-                    to = t * span + block * wide
-                    columns_ref[kernel, to : to + wide, part * LANES : (part + 1) * LANES] = columns[
-                        at : at + wide, lane : lane + LANES
-                    ]
     edge = (tiles - 1) * span
-    for kernel in range(kernels):
-        weight = taps_ref[kernel, 4:5, :]
-        window = jnp.concatenate([columns_ref[kernel, 0:edge], columns_ref[kernel, span:]], axis=1)
-        inner = jnp.dot(window, row_table_ref[kernel], preferred_element_type=F32)
-        outer = jnp.dot(
-            columns_ref[kernel, edge:], row_table_ref[kernel, 0 : 2 * LANES], preferred_element_type=F32
-        )
-        for t in range(tiles):
-            part = inner[t * span : (t + 1) * span] if t + 1 < tiles else outer
-            scaled = weight * part
-            field_ref[kernel, t] = scaled.astype(field_ref.dtype)
-            total_ref[t] += scaled * part
+    each = kernels // GROUPS
+    for group in range(GROUPS):
+        first = group * each
+        lines = slice(first * 2 * wide, (first + each) * 2 * wide)
+        columns = jnp.dot(near_ref[lines, :], source_ref[...], preferred_element_type=F32).astype(BF16)
+        for kernel in range(first, first + each):
+            for part in range(2):
+                at = ((kernel - first) * 2 + part) * wide
+                for block in range(span // wide):
+                    for t in range(tiles):
+                        lane = block * long + t * LANES
+                        to = t * span + block * wide
+                        columns_ref[kernel, to : to + wide, part * LANES : (part + 1) * LANES] = columns[
+                            at : at + wide, lane : lane + LANES
+                        ]
+        for kernel in range(first, first + each):
+            weight = taps_ref[kernel, 4:5, :]
+            window = jnp.concatenate([columns_ref[kernel, 0:edge], columns_ref[kernel, span:]], axis=1)
+            inner = jnp.dot(window, row_table_ref[kernel], preferred_element_type=F32)
+            outer = jnp.dot(
+                columns_ref[kernel, edge:], row_table_ref[kernel, 0 : 2 * LANES], preferred_element_type=F32
+            )
+            for t in range(tiles):
+                part = inner[t * span : (t + 1) * span] if t + 1 < tiles else outer
+                scaled = weight * part
+                field_ref[kernel, t] = scaled.astype(field_ref.dtype)
+                total_ref[t] += scaled * part
 
 
 def back_tables_kernel(

time: 34.8 us -> 34.7 us (level)
  no operation moved by 1% of the time
where the time goes in v10:
time: 34.7 us; the launch traced here: 34.4 us
  Pallas kernels  15.5 us (45%)
  starting transfers between devices  10.5 us (30%)
  waiting for transfers between devices  7.75 us (22%)
  between operations  0.71 us (2%)
    ppermute x3, starting transfers between devices, total_over(): lax.ppermute(value, both, partners(peers, lambda i, r=reach: i ^ r))  5.36 us
    ppermute x3, waiting for transfers between devices, total_over(): lax.ppermute(value, both, partners(peers, lambda i, r=reach: i ^ r))  4.53 us
    pallas_call x1, Pallas kernels, shards(): call(backward_kernel, 'backward', [vmem] * 9, (full, full, array((2, LANE...  4.23 us
    pallas_call x1, Pallas kernels, shards(): call(side_kernel, 'side', [vmem] * 7, (fields, array(plane, F32)), scratc...  3.74 us
    ppermute x1, starting transfers between devices, shards(): from_behind = lax.ppermute(ahead, ('tiles', 'strip'), snake(1))  3.1 us
    pallas_call x1, Pallas kernels, shards(): call(load_kernel, 'load', [hbm] * 5, (full, plain, plain, array((kernels,...  2.33 us
    pallas_call x1, Pallas kernels, shards(): call(middle_kernel, 'middle', [vmem] * 4, (fields, array((tiles, wide, LA...  2.19 us
    ppermute x1, starting transfers between devices, shards(): before = after = lax.ppermute(messages[0], 'col', ring('col', 1))  1.56 us
  transfers between devices with their start and end apart: 8, of which 7 were waited for; matrix products, arithmetic and copies ran while one was open for 0% of the time, Pallas kernels for 17%

profile of v10, /device:TPU:0, one launch (start us, length us, event | category | flops | bytes accessed | tf_op | source)
XLA Modules:
  0.0 34.4 jit_solution(9272711771905045009)
XLA Ops:
  0.6 0.8 %edges.1 = (bf16[96,128]{1,0:T(8,128)(2,1)S(1)}, bf16[96,128]{1,0:T(8,128)(2,1)S(1)}) custom-call(f32[256,128]{1,0:T(8,128)} %bitcast.4, s32[256,128]{1,0:T(8,128)} %target_hbm.3), custom_call_target="tpu_custom_call" | custom-call | flops 1000000 | bytes 1000000 | tf_op jit(solution)/shard_map/edges/pallas_call | solution.py:457
  1.5 3.1 %collective-permute-start = (bf16[96,128]{1,0:T(8,128)(2,1)S(1)}, bf16[96,128]{1,0:T(8,128)(2,1)S(1)}, u32[]{:S(2)}, u32[]{:S(2)}) collective-permute-start(bf16[96,128]{1,0:T(8,128)(2,1)S(1)} %get-tuple-element.30), channel_id=1, source_target_pairs={{0,4},{4,8},{8,12},{12,28},{28,24},{24,20},{20,16},{16,0},{1,5},{5... | collective-permute-start | bytes 73736 | tf_op jit(solution)/shard_map/ppermute | solution.py:468
  4.6 0.0 collective-permute-start.1
  4.6 2.3 %load.1 = (f32[256,128]{1,0:T(8,128)S(1)}, bf16[256,128]{1,0:T(8,128)(2,1)S(1)}, bf16[256,128]{1,0:T(8,128)(2,1)S(1)}, f32[24,8,256]{2,1,0:T(8,128)S(1)}, bf16[3...) custom-call(f32[256,128]{1,0:T(8,128)} %bitcast.5, s32[256,128]{1,0:T(8,128)} %target_hbm.3, f32[24]{0:T(128)} %weights_hbm.1, ...), custom_call_target="tpu_custom_call" | custom-call | flops 100000000 | bytes 1000000 | tf_op jit(solution)/shard_map/load/pallas_call | solution.py:472
  6.9 0.0 collective-permute-done.behind_ref
  6.9 1.5 %collective-permute-done.1.ahead_ref = bf16[96,128]{1,0:T(8,128)(2,1)S(1)} collective-permute-done((bf16[96,128]{1,0:T(8,128)(2,1)S(1)}, bf16[96,128]{1,0:T(8,128)(2,1)S(1)}, u32[]{:S(2)}, u32[]{:S(2)}) %collective-permute-start.1) | collective-permute-done | bytes 24608 | tf_op jit(solution)/shard_map/ppermute | solution.py:469
  8.4 0.2 assemble.1
  8.6 1.6 %collective-permute-start.2 = (bf16[96,384]{1,0:T(8,128)(2,1)S(1)}, bf16[96,384]{1,0:T(8,128)(2,1)S(1)}, u32[]{:S(2)}, u32[]{:S(2)}) collective-permute-start(bf16[96,384]{1,0:T(8,128)(2,1)S(1)} %get-tuple-element.33), channel_id=1, source_target_pairs={{0,2},{2,0},{1,3},{3,1},{4,6},{6,4},{5,7},{7,5},{8,10},{10,8},{9,1... | collective-permute-start | bytes 221192 | tf_op jit(solution)/shard_map/ppermute | solution.py:497
  10.1 2.2 %middle.1 = (bf16[24,3,64,256]{3,2,1,0:T(8,128)(2,1)S(1)}, f32[3,64,128]{2,1,0:T(8,128)S(1)}) custom-call(bf16[128,384]{1,0:T(8,128)(2,1)S(1)} %get-tuple-element.32.centre_ref, f32[24,8,256]{2,1,0:T(8,128)S(1)} %get-tuple-element.34.taps_ref, bf16[3072,128]{1,0:T(8,128)(2,1)S(1)} %get-tuple-element.35.near_ref, ...), custom_call_target="tpu_custom_call" | custom-call | flops 4000000000 | bytes 1000000 | tf_op jit(solution)/shard_map/middle/pallas_call | solution.py:508
  12.3 0.7 %collective-permute-done.2.before_ref.after_ref.code_before_ref.code_after_ref = bf16[96,384]{1,0:T(8,128)(2,1)S(1)} collective-permute-done((bf16[96,384]{1,0:T(8,128)(2,1)S(1)}, bf16[96,384]{1,0:T(8,128)(2,1)S(1)}, u32[]{:S(2)}, u32[]{:S(2)}) %collective-permute-start.2) | collective-permute-done | bytes 73760 | tf_op jit(solution)/shard_map/ppermute | solution.py:497
  13.0 3.7 %side.1 = (bf16[24,3,128,256]{3,2,1,0:T(8,128)(2,1)S(1)}, f32[3,192,128]{2,1,0:T(8,128)S(1)}) custom-call(bf16[128,384]{1,0:T(8,128)(2,1)S(1)} %get-tuple-element.32.centre_ref, bf16[96,384]{1,0:T(8,128)(2,1)S(1)} %collective-permute-done.2.before_ref.after_ref.code_before_ref.code_after_ref, ...), custom_call_target="tpu_custom_call" | custom-call | flops 1000000 | bytes 1000000 | tf_op jit(solution)/shard_map/side/pallas_call | solution.py:519
  16.7 0.1 collective-permute-start.3
  16.8 1.3 %back_tables.1 = (bf16[24,512,256]{2,1,0:T(8,128)(2,1)S(1)}, bf16[2,128,4608]{2,1,0:T(8,128)(2,1)S(1)}, f32[3,192,128]{2,1,0:T(8,128)S(1)}, f32[3,192,128]{2,1,0:T(8,128)S(1)}) custom-call(f32[24,8,256]{2,1,0:T(8,128)S(1)} %get-tuple-element.34.taps_ref, bf16[128,384]{1,0:T(8,128)(2,1)S(1)} %get-tuple-element.39.code_ref, ...), custom_call_target="tpu_custom_call" | custom-call | flops 1000000000 | bytes 1000000 | tf_op jit(solution)/shard_map/back_tables/pallas_call | solution.py:529
  18.2 0.2 collective-permute-done.3.other_ref
  18.4 4.2 %backward.1 = (f32[256,128]{1,0:T(8,128)S(1)}, f32[256,128]{1,0:T(8,128)}, f32[2,128]{1,0:T(2,128)S(1)}) custom-call(f32[3,192,128]{2,1,0:T(8,128)S(1)} %get-tuple-element.38._.own_ref, f32[3,192,128]{2,1,0:T(8,128)S(1)} %collective-permute-done.3.other_ref, f32[3,192,128]{2,1,0:T(8,128)S(1)} %get-tuple-element.40.goal_ref, ...), custom_call_target="tpu_custom_call" | custom-call | flops 1000000 | bytes 1000000 | tf_op jit(solution)/shard_map/backward/pallas_call | solution.py:543
  22.6 0.4 %collective-permute-start.4 = (f32[2,128]{1,0:T(2,128)S(1)}, f32[2,128]{1,0:T(2,128)S(1)}, u32[]{:S(2)}, u32[]{:S(2)}) collective-permute-start(f32[2,128]{1,0:T(2,128)S(1)} %get-tuple-element.47), channel_id=1, source_target_pairs={{0,1},{1,0},{2,3},{3,2},{4,5},{5,4},{6,7},{7,6},{8,9},{9,8},{10,11... | collective-permute-start | bytes 3080 | tf_op jit(solution)/shard_map/ppermute | solution.py:559
  23.0 0.9 %collective-permute-done.4 = f32[2,128]{1,0:T(2,128)S(1)} collective-permute-done((f32[2,128]{1,0:T(2,128)S(1)}, f32[2,128]{1,0:T(2,128)S(1)}, u32[]{:S(2)}, u32[]{:S(2)}) %collective-permute-start.4) | collective-permute-done | bytes 1056 | tf_op jit(solution)/shard_map/ppermute | solution.py:559
  23.8 1.4 %collective-permute-start.5 = (f32[2,128]{1,0:T(2,128)S(1)}, f32[2,128]{1,0:T(2,128)S(1)}, u32[]{:S(2)}, u32[]{:S(2)}) collective-permute-start(f32[2,128]{1,0:T(2,128)S(1)} %add.12), channel_id=1, source_target_pairs={{0,3},{1,2},{2,1},{3,0},{4,7},{5,6},{6,5},{7,4},{8,11},{9,10},{10,... | collective-permute-start | bytes 3080 | tf_op jit(solution)/shard_map/ppermute | solution.py:55
  25.2 1.6 %collective-permute-done.5 = f32[2,128]{1,0:T(2,128)S(1)} collective-permute-done((f32[2,128]{1,0:T(2,128)S(1)}, f32[2,128]{1,0:T(2,128)S(1)}, u32[]{:S(2)}, u32[]{:S(2)}) %collective-permute-start.5) | collective-permute-done | bytes 1056 | tf_op jit(solution)/shard_map/ppermute | solution.py:55
  26.8 1.5 %collective-permute-start.6 = (f32[2,128]{1,0:T(2,128)S(1)}, f32[2,128]{1,0:T(2,128)S(1)}, u32[]{:S(2)}, u32[]{:S(2)}) collective-permute-start(f32[2,128]{1,0:T(2,128)S(1)} %add.13), channel_id=1, source_target_pairs={{0,5},{1,4},{4,1},{5,0},{8,13},{9,12},{12,9},{13,8},{2,7},{3,6},{6... | collective-permute-start | bytes 3080 | tf_op jit(solution)/shard_map/ppermute | solution.py:55
  28.3 1.5 %collective-permute-done.6 = f32[2,128]{1,0:T(2,128)S(1)} collective-permute-done((f32[2,128]{1,0:T(2,128)S(1)}, f32[2,128]{1,0:T(2,128)S(1)}, u32[]{:S(2)}, u32[]{:S(2)}) %collective-permute-start.6) | collective-permute-done | bytes 1056 | tf_op jit(solution)/shard_map/ppermute | solution.py:55
  29.8 2.5 %collective-permute-start.7 = (f32[2,128]{1,0:T(2,128)S(1)}, f32[2,128]{1,0:T(2,128)S(1)}, u32[]{:S(2)}, u32[]{:S(2)}) collective-permute-start(f32[2,128]{1,0:T(2,128)S(1)} %add.14), channel_id=1, source_target_pairs={{0,9},{1,8},{4,13},{5,12},{8,1},{9,0},{12,5},{13,4},{2,11},{3,10},... | collective-permute-start | bytes 3080 | tf_op jit(solution)/shard_map/ppermute | solution.py:55
  32.3 1.4 %collective-permute-done.7 = f32[2,128]{1,0:T(2,128)S(1)} collective-permute-done((f32[2,128]{1,0:T(2,128)S(1)}, f32[2,128]{1,0:T(2,128)S(1)}, u32[]{:S(2)}, u32[]{:S(2)}) %collective-permute-start.7) | collective-permute-done | bytes 1056 | tf_op jit(solution)/shard_map/ppermute | solution.py:55
  33.8 0.7 %finish.1 = (f32[256,128]{1,0:T(8,128)}, f32[1,128]{1,0:T(1,128)}) custom-call(f32[256,128]{1,0:T(8,128)S(1)} %get-tuple-element.27.params_ref, f32[256,128]{1,0:T(8,128)S(1)} %get-tuple-element.46.gradient_ref, f32[2,128]{1,0:T(2,128)S(1)} %add.15.sums_ref), custom_call_target="tpu_custom_call" | custom-call | flops 1000000 | bytes 1000000 | tf_op jit(solution)/shard_map/finish/pallas_call | solution.py:563
  (4 shorter events, 0.0 us)
Async XLA Ops:
  1.5 5.5 %collective-permute-start = (bf16[96,128]{1,0:T(8,128)(2,1)S(1)}, bf16[96,128]{1,0:T(8,128)(2,1)S(1)}, u32[]{:S(2)}, u32[]{:S(2)}) collective-permute-start(bf16[96,128]{1,0:T(8,128)(2,1)S(1)} %get-tuple-element.30), channel_id=1, source_target_pairs={{0,4},{4,8},{8,12},{12,28},{28,24},{24,20},{20,16},{16,0},{1,5},{5... | collective-permute-start | bytes 73736 | tf_op jit(solution)/shard_map/ppermute | solution.py:468
  4.6 3.8 %collective-permute-start.1 = (bf16[96,128]{1,0:T(8,128)(2,1)S(1)}, bf16[96,128]{1,0:T(8,128)(2,1)S(1)}, u32[]{:S(2)}, u32[]{:S(2)}) collective-permute-start(bf16[96,128]{1,0:T(8,128)(2,1)S(1)} %get-tuple-element.31), channel_id=1, source_target_pairs={{0,16},{4,0},{8,4},{12,8},{28,12},{24,28},{20,24},{16,20},{1,17},{... | collective-permute-start | bytes 73736 | tf_op jit(solution)/shard_map/ppermute | solution.py:469
  8.6 4.4 %collective-permute-start.2 = (bf16[96,384]{1,0:T(8,128)(2,1)S(1)}, bf16[96,384]{1,0:T(8,128)(2,1)S(1)}, u32[]{:S(2)}, u32[]{:S(2)}) collective-permute-start(bf16[96,384]{1,0:T(8,128)(2,1)S(1)} %get-tuple-element.33), channel_id=1, source_target_pairs={{0,2},{2,0},{1,3},{3,1},{4,6},{6,4},{5,7},{7,5},{8,10},{10,8},{9,1... | collective-permute-start | bytes 221192 | tf_op jit(solution)/shard_map/ppermute | solution.py:497
  16.7 1.6 %collective-permute-start.3 = (f32[3,192,128]{2,1,0:T(8,128)S(1)}, f32[3,192,128]{2,1,0:T(8,128)S(1)}, u32[]{:S(2)}, u32[]{:S(2)}) collective-permute-start(f32[3,192,128]{2,1,0:T(8,128)S(1)} %get-tuple-element.38._.own_ref), channel_id=1, source_target_pairs={{0,1},{1,0},{2,3},{3,2},{4,5},{5,4},{6,7},{7,6},{8,9},{9,8},{10,11... | collective-permute-start | bytes 884744 | tf_op jit(solution)/shard_map/ppermute | solution.py:528
  22.6 1.2 %collective-permute-start.4 = (f32[2,128]{1,0:T(2,128)S(1)}, f32[2,128]{1,0:T(2,128)S(1)}, u32[]{:S(2)}, u32[]{:S(2)}) collective-permute-start(f32[2,128]{1,0:T(2,128)S(1)} %get-tuple-element.47), channel_id=1, source_target_pairs={{0,1},{1,0},{2,3},{3,2},{4,5},{5,4},{6,7},{7,6},{8,9},{9,8},{10,11... | collective-permute-start | bytes 3080 | tf_op jit(solution)/shard_map/ppermute | solution.py:559
  23.8 3.0 %collective-permute-start.5 = (f32[2,128]{1,0:T(2,128)S(1)}, f32[2,128]{1,0:T(2,128)S(1)}, u32[]{:S(2)}, u32[]{:S(2)}) collective-permute-start(f32[2,128]{1,0:T(2,128)S(1)} %add.12), channel_id=1, source_target_pairs={{0,3},{1,2},{2,1},{3,0},{4,7},{5,6},{6,5},{7,4},{8,11},{9,10},{10,... | collective-permute-start | bytes 3080 | tf_op jit(solution)/shard_map/ppermute | solution.py:55
  26.8 3.0 %collective-permute-start.6 = (f32[2,128]{1,0:T(2,128)S(1)}, f32[2,128]{1,0:T(2,128)S(1)}, u32[]{:S(2)}, u32[]{:S(2)}) collective-permute-start(f32[2,128]{1,0:T(2,128)S(1)} %add.13), channel_id=1, source_target_pairs={{0,5},{1,4},{4,1},{5,0},{8,13},{9,12},{12,9},{13,8},{2,7},{3,6},{6... | collective-permute-start | bytes 3080 | tf_op jit(solution)/shard_map/ppermute | solution.py:55
  29.8 3.9 %collective-permute-start.7 = (f32[2,128]{1,0:T(2,128)S(1)}, f32[2,128]{1,0:T(2,128)S(1)}, u32[]{:S(2)}, u32[]{:S(2)}) collective-permute-start(f32[2,128]{1,0:T(2,128)S(1)} %add.14), channel_id=1, source_target_pairs={{0,9},{1,8},{4,13},{5,12},{8,1},{9,0},{12,5},{13,4},{2,11},{3,10},... | collective-permute-start | bytes 3080 | tf_op jit(solution)/shard_map/ppermute | solution.py:55

commit v11 on v9

--- a/solution.py
+++ b/solution.py
@@ -9,7 +9,7 @@
 HALF = 32
 LANES = 128
 BACKWARD_UNROLL = 12
-CHUNK = 6
+CHUNK = 12
 VMEM = 24 * 2**20
 
 mask_slope = 4.0

time: 34.8 us -> 34.7 us (level)
  no operation moved by 1% of the time
where the time goes in v11:
time: 34.7 us; the launch traced here: 34.5 us
  Pallas kernels  15.6 us (45%)
  starting transfers between devices  10.5 us (30%)
  waiting for transfers between devices  7.74 us (22%)
  between operations  0.71 us (2%)
    ppermute x3, starting transfers between devices, total_over(): lax.ppermute(value, both, partners(peers, lambda i, r=reach: i ^ r))  5.36 us
    ppermute x3, waiting for transfers between devices, total_over(): lax.ppermute(value, both, partners(peers, lambda i, r=reach: i ^ r))  4.54 us
    pallas_call x1, Pallas kernels, shards(): call(backward_kernel, 'backward', [vmem] * 9, (full, full, array((2, LANE...  4.23 us
    pallas_call x1, Pallas kernels, shards(): call(side_kernel, 'side', [vmem] * 7, (fields, array(plane, F32)), scratc...  3.79 us
    ppermute x1, starting transfers between devices, shards(): from_behind = lax.ppermute(ahead, ('tiles', 'strip'), snake(1))  3.1 us
    pallas_call x1, Pallas kernels, shards(): call(load_kernel, 'load', [hbm] * 5, (full, plain, plain, array((kernels,...  2.33 us
    pallas_call x1, Pallas kernels, shards(): call(middle_kernel, 'middle', [vmem] * 4, (fields, array((tiles, wide, LA...  2.21 us
    ppermute x1, starting transfers between devices, shards(): before = after = lax.ppermute(messages[0], 'col', ring('col', 1))  1.56 us
  transfers between devices with their start and end apart: 8, of which 7 were waited for; matrix products, arithmetic and copies ran while one was open for 0% of the time, Pallas kernels for 17%

profile of v11, /device:TPU:0, one launch (start us, length us, event | category | flops | bytes accessed | tf_op | source)
XLA Modules:
  0.0 34.5 jit_solution(9427949319164553532)
XLA Ops:
  0.6 0.8 %edges.1 = (bf16[96,128]{1,0:T(8,128)(2,1)S(1)}, bf16[96,128]{1,0:T(8,128)(2,1)S(1)}) custom-call(f32[256,128]{1,0:T(8,128)} %bitcast.4, s32[256,128]{1,0:T(8,128)} %target_hbm.3), custom_call_target="tpu_custom_call" | custom-call | flops 1000000 | bytes 1000000 | tf_op jit(solution)/shard_map/edges/pallas_call | solution.py:452
  1.5 3.1 %collective-permute-start = (bf16[96,128]{1,0:T(8,128)(2,1)S(1)}, bf16[96,128]{1,0:T(8,128)(2,1)S(1)}, u32[]{:S(2)}, u32[]{:S(2)}) collective-permute-start(bf16[96,128]{1,0:T(8,128)(2,1)S(1)} %get-tuple-element.30), channel_id=1, source_target_pairs={{0,4},{4,8},{8,12},{12,28},{28,24},{24,20},{20,16},{16,0},{1,5},{5... | collective-permute-start | bytes 73736 | tf_op jit(solution)/shard_map/ppermute | solution.py:463
  4.6 0.0 collective-permute-start.1
  4.6 2.3 %load.1 = (f32[256,128]{1,0:T(8,128)S(1)}, bf16[256,128]{1,0:T(8,128)(2,1)S(1)}, bf16[256,128]{1,0:T(8,128)(2,1)S(1)}, f32[24,8,256]{2,1,0:T(8,128)S(1)}, bf16[3...) custom-call(f32[256,128]{1,0:T(8,128)} %bitcast.5, s32[256,128]{1,0:T(8,128)} %target_hbm.3, f32[24]{0:T(128)} %weights_hbm.1, ...), custom_call_target="tpu_custom_call" | custom-call | flops 100000000 | bytes 1000000 | tf_op jit(solution)/shard_map/load/pallas_call | solution.py:467
  6.9 0.0 collective-permute-done.behind_ref
  6.9 1.5 %collective-permute-done.1.ahead_ref = bf16[96,128]{1,0:T(8,128)(2,1)S(1)} collective-permute-done((bf16[96,128]{1,0:T(8,128)(2,1)S(1)}, bf16[96,128]{1,0:T(8,128)(2,1)S(1)}, u32[]{:S(2)}, u32[]{:S(2)}) %collective-permute-start.1) | collective-permute-done | bytes 24608 | tf_op jit(solution)/shard_map/ppermute | solution.py:464
  8.4 0.2 assemble.1
  8.6 1.6 %collective-permute-start.2 = (bf16[96,384]{1,0:T(8,128)(2,1)S(1)}, bf16[96,384]{1,0:T(8,128)(2,1)S(1)}, u32[]{:S(2)}, u32[]{:S(2)}) collective-permute-start(bf16[96,384]{1,0:T(8,128)(2,1)S(1)} %get-tuple-element.33), channel_id=1, source_target_pairs={{0,2},{2,0},{1,3},{3,1},{4,6},{6,4},{5,7},{7,5},{8,10},{10,8},{9,1... | collective-permute-start | bytes 221192 | tf_op jit(solution)/shard_map/ppermute | solution.py:492
  10.1 2.2 %middle.1 = (bf16[24,3,64,256]{3,2,1,0:T(8,128)(2,1)S(1)}, f32[3,64,128]{2,1,0:T(8,128)S(1)}) custom-call(bf16[128,384]{1,0:T(8,128)(2,1)S(1)} %get-tuple-element.32.centre_ref, f32[24,8,256]{2,1,0:T(8,128)S(1)} %get-tuple-element.34.taps_ref, bf16[3072,128]{1,0:T(8,128)(2,1)S(1)} %get-tuple-element.35.near_ref, ...), custom_call_target="tpu_custom_call" | custom-call | flops 4000000000 | bytes 1000000 | tf_op jit(solution)/shard_map/middle/pallas_call | solution.py:503
  12.3 0.6 %collective-permute-done.2.before_ref.after_ref.code_before_ref.code_after_ref = bf16[96,384]{1,0:T(8,128)(2,1)S(1)} collective-permute-done((bf16[96,384]{1,0:T(8,128)(2,1)S(1)}, bf16[96,384]{1,0:T(8,128)(2,1)S(1)}, u32[]{:S(2)}, u32[]{:S(2)}) %collective-permute-start.2) | collective-permute-done | bytes 73760 | tf_op jit(solution)/shard_map/ppermute | solution.py:492
  13.0 3.8 %side.1 = (bf16[24,3,128,256]{3,2,1,0:T(8,128)(2,1)S(1)}, f32[3,192,128]{2,1,0:T(8,128)S(1)}) custom-call(bf16[128,384]{1,0:T(8,128)(2,1)S(1)} %get-tuple-element.32.centre_ref, bf16[96,384]{1,0:T(8,128)(2,1)S(1)} %collective-permute-done.2.before_ref.after_ref.code_before_ref.code_after_ref, ...), custom_call_target="tpu_custom_call" | custom-call | flops 1000000 | bytes 1000000 | tf_op jit(solution)/shard_map/side/pallas_call | solution.py:514
  16.8 0.1 collective-permute-start.3
  16.9 1.3 %back_tables.1 = (bf16[24,512,256]{2,1,0:T(8,128)(2,1)S(1)}, bf16[2,128,4608]{2,1,0:T(8,128)(2,1)S(1)}, f32[3,192,128]{2,1,0:T(8,128)S(1)}, f32[3,192,128]{2,1,0:T(8,128)S(1)}) custom-call(f32[24,8,256]{2,1,0:T(8,128)S(1)} %get-tuple-element.34.taps_ref, bf16[128,384]{1,0:T(8,128)(2,1)S(1)} %get-tuple-element.39.code_ref, ...), custom_call_target="tpu_custom_call" | custom-call | flops 1000000000 | bytes 1000000 | tf_op jit(solution)/shard_map/back_tables/pallas_call | solution.py:524
  18.2 0.2 collective-permute-done.3.other_ref
  18.4 4.2 %backward.1 = (f32[256,128]{1,0:T(8,128)S(1)}, f32[256,128]{1,0:T(8,128)}, f32[2,128]{1,0:T(2,128)S(1)}) custom-call(f32[3,192,128]{2,1,0:T(8,128)S(1)} %get-tuple-element.38._.own_ref, f32[3,192,128]{2,1,0:T(8,128)S(1)} %collective-permute-done.3.other_ref, f32[3,192,128]{2,1,0:T(8,128)S(1)} %get-tuple-element.40.goal_ref, ...), custom_call_target="tpu_custom_call" | custom-call | flops 1000000 | bytes 1000000 | tf_op jit(solution)/shard_map/backward/pallas_call | solution.py:538
  22.7 0.4 %collective-permute-start.4 = (f32[2,128]{1,0:T(2,128)S(1)}, f32[2,128]{1,0:T(2,128)S(1)}, u32[]{:S(2)}, u32[]{:S(2)}) collective-permute-start(f32[2,128]{1,0:T(2,128)S(1)} %get-tuple-element.47), channel_id=1, source_target_pairs={{0,1},{1,0},{2,3},{3,2},{4,5},{5,4},{6,7},{7,6},{8,9},{9,8},{10,11... | collective-permute-start | bytes 3080 | tf_op jit(solution)/shard_map/ppermute | solution.py:554
  23.0 0.9 %collective-permute-done.4 = f32[2,128]{1,0:T(2,128)S(1)} collective-permute-done((f32[2,128]{1,0:T(2,128)S(1)}, f32[2,128]{1,0:T(2,128)S(1)}, u32[]{:S(2)}, u32[]{:S(2)}) %collective-permute-start.4) | collective-permute-done | bytes 1056 | tf_op jit(solution)/shard_map/ppermute | solution.py:554
  23.9 1.4 %collective-permute-start.5 = (f32[2,128]{1,0:T(2,128)S(1)}, f32[2,128]{1,0:T(2,128)S(1)}, u32[]{:S(2)}, u32[]{:S(2)}) collective-permute-start(f32[2,128]{1,0:T(2,128)S(1)} %add.12), channel_id=1, source_target_pairs={{0,3},{1,2},{2,1},{3,0},{4,7},{5,6},{6,5},{7,4},{8,11},{9,10},{10,... | collective-permute-start | bytes 3080 | tf_op jit(solution)/shard_map/ppermute | solution.py:54
  25.3 1.6 %collective-permute-done.5 = f32[2,128]{1,0:T(2,128)S(1)} collective-permute-done((f32[2,128]{1,0:T(2,128)S(1)}, f32[2,128]{1,0:T(2,128)S(1)}, u32[]{:S(2)}, u32[]{:S(2)}) %collective-permute-start.5) | collective-permute-done | bytes 1056 | tf_op jit(solution)/shard_map/ppermute | solution.py:54
  26.9 1.5 %collective-permute-start.6 = (f32[2,128]{1,0:T(2,128)S(1)}, f32[2,128]{1,0:T(2,128)S(1)}, u32[]{:S(2)}, u32[]{:S(2)}) collective-permute-start(f32[2,128]{1,0:T(2,128)S(1)} %add.13), channel_id=1, source_target_pairs={{0,5},{1,4},{4,1},{5,0},{8,13},{9,12},{12,9},{13,8},{2,7},{3,6},{6... | collective-permute-start | bytes 3080 | tf_op jit(solution)/shard_map/ppermute | solution.py:54
  28.4 1.5 %collective-permute-done.6 = f32[2,128]{1,0:T(2,128)S(1)} collective-permute-done((f32[2,128]{1,0:T(2,128)S(1)}, f32[2,128]{1,0:T(2,128)S(1)}, u32[]{:S(2)}, u32[]{:S(2)}) %collective-permute-start.6) | collective-permute-done | bytes 1056 | tf_op jit(solution)/shard_map/ppermute | solution.py:54
  29.9 2.5 %collective-permute-start.7 = (f32[2,128]{1,0:T(2,128)S(1)}, f32[2,128]{1,0:T(2,128)S(1)}, u32[]{:S(2)}, u32[]{:S(2)}) collective-permute-start(f32[2,128]{1,0:T(2,128)S(1)} %add.14), channel_id=1, source_target_pairs={{0,9},{1,8},{4,13},{5,12},{8,1},{9,0},{12,5},{13,4},{2,11},{3,10},... | collective-permute-start | bytes 3080 | tf_op jit(solution)/shard_map/ppermute | solution.py:54
  32.4 1.4 %collective-permute-done.7 = f32[2,128]{1,0:T(2,128)S(1)} collective-permute-done((f32[2,128]{1,0:T(2,128)S(1)}, f32[2,128]{1,0:T(2,128)S(1)}, u32[]{:S(2)}, u32[]{:S(2)}) %collective-permute-start.7) | collective-permute-done | bytes 1056 | tf_op jit(solution)/shard_map/ppermute | solution.py:54
  33.8 0.7 %finish.1 = (f32[256,128]{1,0:T(8,128)}, f32[1,128]{1,0:T(1,128)}) custom-call(f32[256,128]{1,0:T(8,128)S(1)} %get-tuple-element.27.params_ref, f32[256,128]{1,0:T(8,128)S(1)} %get-tuple-element.46.gradient_ref, f32[2,128]{1,0:T(2,128)S(1)} %add.15.sums_ref), custom_call_target="tpu_custom_call" | custom-call | flops 1000000 | bytes 1000000 | tf_op jit(solution)/shard_map/finish/pallas_call | solution.py:558
  (4 shorter events, 0.0 us)
Async XLA Ops:
  1.5 5.5 %collective-permute-start = (bf16[96,128]{1,0:T(8,128)(2,1)S(1)}, bf16[96,128]{1,0:T(8,128)(2,1)S(1)}, u32[]{:S(2)}, u32[]{:S(2)}) collective-permute-start(bf16[96,128]{1,0:T(8,128)(2,1)S(1)} %get-tuple-element.30), channel_id=1, source_target_pairs={{0,4},{4,8},{8,12},{12,28},{28,24},{24,20},{20,16},{16,0},{1,5},{5... | collective-permute-start | bytes 73736 | tf_op jit(solution)/shard_map/ppermute | solution.py:463
  4.6 3.8 %collective-permute-start.1 = (bf16[96,128]{1,0:T(8,128)(2,1)S(1)}, bf16[96,128]{1,0:T(8,128)(2,1)S(1)}, u32[]{:S(2)}, u32[]{:S(2)}) collective-permute-start(bf16[96,128]{1,0:T(8,128)(2,1)S(1)} %get-tuple-element.31), channel_id=1, source_target_pairs={{0,16},{4,0},{8,4},{12,8},{28,12},{24,28},{20,24},{16,20},{1,17},{... | collective-permute-start | bytes 73736 | tf_op jit(solution)/shard_map/ppermute | solution.py:464
  8.6 4.4 %collective-permute-start.2 = (bf16[96,384]{1,0:T(8,128)(2,1)S(1)}, bf16[96,384]{1,0:T(8,128)(2,1)S(1)}, u32[]{:S(2)}, u32[]{:S(2)}) collective-permute-start(bf16[96,384]{1,0:T(8,128)(2,1)S(1)} %get-tuple-element.33), channel_id=1, source_target_pairs={{0,2},{2,0},{1,3},{3,1},{4,6},{6,4},{5,7},{7,5},{8,10},{10,8},{9,1... | collective-permute-start | bytes 221192 | tf_op jit(solution)/shard_map/ppermute | solution.py:492
  16.8 1.6 %collective-permute-start.3 = (f32[3,192,128]{2,1,0:T(8,128)S(1)}, f32[3,192,128]{2,1,0:T(8,128)S(1)}, u32[]{:S(2)}, u32[]{:S(2)}) collective-permute-start(f32[3,192,128]{2,1,0:T(8,128)S(1)} %get-tuple-element.38._.own_ref), channel_id=1, source_target_pairs={{0,1},{1,0},{2,3},{3,2},{4,5},{5,4},{6,7},{7,6},{8,9},{9,8},{10,11... | collective-permute-start | bytes 884744 | tf_op jit(solution)/shard_map/ppermute | solution.py:523
  22.7 1.2 %collective-permute-start.4 = (f32[2,128]{1,0:T(2,128)S(1)}, f32[2,128]{1,0:T(2,128)S(1)}, u32[]{:S(2)}, u32[]{:S(2)}) collective-permute-start(f32[2,128]{1,0:T(2,128)S(1)} %get-tuple-element.47), channel_id=1, source_target_pairs={{0,1},{1,0},{2,3},{3,2},{4,5},{5,4},{6,7},{7,6},{8,9},{9,8},{10,11... | collective-permute-start | bytes 3080 | tf_op jit(solution)/shard_map/ppermute | solution.py:554
  23.9 3.0 %collective-permute-start.5 = (f32[2,128]{1,0:T(2,128)S(1)}, f32[2,128]{1,0:T(2,128)S(1)}, u32[]{:S(2)}, u32[]{:S(2)}) collective-permute-start(f32[2,128]{1,0:T(2,128)S(1)} %add.12), channel_id=1, source_target_pairs={{0,3},{1,2},{2,1},{3,0},{4,7},{5,6},{6,5},{7,4},{8,11},{9,10},{10,... | collective-permute-start | bytes 3080 | tf_op jit(solution)/shard_map/ppermute | solution.py:54
  26.9 3.0 %collective-permute-start.6 = (f32[2,128]{1,0:T(2,128)S(1)}, f32[2,128]{1,0:T(2,128)S(1)}, u32[]{:S(2)}, u32[]{:S(2)}) collective-permute-start(f32[2,128]{1,0:T(2,128)S(1)} %add.13), channel_id=1, source_target_pairs={{0,5},{1,4},{4,1},{5,0},{8,13},{9,12},{12,9},{13,8},{2,7},{3,6},{6... | collective-permute-start | bytes 3080 | tf_op jit(solution)/shard_map/ppermute | solution.py:54
  29.9 3.9 %collective-permute-start.7 = (f32[2,128]{1,0:T(2,128)S(1)}, f32[2,128]{1,0:T(2,128)S(1)}, u32[]{:S(2)}, u32[]{:S(2)}) collective-permute-start(f32[2,128]{1,0:T(2,128)S(1)} %add.14), channel_id=1, source_target_pairs={{0,9},{1,8},{4,13},{5,12},{8,1},{9,0},{12,5},{13,4},{2,11},{3,10},... | collective-permute-start | bytes 3080 | tf_op jit(solution)/shard_map/ppermute | solution.py:54
